TPU v7x, 32 devices: a whole 2x2x4 slice. The times are simulated.
32 devices in a mesh: dp: 8 (over z, y), tensor: 4 (over x, core).
Axes of the slice: x: 2, y: 2, z: 4, core: 2. Of those that a mesh axis runs over, the one named last changes fastest.
Arguments:
- hidden_in: bfloat16 [8192, 1536], P(('dp', 'tensor')), may hold values from -6 to 6
- cotangent: bfloat16 [8192, 1536], P(('dp', 'tensor')), may hold values from -6 to 6
- lengths: int32 [8], P('dp'), may hold values from 256 to 1024, as said below
- routes: int32 [8192, 8], P(('dp', 'tensor')), may hold values from 0 to 63, all different within a row
- gate_values: float32 [8192, 8], P(('dp', 'tensor')), may hold values from 0.05 to 0.25
- pair_order: int32 [32, 2048], P(('dp', 'tensor')), may hold values from 0 to 2047, each once within a row
- query_weight: float32 [1536, 1536], P('dp', 'tensor'), may hold values from -0.15625 to 0.15625
- keyvalue_matrix: float32 [2, 1536, 512], P(None, 'dp', 'tensor'), may hold values from -0.15625 to 0.15625
- outproj_weight: float32 [1536, 1536], P('tensor', 'dp'), may hold values from -1.75 to 1.75
- norm_gains: float32 [2, 1536], P(None, 'dp'), may hold values from 0.5 to 1.5
- upgate_weight: float32 [2, 64, 1536, 512], P(None, 'dp', None, 'tensor'), may hold values from -0.15625 to 0.15625
- downproj_weight: float32 [64, 512, 1536], P('dp', 'tensor'), may hold values from -0.25 to 0.25
- query_mean: float32 [1536, 1536], P('dp', 'tensor'), may hold values from -32 to 32
- query_sqmean: float32 [1536, 1536], P('dp', 'tensor'), may hold values from 49.152 to 229.376
- keyvalue_first_moment: float32 [2, 1536, 512], P(None, 'dp', 'tensor'), may hold values from -32 to 32
- keyvalue_second_moment: float32 [2, 1536, 512], P(None, 'dp', 'tensor'), may hold values from 49.152 to 229.376
- outproj_mean: float32 [1536, 1536], P('tensor', 'dp'), may hold values from -3 to 3
- outproj_sqmean: float32 [1536, 1536], P('tensor', 'dp'), may hold values from 0.49152 to 2.29376
- gains_mean: float32 [2, 1536], P(None, 'dp'), may hold values from -32 to 32
- gains_sqmean: float32 [2, 1536], P(None, 'dp'), may hold values from 49.152 to 229.376
- upgate_mean: float32 [2, 64, 1536, 512], P(None, 'dp', None, 'tensor'), may hold values from -2 to 2
- upgate_sqmean: float32 [2, 64, 1536, 512], P(None, 'dp', None, 'tensor'), may hold values from 0.256 to 1.1264
- downproj_mean: float32 [64, 512, 1536], P('dp', 'tensor'), may hold values from -1.5 to 1.5
- downproj_sqmean: float32 [64, 512, 1536], P('dp', 'tensor'), may hold values from 0.12288 to 0.55296
Outputs:
- block_out: bfloat16 [8192, 1536], P(('dp', 'tensor'))
- input_grad: float32 [8192, 1536], P(('dp', 'tensor'))
- gate_grad: float32 [8192, 8], P(('dp', 'tensor'))
- query_grad: float32 [1536, 1536], P('dp', 'tensor')
- query_newmean: float32 [1536, 1536], P('dp', 'tensor')
- query_newsq: float32 [1536, 1536], P('dp', 'tensor')
- query_update: float32 [1536, 1536], P('dp', 'tensor')
- keyval_grad: float32 [2, 1536, 512], P(None, 'dp', 'tensor')
- keyval_newmean: float32 [2, 1536, 512], P(None, 'dp', 'tensor')
- keyval_newsq: float32 [2, 1536, 512], P(None, 'dp', 'tensor')
- keyval_update: float32 [2, 1536, 512], P(None, 'dp', 'tensor')
- outproj_grad: float32 [1536, 1536], P('tensor', 'dp')
- outproj_newmean: float32 [1536, 1536], P('tensor', 'dp')
- outproj_newsq: float32 [1536, 1536], P('tensor', 'dp')
- outproj_update: float32 [1536, 1536], P('tensor', 'dp')
- gains_grad: float32 [2, 1536], P(None, 'dp')
- gains_newmean: float32 [2, 1536], P(None, 'dp')
- gains_newsq: float32 [2, 1536], P(None, 'dp')
- gains_update: float32 [2, 1536], P(None, 'dp')
- upgate_grad: float32 [2, 64, 1536, 512], P(None, 'dp', None, 'tensor')
- upgate_newmean: float32 [2, 64, 1536, 512], P(None, 'dp', None, 'tensor')
- upgate_newsq: float32 [2, 64, 1536, 512], P(None, 'dp', None, 'tensor')
- upgate_update: float32 [2, 64, 1536, 512], P(None, 'dp', None, 'tensor')
- downproj_grad: float32 [64, 512, 1536], P('dp', 'tensor')
- downproj_newmean: float32 [64, 512, 1536], P('dp', 'tensor')
- downproj_newsq: float32 [64, 512, 1536], P('dp', 'tensor')
- downproj_update: float32 [64, 512, 1536], P('dp', 'tensor')
Inputs may be any that keep to these rules, and one draw needn't show every extreme that they name: `lengths`: positions of a sequence at or past its length are padding; some sequence has length 1024 and some has 256. `routes`: the 8 entries of a token are distinct experts. `pair_order`: each row is a permutation of the 2048 pairs of one block; lower values take slots first.
All inputs are finite; a program needn't handle non-finite values.
Results may differ from a plain program's by a relative error of at most 0.023.
Values may be sent and summed in bfloat16 or wider, within the bound.
No kernel may reach another device: no remote copies, remote signals or barrier semaphores. Data moves between devices by JAX's collectives and lax.ppermute only.
A program may use at most 576 MiB of HBM per device.

v0:
```python
import functools
import jax
import jax.numpy as jnp
from jax import lax
from jax.experimental import pallas as pl
from jax.experimental.pallas import tpu as pltpu
from jax.sharding import PartitionSpec as P

HEAD_SIZE = 64
TOP = 8
SEQUENCE_SLOTS = 1024
ADAM_STEP = 5
NORM_EPS = 1e-05
ROPE_THETA = 10000.0
MASKED = -1e30
BETA_ONE = 0.9
BETA_TWO = 0.95
LEARN_RATE = 0.03
WEIGHT_DECAY = 0.1
ADAM_EPS = 1e-08
BF = jnp.bfloat16
F32 = jnp.float32
BLOCK = 256
NN = (((1,), (0,)), ((), ()))
NT = (((1,), (1,)), ((), ()))
TN = (((0,), (0,)), ((), ()))


def mm(a, b, dims=NN):
    return lax.dot_general(a, b, dims, preferred_element_type=F32)


def params(mib=58):
    return pltpu.CompilerParams(vmem_limit_bytes=mib << 20)


def adam_step(weight, gradient, first_old, second_old, decay_rate):
    first_new = BETA_ONE * first_old + (1.0 - BETA_ONE) * gradient
    second_new = BETA_TWO * second_old + (1.0 - BETA_TWO) * gradient * gradient
    first_hat = first_new / (1.0 - BETA_ONE**ADAM_STEP)
    second_hat = second_new / (1.0 - BETA_TWO**ADAM_STEP)
    update = -LEARN_RATE * (first_hat / (jnp.sqrt(second_hat) + ADAM_EPS) + decay_rate * weight)
    return (gradient, first_new, second_new, update)


def rank_body(cap, ecol, ocol, erow, orow, out):
    pairs = erow.shape[1]
    step = 64
    er, orr = erow[...], orow[...]

    def chunk(i, acc):
        rows = pl.ds(i * step, step)
        hit = (ecol[rows, :] == er) & (ocol[rows, :] < orr)
        return acc + jnp.sum(hit.astype(jnp.int32), axis=0, keepdims=True)

    rank = lax.fori_loop(0, pairs // step, chunk, jnp.zeros((1, pairs), jnp.int32))
    kept = (orr < pairs) & (rank < cap)
    out[...] = jnp.where(kept, er * cap + rank, -1)


def slot_targets(experts, order, live_pairs, cap):
    pairs = experts.shape[0]
    order = jnp.where(live_pairs, order, pairs)
    return pl.pallas_call(
        functools.partial(rank_body, cap),
        out_shape=jax.ShapeDtypeStruct((1, pairs), jnp.int32),
        compiler_params=params(16),
        name="slot_targets",
    )(experts[:, None], order[:, None], experts[None, :], order[None, :])[0]


def swap_halves(u):
    width = u.shape[1]
    lane = lax.broadcasted_iota(jnp.int32, u.shape, 1) % HEAD_SIZE
    half = HEAD_SIZE // 2
    return jnp.where(lane < half, pltpu.roll(u, width - half, 1), pltpu.roll(u, half, 1))


def rope(u, cos, sin):
    reps = u.shape[1] // cos.shape[1]
    if reps > 1:
        cos = jnp.concatenate([cos] * reps, axis=1)
        sin = jnp.concatenate([sin] * reps, axis=1)
    return u * cos + swap_halves(u) * sin


def rope_lanes(rows):
    lane = jnp.arange(128) % HEAD_SIZE
    half = HEAD_SIZE // 2
    positions = (jnp.arange(rows) % SEQUENCE_SLOTS).astype(F32)
    freqs = ROPE_THETA ** (-(2.0 * (lane % half).astype(F32)) / HEAD_SIZE)
    angles = positions[:, None] * freqs[None, :]
    return jnp.cos(angles), jnp.where(lane < half, -1.0, 1.0) * jnp.sin(angles)


ANY = pl.BlockSpec(memory_space=pltpu.HBM)


def cost(flops, nbytes):
    return pl.CostEstimate(flops=int(flops), bytes_accessed=int(nbytes), transcendentals=0)


def qkv_body(qw, kw, xn, wn, at, *refs):
    xs, ws, refs = refs[:xn], refs[xn : xn + wn], refs[xn + wn :]
    cos, sin, a_out, q_out, k_out, v_out, gains, w_out, x_scr, sem = refs
    step = ws[0].shape[0]
    copies = []
    for i, ref in enumerate(ws):
        rows = pl.ds(pl.multiple_of(at[xn + i] * step, 16), step)
        copies.append(pltpu.make_async_copy(ref, w_out.at[rows, :], sem.at[xn + i]))
    for i, ref in enumerate(xs):
        rows = pl.ds(pl.multiple_of(at[i] * BLOCK, BLOCK), BLOCK)
        copies.append(pltpu.make_async_copy(ref, x_scr.at[rows, :], sem.at[i]))
    for c in copies:
        c.start()
    for c in copies:
        c.wait()
    wide = qw + 2 * kw
    gains[...] = w_out[:, wide + qw :].astype(F32).T[0:8, :]

    def block(i, _):
        rows = pl.ds(pl.multiple_of(i * BLOCK, BLOCK), BLOCK)
        v = x_scr[rows, :].astype(F32)
        r = lax.rsqrt(jnp.mean(v * v, axis=-1, keepdims=True) + NORM_EPS)
        a = (v * r * gains[0:1, :]).astype(BF)
        a_out[rows, :] = a
        y = mm(a, w_out[:, :wide])
        c, s = cos[rows, :], sin[rows, :]
        q_out[rows, :] = rope(y[:, :qw], c, s).astype(BF)
        k_out[rows, :] = rope(y[:, qw : qw + kw], c, s).astype(BF)
        v_out[rows, :] = y[:, qw + kw :].astype(BF)
        return 0

    lax.fori_loop(0, len(xs), block, 0)


def qkv(at, xs, ws, qw, kw, cos, sin):
    rows, width = BLOCK * len(xs), xs[0].shape[1]
    cols = ws[0].shape[1]
    depth = ws[0].shape[0] * len(ws)
    vm = pl.BlockSpec(memory_space=pltpu.VMEM)
    return pl.pallas_call(
        functools.partial(qkv_body, qw, kw, len(xs), len(ws)),
        in_specs=[pl.BlockSpec(memory_space=pltpu.SMEM)]
        + [ANY] * (len(xs) + len(ws))
        + [vm, vm],
        out_specs=[vm] * 6,
        out_shape=[
            jax.ShapeDtypeStruct((rows, width), BF),
            jax.ShapeDtypeStruct((rows, qw), BF),
            jax.ShapeDtypeStruct((rows, kw), BF),
            jax.ShapeDtypeStruct((rows, kw), BF),
            jax.ShapeDtypeStruct((8, width), F32),
            jax.ShapeDtypeStruct((depth, cols), BF),
        ],
        scratch_shapes=[
            pltpu.VMEM((rows, width), BF),
            pltpu.SemaphoreType.DMA((len(xs) + len(ws),)),
        ],
        compiler_params=params(32),
        cost_estimate=cost(2 * rows * width * cols, 2e7),
        name="qkv",
    )(at, *xs, *ws, cos, sin)


def project_body(cols, at, v, w, far, near):
    def block(i, _):
        for j, out in ((2, far), (0, near)):
            rows = pl.ds(pl.multiple_of(at[j + i] * BLOCK, BLOCK), BLOCK)
            out[i] = mm(v[rows, :], w[:, cols[0] : cols[1]], NT).astype(BF)
        return 0

    lax.fori_loop(0, 2, block, 0)


def project(at, v, w, cols):
    rows, depth = v.shape
    width = w.shape[0]
    vm = pl.BlockSpec(memory_space=pltpu.VMEM)
    return pl.pallas_call(
        functools.partial(project_body, cols),
        in_specs=[pl.BlockSpec(memory_space=pltpu.SMEM), vm, vm],
        out_specs=[vm] * 2,
        out_shape=[jax.ShapeDtypeStruct((2, BLOCK, width), BF)] * 2,
        compiler_params=params(32),
        cost_estimate=cost(2 * rows * depth * width, 1e7),
        name="project",
    )(at, v, w)


def heads_back_body(cols, at, m0, m1, m2, m3, w, h_out, m_out, sem):
    copies = []
    for i, ref in enumerate((m0, m1, m2, m3)):
        rows = pl.ds(pl.multiple_of(at[i] * BLOCK, BLOCK), BLOCK)
        copies.append(pltpu.make_async_copy(ref, m_out.at[rows, :], sem.at[i]))
    for c in copies:
        c.start()
    for c in copies:
        c.wait()

    def block(i, _):
        rows = pl.ds(pl.multiple_of(i * BLOCK, BLOCK), BLOCK)
        h_out[rows, :] = mm(m_out[rows, :], w[:, cols[0] : cols[1]]).astype(BF)
        return 0

    lax.fori_loop(0, 4, block, 0)


def heads_back(at, ms, w, cols):
    width, qw = w.shape[0], cols[1] - cols[0]
    rows = 4 * BLOCK
    vm = pl.BlockSpec(memory_space=pltpu.VMEM)
    return pl.pallas_call(
        functools.partial(heads_back_body, cols),
        in_specs=[pl.BlockSpec(memory_space=pltpu.SMEM)] + [ANY] * 4 + [vm],
        out_specs=[vm, vm],
        out_shape=[
            jax.ShapeDtypeStruct((rows, qw), BF),
            jax.ShapeDtypeStruct((rows, width), BF),
        ],
        scratch_shapes=[pltpu.SemaphoreType.DMA((4,))],
        compiler_params=params(32),
        cost_estimate=cost(2 * rows * qw * width, 1e7),
        name="heads_back",
    )(at, *ms, w)


def spread(pair_lanes, out):
    lane = lax.broadcasted_iota(jnp.int32, pair_lanes.shape, 1)
    full = pair_lanes.astype(F32)
    first = jnp.where(lane < HEAD_SIZE, full, 0.0)
    second = jnp.where(lane < HEAD_SIZE, 0.0, full)
    out[0] = first.astype(BF)
    out[1] = pltpu.roll(first, HEAD_SIZE, 1).astype(BF)
    out[2] = pltpu.roll(second, HEAD_SIZE, 1).astype(BF)
    out[3] = second.astype(BF)


def attend_body(share, length, q, k, v, o, lse, ks, vs):
    pair, qb = pl.program_id(0), pl.program_id(1)

    @pl.when((pair == 0) & (qb == 0))
    def _():
        spread(k[...], ks)
        spread(v[...], vs)

    scale = HEAD_SIZE**-0.5
    for j in range(SEQUENCE_SLOTS // BLOCK):

        @pl.when(qb == j)
        def _():
            keys = (j + 1) * BLOCK
            kpos = lax.broadcasted_iota(jnp.int32, (BLOCK, keys), 1)
            qpos = lax.broadcasted_iota(jnp.int32, (BLOCK, keys), 0) + j * BLOCK
            allowed = (kpos <= qpos) & (kpos < length[0])
            total = jnp.zeros((BLOCK, 128), F32)
            for u in range(2):
                which = 2 * ((2 * pair + u) // share) + u
                s = mm(q[...], ks[which, :keys, :], NT) * scale
                s = jnp.where(allowed, s, MASKED)
                top = jnp.max(s, axis=-1, keepdims=True)
                e = jnp.exp(s - top)
                den = jnp.sum(e, axis=-1, keepdims=True)
                total += mm(e.astype(BF), vs[which, :keys, :]) / den
                full = jnp.broadcast_to(top + jnp.log(den), (BLOCK, 128))
                lse[0, u : u + 1, :] = full.T[0:1, :]
            o[...] = total.astype(BF)


def attend(length, q, k, v, share):
    rows, qw = q.shape
    kw = k.shape[1]
    assert kw == 128 and rows == SEQUENCE_SLOTS
    pairs = qw // 128
    blocks = rows // BLOCK
    fix = lambda p, b, n: (0, 0)
    return pl.pallas_call(
        functools.partial(attend_body, share),
        grid_spec=pltpu.PrefetchScalarGridSpec(
            num_scalar_prefetch=1,
            grid=(pairs, blocks),
            in_specs=[
                pl.BlockSpec((BLOCK, 128), lambda p, b, n: (b, p)),
                pl.BlockSpec((rows, kw), fix),
                pl.BlockSpec((rows, kw), fix),
            ],
            out_specs=[
                pl.BlockSpec((BLOCK, 128), lambda p, b, n: (b, p)),
                pl.BlockSpec((1, 8, BLOCK), lambda p, b, n: (p, 0, b)),
            ],
            scratch_shapes=[pltpu.VMEM((4, rows, 128), BF), pltpu.VMEM((4, rows, 128), BF)],
        ),
        out_shape=[
            jax.ShapeDtypeStruct((rows, qw), BF),
            jax.ShapeDtypeStruct((pairs, 8, rows), F32),
        ],
        compiler_params=params(32),
        name="attend",
    )(length, q, k, v)


def attend_back_body(
    share, length, q, k, v, o, do, lse, cos, sin, coskv, sinkv, dq, dk, dv, ks, vs, kt, dka, dva
):
    pair, qb = pl.program_id(0), pl.program_id(1)
    scale = HEAD_SIZE**-0.5

    @pl.when((pair == 0) & (qb == 0))
    def _():
        spread(k[...], ks)
        spread(v[...], vs)
        for i in range(4):
            kt[i] = ks[i].astype(F32).T.astype(BF)
        dka[...] = jnp.zeros_like(dka)
        dva[...] = jnp.zeros_like(dva)

    live = length[0]

    @pl.when(qb * BLOCK >= live)
    def _():
        dq[...] = jnp.zeros_like(dq)

    @pl.when(qb * BLOCK < live)
    def _():
        qt, dot_ = q[...], do[...]
        lane = lax.broadcasted_iota(jnp.int32, (BLOCK, 128), 1)
        both = (dot_.astype(F32) * o[...].astype(F32)).T
        zero = jnp.zeros((), BF)
        mine = [lane < HEAD_SIZE, lane >= HEAD_SIZE]
        qm = [jnp.where(m, qt, zero) for m in mine]
        dm = [jnp.where(m, dot_, zero) for m in mine]
        delta = [
            jnp.sum(both[:HEAD_SIZE], axis=0, keepdims=True),
            jnp.sum(both[HEAD_SIZE:], axis=0, keepdims=True),
        ]

        def step(kb, acc):
            rows = pl.ds(pl.multiple_of(kb * BLOCK, BLOCK), BLOCK)
            kpos = lax.broadcasted_iota(jnp.int32, (BLOCK, BLOCK), 0) + kb * BLOCK
            qpos = lax.broadcasted_iota(jnp.int32, (BLOCK, BLOCK), 1) + qb * BLOCK
            allowed = (kpos <= qpos) & (kpos < live)
            for u in range(2):
                g = (2 * pair + u) // share
                which = 2 * g + u
                st = mm(ks[which, rows, :], qt, NT) * scale
                pt = jnp.where(allowed, jnp.exp(st - lse[0, u : u + 1, :]), 0.0)
                dpt = mm(vs[which, rows, :], dot_, NT)
                dst = (pt * (dpt - delta[u])).astype(BF)
                dka[g, rows, :] += mm(dst, qm[u])
                dva[g, rows, :] += mm(pt.astype(BF), dm[u])
                acc += mm(kt[which, :, rows], dst)
            return acc

        last = jnp.minimum(qb + 1, (live + BLOCK - 1) // BLOCK)
        acc = lax.fori_loop(0, last, step, jnp.zeros((128, BLOCK), F32))
        dq[...] = rope(acc.T * scale, cos[...], -sin[...]).astype(BF)

    @pl.when((pair == pl.num_programs(0) - 1) & (qb == pl.num_programs(1) - 1))
    def _():
        lane = lax.broadcasted_iota(jnp.int32, (SEQUENCE_SLOTS, 128), 1)

        def joined(acc):
            both = [acc[g] + pltpu.roll(acc[g], HEAD_SIZE, 1) for g in range(2)]
            return jnp.where(lane < HEAD_SIZE, both[0], both[1])

        dk[...] = rope(joined(dka) * scale, coskv[...], -sinkv[...]).astype(BF)
        dv[...] = joined(dva).astype(BF)


def attend_back(length, q, k, v, o, do, lse, cos, sin, share):
    rows, qw = q.shape
    kw = k.shape[1]
    pairs, blocks = qw // 128, rows // BLOCK
    fix = lambda p, b, n: (0, 0)
    tile = pl.BlockSpec((BLOCK, 128), lambda p, b, n: (b, p))
    whole = pl.BlockSpec((rows, kw), fix)
    part = pl.BlockSpec((BLOCK, 128), lambda p, b, n: (b, 0))
    return pl.pallas_call(
        functools.partial(attend_back_body, share),
        grid_spec=pltpu.PrefetchScalarGridSpec(
            num_scalar_prefetch=1,
            grid=(pairs, blocks),
            in_specs=[
                tile,
                whole,
                whole,
                tile,
                tile,
                pl.BlockSpec((1, 8, BLOCK), lambda p, b, n: (p, 0, b)),
                part,
                part,
                whole,
                whole,
            ],
            out_specs=[tile, whole, whole],
            scratch_shapes=[
                pltpu.VMEM((4, rows, 128), BF),
                pltpu.VMEM((4, rows, 128), BF),
                pltpu.VMEM((4, 128, rows), BF),
                pltpu.VMEM((2, rows, 128), F32),
                pltpu.VMEM((2, rows, 128), F32),
            ],
        ),
        out_shape=[
            jax.ShapeDtypeStruct((rows, qw), BF),
            jax.ShapeDtypeStruct((rows, kw), BF),
            jax.ShapeDtypeStruct((rows, kw), BF),
        ],
        compiler_params=params(32),
        name="attend_back",
    )(length, q, k, v, o, do, lse, cos, sin, cos, sin)


NB = 8


def local_slots(table, first, local):
    at = (lax.broadcasted_iota(jnp.int32, (local, BLOCK), 0) + first).astype(F32)
    slot = jnp.full((local, BLOCK), -1.0, F32)
    gate = jnp.zeros((local, BLOCK), F32)
    for k in range(TOP):
        row = table[k : k + 1, :]
        here = row[:, :BLOCK] == at
        slot = jnp.where(here, row[:, BLOCK : 2 * BLOCK], slot)
        gate = jnp.where(here, row[:, 2 * BLOCK : 3 * BLOCK] + row[:, 3 * BLOCK :], gate)
    return slot, gate


def one_hot(slot, cap):
    at = lax.broadcasted_iota(jnp.int32, (cap, BLOCK), 0).astype(F32)
    return jnp.concatenate(
        [jnp.where(at == slot[e : e + 1, :], 1.0, 0.0) for e in range(slot.shape[0])], axis=0
    )


def load_plane(own, sib, buf, sem):
    return [
        pltpu.make_async_copy(
            ref.at[n % 4, pl.ds(0, BLOCK), :], buf.at[n], sem.at[n]
        )
        for n in range(NB)
        for ref in (own if n < 4 else sib,)
    ]


def gather_pair(i, buf, hots, out, local, cap):
    width = buf.shape[2]
    cut = width // 3
    rows = pl.ds(pl.multiple_of(i * 2 * cap, 16), 2 * cap)
    for c in range(3):
        cols = slice(c * cut, (c + 1) * cut)
        got = [mm(hots[j], buf[2 * i + j, :, cols]) for j in range(2)]
        for e in range(local):
            mine = [g[e * cap : (e + 1) * cap, :] for g in got]
            out[e, rows, cols] = jnp.concatenate(mine, axis=0).astype(BF)


def seed_body(cap, plane, fresh, first, own, sib, *refs):
    down = refs[0]
    s_out, u_out, tab, buf, s_scr, d_scr, t_scr, sem, t_sem = refs[1 if fresh else 2 :]
    local = d_scr.shape[0]
    copies = load_plane(own, sib, buf, sem)
    for n in range(NB):
        ref = (own if n < 4 else sib).at[n % 4, pl.ds(BLOCK, TOP), :]
        copies.append(pltpu.make_async_copy(ref, t_scr.at[n], t_sem.at[n]))
    weights = pltpu.make_async_copy(down, d_scr, sem.at[NB + 2])
    for c in copies:
        c.start()
    weights.start()
    for c in copies:
        c.wait()
    for n in range(NB):
        tab[n] = t_scr[n, :, : 4 * BLOCK].astype(F32)

    def gather(i, _):
        hots = []
        for j in range(2):
            slot, _g = local_slots(tab[2 * i + j], first[0], local)
            hots.append(one_hot(slot, cap).astype(BF))
        gather_pair(i, buf, hots, s_scr, local, cap)
        return 0

    lax.fori_loop(0, NB // 2, gather, 0, unroll=2)
    rows = NB * cap
    keep = pltpu.make_async_copy(s_scr, s_out.at[:, pl.ds(plane * rows, rows), :], sem.at[NB + 3])
    keep.start()
    weights.wait()

    def expert(e, _):
        u_out[e] = mm(s_scr[e], d_scr[e], NT)
        return 0

    lax.fori_loop(0, local, expert, 0, unroll=4 if local % 4 == 0 else 1)
    keep.wait()


def seed_rows(plane, planes, first, own, sib, down, kept, cap):
    local, hidden, width = down.shape
    rows = NB * cap
    vm = pl.BlockSpec(memory_space=pltpu.VMEM)
    smem = pl.BlockSpec(memory_space=pltpu.SMEM)
    fresh = kept is None
    more = () if fresh else (kept,)
    return pl.pallas_call(
        functools.partial(seed_body, cap, plane, fresh),
        in_specs=[smem] + [ANY] * (3 + len(more)),
        out_specs=[ANY, vm, vm],
        out_shape=[
            jax.ShapeDtypeStruct((local, planes * rows, width), BF),
            jax.ShapeDtypeStruct((local, rows, hidden), F32),
            jax.ShapeDtypeStruct((NB, TOP, 4 * BLOCK), F32),
        ],
        scratch_shapes=[
            pltpu.VMEM((NB, BLOCK, width), BF),
            pltpu.VMEM((local, rows, width), BF),
            pltpu.VMEM((local, hidden, width), BF),
            pltpu.VMEM((NB, TOP, width), BF),
            pltpu.SemaphoreType.DMA((NB + 4,)),
            pltpu.SemaphoreType.DMA((NB,)),
        ],
        input_output_aliases={} if fresh else {4: 0},
        compiler_params=params(50),
        cost_estimate=cost(2 * rows * local * (BLOCK + hidden) * width, 2e7),
        name="seed_rows",
    )(first, own, sib, down, *more)


def main_body(cap, plane, fresh, first, tab, u, own_in, sib_in, *refs):
    wgu = refs[0]
    refs = refs[1 if fresh else 4 :]
    x_out, d_out, a_out, own, sib = refs[:5]
    buf, x_scr, w_scr, z_scr, p_scr, g_scr, r_scr, d_scr, a_scr, m_scr, sem, out_sem = refs[5:]
    local, hidden = a_scr.shape[0], a_scr.shape[2]
    rows = NB * cap
    slots = local * cap
    copies = load_plane(own_in, sib_in, buf, sem)
    weights = pltpu.make_async_copy(wgu, w_scr, sem.at[NB + 2])
    for c in copies:
        c.start()
    weights.start()
    for c in copies:
        c.wait()

    def gather(i, _):
        hots = []
        for j in range(2):
            b = 2 * i + j
            slot, gate = local_slots(tab[b], first[0], local)
            hot = one_hot(slot, cap)
            spread_gate = jnp.concatenate(
                [jnp.broadcast_to(gate[e : e + 1, :], (cap, BLOCK)) for e in range(local)], axis=0
            )
            weight = jnp.sum(hot * spread_gate, axis=1, keepdims=True)
            weight = jnp.broadcast_to(weight, (slots, hidden))
            for e in range(local):
                g_scr[e, pl.ds(b * cap, cap), :] = weight[e * cap : (e + 1) * cap, :]
            hots.append(hot.astype(BF))
            p_scr[b] = hots[-1]
        gather_pair(i, buf, hots, x_scr, local, cap)
        return 0

    lax.fori_loop(0, NB // 2, gather, 0, unroll=2)
    here = pl.ds(plane * rows, rows)
    keep_x = pltpu.make_async_copy(x_scr, x_out.at[:, here, :], sem.at[NB + 3])
    keep_x.start()
    weights.wait()

    def expert(e, _):
        gu = mm(x_scr[e], w_scr[e])
        gate, up = gu[:, :hidden], gu[:, hidden:]
        sig = 1.0 / (1.0 + jnp.exp(-gate))
        silu = gate * sig
        act = (silu * up).astype(BF).astype(F32)
        ue = u[e]
        w = g_scr[e]
        inner = w * ue
        dg = inner * up * sig * (1.0 + gate * (1.0 - sig))
        d = jnp.concatenate([dg, inner * silu], axis=1).astype(BF)
        d_scr[e] = d
        a_scr[e] = (act * w).astype(BF)
        r_scr[e] = act * ue
        z_scr[e] = mm(d, w_scr[e], NT)
        return 0

    lax.fori_loop(0, local, expert, 0, unroll=4 if local % 4 == 0 else 1)
    keep_d = pltpu.make_async_copy(d_scr, d_out.at[:, here, :], sem.at[NB + 4])
    keep_a = pltpu.make_async_copy(a_scr, a_out.at[:, here, :], sem.at[NB + 5])
    keep_d.start()
    keep_a.start()

    for half, out in ((1, sib), (0, own)):

        def combine(i, _):
            b = 4 * half + i
            at = pl.ds(b * cap, cap)
            zb = z_scr[:, at, :].reshape(slots, -1).astype(BF)
            m_scr[b, :BLOCK, :] = mm(p_scr[b], zb, TN).astype(BF)
            pair = jnp.sum(r_scr[:, at, :].reshape(slots, hidden), axis=1, keepdims=True)
            hot = p_scr[b].astype(F32) * pair
            per = jnp.concatenate(
                [
                    jnp.sum(hot[e * cap : (e + 1) * cap, :], axis=0, keepdims=True)
                    for e in range(local)
                ],
                axis=0,
            )
            ids = (lax.broadcasted_iota(jnp.int32, (local, BLOCK), 0) + first[0]).astype(F32)
            pairs = []
            for k in range(TOP):
                mine = tab[b, k : k + 1, :BLOCK] == ids
                pairs.append(jnp.sum(jnp.where(mine, per, 0.0), axis=0, keepdims=True))
            tail = jnp.zeros((TOP, m_scr.shape[2] - BLOCK), F32)
            pairs = jnp.concatenate([jnp.concatenate(pairs, axis=0), tail], axis=1)
            m_scr[b, BLOCK:, :] = pairs.astype(BF)
            pltpu.make_async_copy(m_scr.at[b], out.at[i], out_sem.at[b]).start()
            return 0

        lax.fori_loop(0, 4, combine, 0, unroll=2)
    for half, out in ((1, sib), (0, own)):
        for i in range(4):
            b = 4 * half + i
            pltpu.make_async_copy(m_scr.at[b], out.at[i], out_sem.at[b]).wait()
    keep_x.wait()
    keep_d.wait()
    keep_a.wait()


def expert_rows(plane, planes, first, tab, u, own, sib, wgu, kept, cap):
    local, width, two = wgu.shape
    hidden = two // 2
    rows = NB * cap
    vm = pl.BlockSpec(memory_space=pltpu.VMEM)
    smem = pl.BlockSpec(memory_space=pltpu.SMEM)
    fresh = kept is None
    more = () if fresh else tuple(kept)
    total = planes * rows
    return pl.pallas_call(
        functools.partial(main_body, cap, plane, fresh),
        in_specs=[smem, vm, vm] + [ANY] * (3 + len(more)),
        out_specs=[ANY] * 5,
        out_shape=[
            jax.ShapeDtypeStruct((local, total, width), BF),
            jax.ShapeDtypeStruct((local, total, two), BF),
            jax.ShapeDtypeStruct((local, total, hidden), BF),
            jax.ShapeDtypeStruct((4, BLOCK + TOP, width), BF),
            jax.ShapeDtypeStruct((4, BLOCK + TOP, width), BF),
        ],
        scratch_shapes=[
            pltpu.VMEM((NB, BLOCK, width), BF),
            pltpu.VMEM((local, rows, width), BF),
            pltpu.VMEM((local, width, two), BF),
            pltpu.VMEM((local, rows, width), F32),
            pltpu.VMEM((NB, local * cap, BLOCK), BF),
            pltpu.VMEM((local, rows, hidden), F32),
            pltpu.VMEM((local, rows, hidden), F32),
            pltpu.VMEM((local, rows, two), BF),
            pltpu.VMEM((local, rows, hidden), BF),
            pltpu.VMEM((NB, BLOCK + TOP, width), BF),
            pltpu.SemaphoreType.DMA((NB + 6,)),
            pltpu.SemaphoreType.DMA((NB,)),
        ],
        input_output_aliases={} if fresh else {6: 0, 7: 1, 8: 2},
        compiler_params=params(60),
        cost_estimate=cost(2 * rows * local * (2 * BLOCK + 2 * two) * width, 3e7),
        name="expert_rows",
    )(first, tab, u, own, sib, wgu, *more)


def mix_body(cap, plane, first, tab, a, down, own, sib, y_scr, m_scr, a_scr, sem, out_sem):
    local = down.shape[0]
    slots = local * cap
    rows = NB * cap
    load = pltpu.make_async_copy(a.at[:, pl.ds(plane * rows, rows), :], a_scr, sem)
    load.start()
    load.wait()

    def expert(e, _):
        y_scr[e] = mm(a_scr[e], down[e])
        return 0

    lax.fori_loop(0, local, expert, 0, unroll=4 if local % 4 == 0 else 1)
    for half, out in ((1, sib), (0, own)):

        def combine(i, _):
            b = 4 * half + i
            slot, _g = local_slots(tab[b], first[0], local)
            hot = one_hot(slot, cap).astype(BF)
            yb = y_scr[:, pl.ds(b * cap, cap), :].reshape(slots, -1).astype(BF)
            m_scr[b] = mm(hot, yb, TN).astype(BF)
            pltpu.make_async_copy(m_scr.at[b], out.at[i], out_sem.at[b]).start()
            return 0

        lax.fori_loop(0, 4, combine, 0, unroll=2)
    for half, out in ((1, sib), (0, own)):
        for i in range(4):
            b = 4 * half + i
            pltpu.make_async_copy(m_scr.at[b], out.at[i], out_sem.at[b]).wait()


def mix_rows(plane, first, tab, a, down, cap):
    local, hidden, width = down.shape
    rows = NB * cap
    vm = pl.BlockSpec(memory_space=pltpu.VMEM)
    return pl.pallas_call(
        functools.partial(mix_body, cap, plane),
        in_specs=[pl.BlockSpec(memory_space=pltpu.SMEM), vm, ANY, vm],
        out_specs=[ANY, ANY],
        out_shape=[jax.ShapeDtypeStruct((4, BLOCK, width), BF)] * 2,
        scratch_shapes=[
            pltpu.VMEM((local, rows, width), F32),
            pltpu.VMEM((NB, BLOCK, width), BF),
            pltpu.VMEM((local, rows, hidden), BF),
            pltpu.SemaphoreType.DMA(()),
            pltpu.SemaphoreType.DMA((NB,)),
        ],
        compiler_params=params(50),
        cost_estimate=cost(2 * rows * local * (BLOCK + hidden) * width, 2e7),
        name="mix_rows",
    )(first, tab, a, down)


def weights_body(older, turn, x, s, d, a, *refs):
    hidden = a.shape[2]
    ins, outs = refs[:6], refs[6 + older :]
    done = outs[-1]
    done[0] = turn[0]
    dgu = mm(d[0], x[0], TN).T
    for part in range(2):
        grad = dgu[:, part * hidden : (part + 1) * hidden]
        w, mean, sq = (r[part, 0] for r in ins[:3])
        for ref, val in zip(outs[:4], adam_step(w, grad, mean, sq, WEIGHT_DECAY)):
            ref[part, 0] = val
    ddown = mm(a[0], s[0], TN)
    w, mean, sq = (r[0] for r in ins[3:6])
    for ref, val in zip(outs[4:8], adam_step(w, ddown, mean, sq, WEIGHT_DECAY)):
        ref[0] = val


def weights_step(turn, begin, count, x, s, d, a, up, down, older, cuts=2):
    local, rows, width = x.shape
    hidden = a.shape[2]
    part = width // cuts
    wide = pl.BlockSpec((1, rows, part), lambda e, j: (e + begin, 0, j))
    slim = lambda n: pl.BlockSpec((1, rows, n), lambda e, j: (e + begin, 0, 0))
    ups = pl.BlockSpec((2, 1, part, hidden), lambda e, j: (0, e + begin, j, 0))
    downs = pl.BlockSpec((1, hidden, part), lambda e, j: (e + begin, 0, j))
    smem = pl.BlockSpec(memory_space=pltpu.SMEM)
    out = pl.pallas_call(
        functools.partial(weights_body, len(older)),
        grid=(count, cuts),
        in_specs=[smem, wide, wide, slim(2 * hidden), slim(hidden)]
        + [ups] * 3
        + [downs] * 3
        + [ANY] * len(older),
        out_specs=[ups] * 4 + [downs] * 4 + [smem],
        out_shape=[jax.ShapeDtypeStruct(up[0].shape, F32)] * 4
        + [jax.ShapeDtypeStruct(down[0].shape, F32)] * 4
        + [jax.ShapeDtypeStruct((1,), jnp.int32)],
        input_output_aliases={11 + i: i for i in range(len(older))},
        compiler_params=params(),
        cost_estimate=cost(2 * count * rows * width * 3 * hidden, 26e6 * count),
        name="weights_step",
    )(turn, x, s, d, a, *up, *down, *older)
    return list(out[:8]), out[8]


def experts_by_slot(
    moe_in, cotangent, live_rows, target, gate_values, lengths, up, down, capacity, data_size
):
    tensor_size = lax.axis_size("tensor")
    own_rows, model_width = moe_in.shape
    upgate_low, downproj_low = up[0].astype(BF), down[0].astype(BF)
    local_blocks = upgate_low.shape[1]
    expert_total = local_blocks * data_size
    slots = local_blocks * capacity
    kept = target >= 0
    put_at = jnp.where(kept, target, expert_total * capacity)
    fetch_at = jnp.where(kept, target, 0)
    pair_weight = jnp.where(kept, gate_values.reshape(-1), 0.0)

    def send(pair_rows):
        empty = jnp.zeros((expert_total * capacity, model_width), BF)
        filled = empty.at[put_at].set(pair_rows, mode="drop")
        filled = filled.reshape(1, data_size, slots, model_width)
        wide = lax.all_gather(filled, "tensor", axis=0, tiled=True)
        wide = lax.all_to_all(wide, "dp", split_axis=1, concat_axis=1, tiled=True)
        return wide.reshape(tensor_size, data_size, local_blocks, capacity, model_width)

    def bring(parts):
        parts = parts.reshape(tensor_size, data_size, slots, model_width)
        wide = lax.all_to_all(parts.astype(BF), "dp", split_axis=1, concat_axis=1, tiled=True)
        wide = lax.all_to_all(wide, "tensor", split_axis=0, concat_axis=0, tiled=True)
        summed = jnp.sum(wide.astype(F32), axis=0).astype(BF)
        return summed.reshape(expert_total * capacity, model_width)

    def dot(spec, a, b):
        return jnp.einsum(spec, a, b, preferred_element_type=F32)

    rows_in = send(jnp.repeat(moe_in, TOP, axis=0))
    gate_pre = dot("abecd,edf->abecf", rows_in, upgate_low[0])
    up_pre = dot("abecd,edf->abecf", rows_in, upgate_low[1])
    inner_act = (jax.nn.silu(gate_pre) * up_pre).astype(BF)
    pair_out = bring(dot("abecf,efd->abecd", inner_act, downproj_low))[fetch_at].astype(F32)
    mixed = jnp.sum((pair_weight[:, None] * pair_out).reshape(own_rows, TOP, model_width), axis=1)
    seed_grad = cotangent.astype(F32) * live_rows[:, None].astype(F32)
    seed_pairs = jnp.repeat(seed_grad, TOP, axis=0)
    gate_grad = jnp.where(kept, jnp.sum(pair_out * seed_pairs, axis=1), 0.0)
    out_seed = send((pair_weight[:, None] * seed_pairs).astype(BF))
    inner_grad = dot("abecd,efd->abecf", out_seed, downproj_low)
    down_grad = dot("abecf,abecd->efd", inner_act, out_seed)
    sig = jax.nn.sigmoid(gate_pre)
    gate_back = (inner_grad * up_pre * sig * (1.0 + gate_pre * (1.0 - sig))).astype(BF)
    up_back = (inner_grad * gate_pre * sig).astype(BF)
    up_grad = jnp.stack(
        [
            dot("abecd,abecf->edf", rows_in, gate_back),
            dot("abecd,abecf->edf", rows_in, up_back),
        ]
    )
    rows_grad = dot("abecf,edf->abecd", gate_back, upgate_low[0])
    rows_grad = rows_grad + dot("abecf,edf->abecd", up_back, upgate_low[1])
    back = bring(rows_grad)[fetch_at].astype(F32)
    back = jnp.where(kept[:, None], back, 0.0)
    moe_grad = jnp.sum(back.reshape(own_rows, TOP, model_width), axis=1)
    return (
        mixed,
        gate_grad.reshape(own_rows, TOP),
        moe_grad,
        adam_step(up[0], up_grad, *up[1:], WEIGHT_DECAY),
        adam_step(down[0], down_grad, *down[1:], WEIGHT_DECAY),
    )


def flip(v, axis, bit):
    return lax.ppermute(v, axis, [(i, i ^ bit) for i in range(lax.axis_size(axis))])


def core(v):
    return flip(v, "tensor", 1)


def across(v):
    return flip(v, "tensor", 2)


def side(v):
    return flip(v, "dp", 1)


def onward(v, planes=1):
    n = lax.axis_size("dp")
    return lax.ppermute(v, "dp", [(i, (i + 2 * planes) % n) for i in range(n)])


def plus(*vs):
    return functools.reduce(lambda a, b: a + b, [v.astype(F32) for v in vs]).astype(BF)


def meet(*vs):
    return lax.optimization_barrier(vs)


def group_sum(far, near):
    sent = across(plus(far[0], core(far[1])))
    return plus(near[0], core(near[1])).astype(F32) + sent.astype(F32)


HALF = BLOCK // 2


class Spread:
    def __init__(self, own):
        self.z, self.x, self.y, self.top, self.low, self.own, self.sib = (
            {0: own}, {}, {}, {}, {}, {}, {},
        )

    def on(self, r):
        self.z[r] = onward(self.z[r - 1])

    def x_(self, r):
        self.x[r] = across(self.z[r])

    def y_(self, r):
        self.y[r] = side(self.z[r])

    def wide(self, r):
        self.x_(r), self.y_(r)

    def corner(self, r):
        self.top[r], self.low[r] = side(self.x[r][:HALF]), across(self.y[r][HALF:])

    def cores(self, r):
        z = self.z[r]
        last = jnp.concatenate([self.top.pop(r), self.low.pop(r)], axis=0)
        self.own[r] = jnp.stack([z, self.x.pop(r), self.y.pop(r), last])
        self.sib[r] = core(self.own[r])

    def state(self):
        return [self.z, self.x, self.y, self.top, self.low, self.own, self.sib]

    def put(self, state):
        self.z, self.x, self.y, self.top, self.low, self.own, self.sib = state


class Reduce:
    def __init__(self):
        self.own, self.sib, self.came, self.here, self.x, self.y, self.top, self.low = (
            {} for _ in range(8)
        )
        self.wx, self.wy, self.total = {}, {}, {}

    def cores(self, r):
        self.came[r] = core(self.sib.pop(r))

    def corner(self, r):
        part = plus(self.own.pop(r), self.came.pop(r))
        self.here[r], self.x[r], self.y[r] = part[0], part[1], part[2]
        self.top[r], self.low[r] = side(part[3][:HALF]), across(part[3][HALF:])

    def x_(self, r):
        x = self.x.pop(r)
        self.wx[r] = across(jnp.concatenate([plus(x[:HALF], self.top.pop(r)), x[HALF:]], axis=0))

    def y_(self, r):
        y = self.y.pop(r)
        self.wy[r] = side(jnp.concatenate([y[:HALF], plus(y[HALF:], self.low.pop(r))], axis=0))

    def wide(self, r):
        self.x_(r), self.y_(r)

    def plane(self, r):
        vs = (self.here.pop(r), self.wx.pop(r), self.wy.pop(r))
        if r in self.total:
            vs = vs + (self.total.pop(r),)
        return functools.reduce(lambda a, b: a + b, [v.astype(F32) for v in vs])

    def on(self, r, count):
        self.total[(r + 1) % count] = onward(self.plane(r).astype(BF))

    def state(self):
        return [
            self.own, self.sib, self.came, self.here, self.x, self.y, self.top, self.low,
            self.wx, self.wy, self.total,
        ]

    def put(self, state):
        (
            self.own, self.sib, self.came, self.here, self.x, self.y, self.top, self.low,
            self.wx, self.wy, self.total,
        ) = state


def data_parts(part):
    n = lax.axis_size("dp")
    me = lax.axis_index("dp")
    planes = n // 2
    pairs = part.reshape((planes, 2, part.shape[0] // n) + part.shape[1:])
    mine = lax.dynamic_index_in_dim(pairs, me % 2, 1, keepdims=False)
    other = lax.dynamic_index_in_dim(pairs, 1 - me % 2, 1, keepdims=False)
    order = [((me // 2) + planes - r) % planes for r in range(planes)]
    at = lambda a, r: lax.dynamic_index_in_dim(a, order[r], 0, keepdims=False)
    return tuple(jnp.stack([at(a, r) for r in range(planes)]) for a in (mine, other))


def sum_all(v):
    for axis in ("tensor", "dp"):
        bit = 1
        while bit < lax.axis_size(axis):
            v = v + flip(v, axis, bit)
            bit *= 2
    return v


def pack_weights(query_weight, keyvalue_matrix, outproj_weight, norm_gains):
    return jnp.concatenate(
        [
            query_weight.astype(BF),
            keyvalue_matrix[0].astype(BF),
            keyvalue_matrix[1].astype(BF),
            outproj_weight.astype(BF).T,
            jnp.pad(norm_gains.astype(BF).T, ((0, 0), (0, 126))),
        ],
        axis=1,
    )


def normed(v):
    rms = lax.rsqrt(jnp.mean(v * v, axis=-1, keepdims=True) + NORM_EPS)
    return rms, v * rms


def norm_back(grad, gain, rms, norm):
    scaled = grad * gain
    return rms * (scaled - norm * jnp.mean(scaled * norm, axis=-1, keepdims=True))


def few_groups(
    hidden_in, cotangent, lengths, routes, gate_values, target, live_rows, capacity,
    query_weight, keyvalue_matrix, outproj_weight, norm_gains, up, down,
):
    tensor_index, me = lax.axis_index("tensor"), lax.axis_index("dp")
    count = lax.axis_size("dp") // 2
    qw, kw = query_weight.shape[1], keyvalue_matrix.shape[2]
    share = qw // kw
    local = up[0].shape[1]
    width = hidden_in.shape[1]

    wide = qw + 2 * kw
    out_cols, in_cols = (wide, wide + qw), (0, wide)

    w = [pack_weights(query_weight, keyvalue_matrix, outproj_weight, norm_gains)]
    hx, hc = across(hidden_in), core(hidden_in)
    sides = []
    for r in range(count - 1):
        sides.append(side(w[r]))
        w.append(onward(w[r]))
        w[r + 1], sides[r] = meet(w[r + 1], sides[r])
    sides.append(side(w[-1]))
    hxc = core(hx)
    upgate_low, down_low = up[0].astype(BF), down[0].astype(BF)
    wgu = jnp.concatenate([upgate_low[0], upgate_low[1]], axis=-1)
    places = [(me + 2 * (count - r)) % (2 * count) for r in range(count)]
    weight_places = [p for r in range(count) for p in (places[r], places[r] ^ 1)]
    at = [tensor_index ^ j for j in range(4)] + weight_places
    at = jnp.stack([jnp.asarray(p, jnp.int32) for p in at])
    cos, sin = rope_lanes(4 * BLOCK)

    seeds = jnp.where(live_rows[:, None], cotangent, jnp.zeros((), BF))
    slot = jnp.where(target >= 0, target - routes.reshape(-1) * capacity, -1).reshape(-1, TOP)
    high = gate_values.astype(BF)
    low = (gate_values - high.astype(F32)).astype(BF)
    table = jnp.concatenate([routes.astype(BF).T, slot.astype(BF).T, high.T, low.T], axis=1)
    table = jnp.pad(table, ((0, 0), (0, width - table.shape[1])))
    first = (me * local).astype(jnp.int32).reshape(1)
    c = Spread(jnp.concatenate([seeds, table], axis=0))
    c.z[0], w[-1] = meet(c.z[0], w[-1])
    c.x_(0), c.on(1)

    (rows_of, w, sides, wgu, down_low, cos, sin, st) = meet(
        [hidden_in, hc, hx, hxc], w, sides, wgu, down_low, cos, sin, c.state()
    )
    c.put(st)
    weight_blocks = [b for r in range(count) for b in (w[r], sides[r])]
    attn_in, q, k, v, gains, packed = qkv(at, rows_of, weight_blocks, qw, kw, cos, sin)
    c.y_(0), c.x_(1), c.on(2)
    q, k, v, gains, st = meet(q, k, v, gains, c.state())
    c.put(st)
    gain_attn, gain_moe = gains[0:1], gains[1:2]
    heads, lse = attend(lengths, q, k, v, share)
    c.corner(0), c.y_(1), c.on(3), c.x_(2)
    heads, st = meet(heads, c.state())
    c.put(st)
    far, near = project(at, heads, packed, out_cols)
    far1 = core(far[1])
    c.cores(0)
    far, near, far1, st, first = meet(far, near, far1, c.state(), first)
    c.put(st)
    sent, near1 = across(plus(far[0], far1)), core(near[1])
    us, tabs, kept_s = {}, {}, None

    def seed(r):
        nonlocal kept_s
        kept_s, us[r], tabs[r] = seed_rows(
            r, count, first, c.own.pop(r), c.sib.pop(r), down_low, kept_s, capacity
        )

    seed(0)
    c.y_(2)
    sent, near, near1, us[0], tabs[0], st = meet(sent, near, near1, us[0], tabs[0], c.state())
    c.put(st)
    attn_own = plus(near[0], near1).astype(F32) + sent.astype(F32)
    hidden = hidden_in.astype(F32)
    middle = hidden + attn_own
    rms_moe, normed_moe = normed(middle)
    m = Spread((normed_moe * gain_moe).astype(BF))
    back, mix = Reduce(), Reduce()
    kept, news, turn = None, [], first

    def expert(r):
        nonlocal kept
        x, dgu, act, back.own[r], back.sib[r] = expert_rows(
            r, count, first, tabs[r], us[r], m.own.pop(r), m.sib.pop(r), wgu, kept, capacity
        )
        kept = (x, dgu, act)

    def mixes(r):
        mix.own[r], mix.sib[r] = mix_rows(r, first, tabs[r], kept[2], down_low, capacity)

    def weights(begin, size):
        nonlocal news, turn
        news, turn = weights_step(
            turn, begin, size, kept[0], kept_s, kept[1], kept[2], up, down, news
        )

    def step():
        nonlocal first, us, tabs, turn
        first, turn, us, tabs, sc, sm, sb, sx = meet(
            first, turn, us, tabs, c.state(), m.state(), back.state(), mix.state()
        )
        c.put(sc), m.put(sm), back.put(sb), mix.put(sx)

    m.z[0], st = meet(m.z[0], c.state())
    c.put(st)
    m.wide(0), m.on(1), c.corner(1)
    step()
    m.corner(0), c.wide(3), c.cores(1), m.on(2)
    step()
    m.wide(1), c.corner(2), m.cores(0)
    seed(1)
    step()
    m.corner(1), m.wide(2), c.cores(2), m.on(3)
    expert(0)
    step()
    c.corner(3), m.wide(3), m.cores(1)
    seed(2)
    mixes(0)
    step()
    m.corner(2), c.cores(3), back.cores(0), mix.cores(0)
    expert(1)
    step()
    m.corner(3), m.cores(2), back.corner(0), back.cores(1)
    seed(3)
    mixes(1)
    step()
    back.corner(1), m.cores(3), mix.corner(0), mix.cores(1)
    expert(2)
    step()
    back.wide(1), back.cores(2), mix.corner(1)
    expert(3)
    step()
    back.on(1, count), back.wide(0), back.corner(2), back.cores(3)
    mixes(2)
    mixes(3)
    step()
    back.wide(2), back.corner(3), mix.cores(2)
    weights(0, 2)
    step()
    back.on(2, count), back.wide(3), mix.cores(3)
    weights(2, 2)
    step()
    back.on(3, count), mix.wide(1)
    step()
    whole = back.plane(0)
    gate_grad, moe_grad = whole[BLOCK:, :BLOCK].T, whole[:BLOCK]

    seed_grad = cotangent.astype(F32) * live_rows[:, None].astype(F32)
    gain_moe_part = jnp.sum(moe_grad * normed_moe, axis=0)
    middle_grad = seed_grad + norm_back(moe_grad, gain_moe, rms_moe, normed_moe)
    mid, turn, st = meet(middle_grad.astype(BF), turn, mix.state())
    mix.put(st)
    mx, mc = across(mid), core(mid)
    mix.on(1, count), mix.y_(0)
    weights(4, 2)
    mx, mc, turn, st, gain_moe_part = meet(mx, mc, turn, mix.state(), gain_moe_part)
    mix.put(st)
    mxc = core(mx)
    mix.corner(2)
    heads_grad, middle_low = heads_back(at, [mid, mc, mx, mxc], packed, out_cols)
    omine, oother = data_parts(mm(middle_low, heads, TN).astype(BF))
    heads_grad, omine, oother, st = meet(heads_grad, omine, oother, mix.state())
    mix.put(st)
    dq, dk, dv = attend_back(lengths, q, k, v, heads, heads_grad, lse, cos, sin, share)
    ocame = side(oother)
    mix.x_(0), mix.corner(3)
    dq, dk, dv, ocame, omine, st = meet(dq, dk, dv, ocame, omine, mix.state())
    mix.put(st)
    dqkv = jnp.concatenate([dq, dk, dv], axis=1)
    far, near = project(at, dqkv, packed, in_cols)
    far1 = core(far[1])
    osums = plus(omine, ocame)
    oring = onward(osums[1])
    qmine, qother = data_parts(mm(attn_in, dqkv, TN).astype(BF))
    far, near, far1, oring, osums, qmine, qother, st = meet(
        far, near, far1, oring, osums, qmine, qother, mix.state()
    )
    mix.put(st)
    sent, near1 = across(plus(far[0], far1)), core(near[1])
    qcame = side(qother)
    oring = onward(plus(osums[2], oring))
    weights(6, 2)
    sent, near, near1, qcame, qmine, oring, turn, st = meet(
        sent, near, near1, qcame, qmine, oring, turn, mix.state()
    )
    mix.put(st)
    attn_grad = plus(near[0], near1).astype(F32) + sent.astype(F32)
    rms_attn, normed_attn = normed(hidden)
    gain_attn_part = jnp.sum(attn_grad * normed_attn, axis=0)
    input_grad = middle_grad + norm_back(attn_grad, gain_attn, rms_attn, normed_attn)
    gains_sum = sum_all(jnp.stack([gain_attn_part, gain_moe_part]))
    qsums = plus(qmine, qcame)
    mix.wide(2)
    oring = onward(plus(osums[3], oring))
    qring = onward(qsums[1])
    oring, qring, st = meet(oring, qring, mix.state())
    mix.put(st)
    mix.wide(3), mix.on(2, count)
    qring = onward(plus(qsums[2], qring))
    qring, st = meet(qring, mix.state())
    mix.put(st)
    mix.on(3, count)
    qring = onward(plus(qsums[3], qring))
    outproj_sum = (osums[0].astype(F32) + oring.astype(F32)).T
    qkv_sum = qsums[0].astype(F32) + qring.astype(F32)
    block_out = (middle + mix.plane(0)).astype(BF)
    return (
        block_out, input_grad, gate_grad, qkv_sum, outproj_sum, gains_sum,
        tuple(news[:4]), tuple(news[4:]),
    )


def many_groups(
    hidden_in, cotangent, lengths, routes, gate_values, target, live_rows, capacity,
    query_weight, keyvalue_matrix, outproj_weight, norm_gains, up, down,
):
    qw, kw = query_weight.shape[1], keyvalue_matrix.shape[2]
    share = qw // kw
    packed = pack_weights(query_weight, keyvalue_matrix, outproj_weight, norm_gains)
    packed = lax.all_gather(packed, "dp", axis=0, tiled=True)
    group = lax.all_gather(hidden_in, "tensor", axis=0, tiled=True)
    rows_of = [group[i * BLOCK : (i + 1) * BLOCK] for i in range(4)]
    at = jnp.concatenate([jnp.arange(4, dtype=jnp.int32), jnp.zeros((1,), jnp.int32)])
    cos, sin = rope_lanes(4 * BLOCK)
    attn_in, q, k, v, gains, packed = qkv(at, rows_of, [packed], qw, kw, cos, sin)
    wide = qw + 2 * kw
    qkv_low, outproj_low = packed[:, :wide], packed[:, wide : wide + qw]
    gain_attn, gain_moe = gains[0:1], gains[1:2]
    heads, lse = attend(lengths, q, k, v, share)

    def scattered(part):
        part = lax.psum_scatter(part.astype(BF), "tensor", scatter_dimension=0, tiled=True)
        return part.astype(F32)

    hidden = hidden_in.astype(F32)
    middle = hidden + scattered(mm(heads, outproj_low, NT))
    rms_moe, normed_moe = normed(middle)
    moe_in = (normed_moe * gain_moe).astype(BF)
    mixed, gate_grad, moe_grad, up_new, down_new = experts_by_slot(
        moe_in, cotangent, live_rows, target, gate_values, lengths, up, down, capacity,
        lax.axis_size("dp"),
    )
    block_out = (middle + mixed).astype(BF)
    seed_grad = cotangent.astype(F32) * live_rows[:, None].astype(F32)
    gain_moe_part = jnp.sum(moe_grad * normed_moe, axis=0)
    middle_grad = seed_grad + norm_back(moe_grad, gain_moe, rms_moe, normed_moe)
    middle_low = lax.all_gather(middle_grad.astype(BF), "tensor", axis=0, tiled=True)
    heads_grad = mm(middle_low, outproj_low).astype(BF)
    dq, dk, dv = attend_back(lengths, q, k, v, heads, heads_grad, lse, cos, sin, share)
    dqkv = jnp.concatenate([dq, dk, dv], axis=1)
    attn_grad = scattered(mm(dqkv, qkv_low, NT))
    rms_attn, normed_attn = normed(hidden)
    gain_attn_part = jnp.sum(attn_grad * normed_attn, axis=0)
    input_grad = middle_grad + norm_back(attn_grad, gain_attn, rms_attn, normed_attn)
    gains_sum = lax.psum(jnp.stack([gain_attn_part, gain_moe_part]), ("dp", "tensor"))
    part = jnp.concatenate([mm(attn_in, dqkv, TN), mm(middle_low, heads, TN)], axis=1)
    summed = lax.psum_scatter(part, "dp", scatter_dimension=0, tiled=True)
    return (
        block_out, input_grad, gate_grad, summed[:, :wide], summed[:, wide:].T, gains_sum,
        up_new, down_new,
    )


def on_device(
    hidden_in,
    cotangent,
    lengths,
    routes,
    gate_values,
    pair_order,
    query_weight,
    keyvalue_matrix,
    outproj_weight,
    norm_gains,
    upgate_weight,
    downproj_weight,
    query_mean,
    query_sqmean,
    keyvalue_first_moment,
    keyvalue_second_moment,
    outproj_mean,
    outproj_sqmean,
    gains_mean,
    gains_sqmean,
    upgate_mean,
    upgate_sqmean,
    downproj_mean,
    downproj_sqmean,
):
    tensor_size = lax.axis_size("tensor")
    data_size = lax.axis_size("dp")
    own_rows, model_width = hidden_in.shape
    group_rows = own_rows * tensor_size
    qw = query_weight.shape[1]
    kw = keyvalue_matrix.shape[2]
    assert lengths.shape[0] == 1 and group_rows == SEQUENCE_SLOTS and own_rows == BLOCK

    tensor_index = lax.axis_index("tensor")
    row_ids = tensor_index * own_rows + jnp.arange(own_rows, dtype=jnp.int32)
    live_rows = row_ids < lengths[0]
    capacity = max(2, own_rows * TOP * 5 // (4 * upgate_weight.shape[1] * data_size))
    target = slot_targets(routes.reshape(-1), pair_order[0], jnp.repeat(live_rows, TOP), capacity)
    few = data_size * group_rows * model_width <= 1 << 24
    block_out, input_grad, gate_grad, qkv_sum, outproj_sum, gains_sum, up_new, down_new = (
        few_groups if few else many_groups
    )(
        hidden_in, cotangent, lengths, routes, gate_values, target, live_rows, capacity,
        query_weight, keyvalue_matrix, outproj_weight, norm_gains,
        (upgate_weight, upgate_mean, upgate_sqmean),
        (downproj_weight, downproj_mean, downproj_sqmean),
    )
    own_cols = norm_gains.shape[1]
    gains_sum = lax.dynamic_slice_in_dim(gains_sum, lax.axis_index("dp") * own_cols, own_cols, 1)
    query_sum = qkv_sum[:, :qw]
    keyval_sum = jnp.stack([qkv_sum[:, qw : qw + kw], qkv_sum[:, qw + kw :]])
    return (
        (block_out, input_grad, gate_grad)
        + adam_step(query_weight, query_sum, query_mean, query_sqmean, WEIGHT_DECAY)
        + adam_step(
            keyvalue_matrix, keyval_sum, keyvalue_first_moment, keyvalue_second_moment, WEIGHT_DECAY
        )
        + adam_step(outproj_weight, outproj_sum, outproj_mean, outproj_sqmean, WEIGHT_DECAY)
        + adam_step(norm_gains, gains_sum, gains_mean, gains_sqmean, 0.0)
        + up_new
        + down_new
    )


def solution(mesh):
    placed = (
        P(("dp", "tensor"), None),
        P(("dp", "tensor"), None),
        P("dp"),
        P(("dp", "tensor"), None),
        P(("dp", "tensor"), None),
        P(("dp", "tensor"), None),
        P("dp", "tensor"),
        P(None, "dp", "tensor"),
        P("tensor", "dp"),
        P(None, "dp"),
        P(None, "dp", None, "tensor"),
        P("dp", "tensor", None),
        P("dp", "tensor"),
        P("dp", "tensor"),
        P(None, "dp", "tensor"),
        P(None, "dp", "tensor"),
        P("tensor", "dp"),
        P("tensor", "dp"),
        P(None, "dp"),
        P(None, "dp"),
        P(None, "dp", None, "tensor"),
        P(None, "dp", None, "tensor"),
        P("dp", "tensor", None),
        P("dp", "tensor", None),
    )
    return jax.shard_map(
        on_device,
        mesh=mesh,
        in_specs=placed,
        out_specs=(
            P(("dp", "tensor"), None),
            P(("dp", "tensor"), None),
            P(("dp", "tensor"), None),
            P("dp", "tensor"),
            P("dp", "tensor"),
            P("dp", "tensor"),
            P("dp", "tensor"),
            P(None, "dp", "tensor"),
            P(None, "dp", "tensor"),
            P(None, "dp", "tensor"),
            P(None, "dp", "tensor"),
            P("tensor", "dp"),
            P("tensor", "dp"),
            P("tensor", "dp"),
            P("tensor", "dp"),
            P(None, "dp"),
            P(None, "dp"),
            P(None, "dp"),
            P(None, "dp"),
            P(None, "dp", None, "tensor"),
            P(None, "dp", None, "tensor"),
            P(None, "dp", None, "tensor"),
            P(None, "dp", None, "tensor"),
            P("dp", "tensor", None),
            P("dp", "tensor", None),
            P("dp", "tensor", None),
            P("dp", "tensor", None),
        ),
        check_vma=False,
    )
```

profile of v0, /device:TPU:0, one launch (start us, length us, event | category | flops | bytes accessed | tf_op | source)
XLA Modules:
  0.0 832.4 jit_solution(11138504301066618465)
XLA Ops:
  16.5 5.6 slot_targets.1
  23.5 8.4 %convert_element_type.568 = bf16[2,8,1536,128]{3,2,1,0:T(8,128)(2,1)} convert(f32[2,8,1536,128]{3,2,1,0:T(8,128)} %refs_0_.8) | non-fusion elementwise | flops 3145728 | bytes 18874368 | tf_op jit(solution)/shard_map/convert_element_type | solution.py:1020
  37.6 12.3 %collective-permute-done.5.refs_8_ = bf16[192,1152]{1,0:T(8,128)(2,1)S(1)} collective-permute-done((bf16[192,1152]{1,0:T(8,128)(2,1)S(1)}, bf16[192,1152]{1,0:T(8,128)(2,1)S(1)}, u32[]{:S(2)}, u32[]{:S(2)}) %collective-permute-start.5) | collective-permute-done | bytes 442400 | tf_op jit(solution)/shard_map/ppermute | solution.py:852
  53.1 11.1 %collective-permute-done.7.refs_10_ = bf16[192,1152]{1,0:T(8,128)(2,1)S(1)} collective-permute-done((bf16[192,1152]{1,0:T(8,128)(2,1)S(1)}, bf16[192,1152]{1,0:T(8,128)(2,1)S(1)}, u32[]{:S(2)}, u32[]{:S(2)}) %collective-permute-start.7) | collective-permute-done | bytes 442400 | tf_op jit(solution)/shard_map/ppermute | solution.py:852
  67.5 5.2 convert_element_type.569.refs_0_.down
  78.3 6.9 collective-permute-done.10
  93.6 8.2 qkv.1
  111.7 13.9 %attend.1 = (bf16[1024,384]{1,0:T(8,128)(2,1)S(1)}, f32[3,8,1024]{2,1,0:T(8,128)S(1)}) custom-call(s32[1]{0:T(128)} %copy.140.length, bf16[1024,384]{1,0:T(8,128)(2,1)S(1)} %get-tuple-element.643.q, bf16[1024,128]{1,0:T(8,128)(2,1)S(1)} %get-tuple-element.644.k, bf16[1024,128]{1,0:T(8,128)(2,1)S(1)} %get-tuple-element.645.v), custom_call_target="tpu_custom_call" | custom-call | tf_op jit(solution)/shard_map/attend/pallas_call | solution.py:277
  125.6 5.7 collective-permute-done.18
  147.2 8.5 %seed_rows.4 = (bf16[8,1280,1536]{2,1,0:T(8,128)(2,1)}, f32[8,320,128]{2,1,0:T(8,128)S(1)}, f32[8,8,1024]{2,1,0:T(8,128)S(1)}) custom-call(s32[1]{0:T(128)} %bitcast.29.first.turn, bf16[4,264,1536]{2,1,0:T(8,128)(2,1)} %pad_maximum_fusion.1.own, bf16[4,264,1536]{2,1,0:T(8,128)(2,1)} %collective-permute-done.21.sib, ...), custom_call_target="tpu_custom_call" | custom-call | flops 3019898880 | bytes 20000000 | tf_op jit(solution)/shard_map/seed_rows/pallas_call | solution.py:504
  155.7 8.8 %collective-permute-done.22 = bf16[256,1536]{1,0:T(8,128)(2,1)S(1)} collective-permute-done((bf16[256,1536]{1,0:T(8,128)(2,1)S(1)}, bf16[256,1536]{1,0:T(8,128)(2,1)S(1)}, u32[]{:S(2)}, u32[]{:S(2)}) %collective-permute-start.22) | collective-permute-done | bytes 786464 | tf_op jit(solution)/shard_map/ppermute | solution.py:835
  173.0 22.4 %collective-permute-done.25 = bf16[128,1536]{1,0:T(8,128)(2,1)S(1)} collective-permute-done((bf16[128,1536]{1,0:T(8,128)(2,1)S(1)}, bf16[128,1536]{1,0:T(8,128)(2,1)S(1)}, u32[]{:S(2)}, u32[]{:S(2)}) %collective-permute-start.25) | collective-permute-done | bytes 393248 | tf_op jit(solution)/shard_map/ppermute | solution.py:835
  202.8 24.3 %collective-permute-done.34 = bf16[128,1536]{1,0:T(8,128)(2,1)S(1)} collective-permute-done((bf16[128,1536]{1,0:T(8,128)(2,1)S(1)}, bf16[128,1536]{1,0:T(8,128)(2,1)S(1)}, u32[]{:S(2)}, u32[]{:S(2)}) %collective-permute-start.34) | collective-permute-done | bytes 393248 | tf_op jit(solution)/shard_map/ppermute | solution.py:835
  227.9 9.6 %collective-permute-done.35 = bf16[128,1536]{1,0:T(8,128)(2,1)S(1)} collective-permute-done((bf16[128,1536]{1,0:T(8,128)(2,1)S(1)}, bf16[128,1536]{1,0:T(8,128)(2,1)S(1)}, u32[]{:S(2)}, u32[]{:S(2)}) %collective-permute-start.35) | collective-permute-done | bytes 393248 | tf_op jit(solution)/shard_map/ppermute | solution.py:835
  245.3 8.5 %seed_rows.5 = (bf16[8,1280,1536]{2,1,0:T(8,128)(2,1)}, f32[8,320,128]{2,1,0:T(8,128)S(1)}, f32[8,8,1024]{2,1,0:T(8,128)S(1)}) custom-call(s32[1]{0:T(128)} %bitcast.29.first.turn, bf16[4,264,1536]{2,1,0:T(8,128)(2,1)} %copy-done.56, bf16[4,264,1536]{2,1,0:T(8,128)(2,1)} %copy-done.70, ...), custom_call_target="tpu_custom_call", output_to_operand_aliasing={{0}: (4, {})} | custom-call | flops 3019898880 | bytes 20000000 | tf_op jit(solution)/shard_map/seed_rows/pallas_call | solution.py:504
  253.9 15.3 %collective-permute-done.36 = bf16[128,1536]{1,0:T(8,128)(2,1)S(1)} collective-permute-done((bf16[128,1536]{1,0:T(8,128)(2,1)S(1)}, bf16[128,1536]{1,0:T(8,128)(2,1)S(1)}, u32[]{:S(2)}, u32[]{:S(2)}) %collective-permute-start.36) | collective-permute-done | bytes 393248 | tf_op jit(solution)/shard_map/ppermute | solution.py:835
  278.5 6.1 collective-permute-done.45
  286.6 17.5 %expert_rows.4 = (bf16[8,1280,1536]{2,1,0:T(8,128)(2,1)}, bf16[8,1280,256]{2,1,0:T(8,128)(2,1)}, bf16[8,1280,128]{2,1,0:T(8,128)(2,1)}, bf16[4,264,1536]{2,1,0:T(8,128)(2,1)}, bf16[4,264,1536]{2,1,0:T(8,128)(2,1)}) custom-call(s32[1]{0:T(128)} %bitcast.29.first.turn, f32[8,8,1024]{2,1,0:T(8,128)} %copy-done.47, f32[8,320,128]{2,1,0:T(8,128)} %copy-done.46, ...), custom_call_target="tpu_custom_call" | custom-call | flops 8053063680 | bytes 30000000 | tf_op jit(solution)/shard_map/expert_rows/pallas_call | solution.py:637
  313.5 9.4 %mix_rows.4 = (bf16[4,256,1536]{2,1,0:T(8,128)(2,1)}, bf16[4,256,1536]{2,1,0:T(8,128)(2,1)}) custom-call(s32[1]{0:T(128)} %bitcast.29.first.turn, f32[8,8,1024]{2,1,0:T(8,128)S(1)} %copy-done.48, bf16[8,1280,128]{2,1,0:T(8,128)(2,1)S(1)} %copy-done, bf16[8,128,1536]{2,1,0:T(8,128)(2,1)} %convert_element_type.569.refs_0_.down), custom_call_target="tpu_custom_call" | custom-call | flops 3019898880 | bytes 20000000 | tf_op jit(solution)/shard_map/mix_rows/pallas_call | solution.py:704
  323.0 8.7 %seed_rows.6 = (bf16[8,1280,1536]{2,1,0:T(8,128)(2,1)}, f32[8,320,128]{2,1,0:T(8,128)S(1)}, f32[8,8,1024]{2,1,0:T(8,128)S(1)}) custom-call(s32[1]{0:T(128)} %bitcast.29.first.turn, bf16[4,264,1536]{2,1,0:T(8,128)(2,1)} %pad_maximum_fusion.3.own, bf16[4,264,1536]{2,1,0:T(8,128)(2,1)} %collective-permute-done.41.sib, ...), custom_call_target="tpu_custom_call", output_to_operand_aliasing={{0}: (4, {})} | custom-call | flops 3019898880 | bytes 20000000 | tf_op jit(solution)/shard_map/seed_rows/pallas_call | solution.py:504
  331.7 5.4 collective-permute-done.47
  345.6 17.7 %expert_rows.5 = (bf16[8,1280,1536]{2,1,0:T(8,128)(2,1)}, bf16[8,1280,256]{2,1,0:T(8,128)(2,1)}, bf16[8,1280,128]{2,1,0:T(8,128)(2,1)}, bf16[4,264,1536]{2,1,0:T(8,128)(2,1)}, bf16[4,264,1536]{2,1,0:T(8,128)(2,1)}) custom-call(s32[1]{0:T(128)} %bitcast.29.first.turn, ...), custom_call_target="tpu_custom_call", output_to_operand_aliasing={{0}: (6, {}), {1}: (7, {}), {2}: (8, {})} | custom-call | flops 8053063680 | bytes 30000000 | tf_op jit(solution)/shard_map/expert_rows/pallas_call | solution.py:637
  378.0 7.7 collective-permute-done.61
  387.0 9.3 %mix_rows.5 = (bf16[4,256,1536]{2,1,0:T(8,128)(2,1)}, bf16[4,256,1536]{2,1,0:T(8,128)(2,1)}) custom-call(s32[1]{0:T(128)} %bitcast.29.first.turn, f32[8,8,1024]{2,1,0:T(8,128)S(1)} %copy-done.29, bf16[8,1280,128]{2,1,0:T(8,128)(2,1)S(1)} %copy-done.1, bf16[8,128,1536]{2,1,0:T(8,128)(2,1)} %convert_element_type.569.refs_0_.down), custom_call_target="tpu_custom_call" | custom-call | flops 3019898880 | bytes 20000000 | tf_op jit(solution)/shard_map/mix_rows/pallas_call | solution.py:704
  396.3 8.7 %seed_rows.7 = (bf16[8,1280,1536]{2,1,0:T(8,128)(2,1)}, f32[8,320,128]{2,1,0:T(8,128)S(1)}, f32[8,8,1024]{2,1,0:T(8,128)S(1)}) custom-call(s32[1]{0:T(128)} %bitcast.29.first.turn, bf16[4,264,1536]{2,1,0:T(8,128)(2,1)} %pad_maximum_fusion.4.own, bf16[4,264,1536]{2,1,0:T(8,128)(2,1)} %collective-permute-done.52.sib, ...), custom_call_target="tpu_custom_call", output_to_operand_aliasing={{0}: (4, {})} | custom-call | flops 3019898880 | bytes 20000000 | tf_op jit(solution)/shard_map/seed_rows/pallas_call | solution.py:504
  421.2 17.4 %expert_rows.6 = (bf16[8,1280,1536]{2,1,0:T(8,128)(2,1)}, bf16[8,1280,256]{2,1,0:T(8,128)(2,1)}, bf16[8,1280,128]{2,1,0:T(8,128)(2,1)}, bf16[4,264,1536]{2,1,0:T(8,128)(2,1)}, bf16[4,264,1536]{2,1,0:T(8,128)(2,1)}) custom-call(s32[1]{0:T(128)} %bitcast.29.first.turn, ...), custom_call_target="tpu_custom_call", output_to_operand_aliasing={{0}: (6, {}), {1}: (7, {}), {2}: (8, {})} | custom-call | flops 8053063680 | bytes 30000000 | tf_op jit(solution)/shard_map/expert_rows/pallas_call | solution.py:637
  442.7 8.0 collective-permute-done.64
  461.8 17.8 %expert_rows.7 = (bf16[8,1280,1536]{2,1,0:T(8,128)(2,1)}, bf16[8,1280,256]{2,1,0:T(8,128)(2,1)}, bf16[8,1280,128]{2,1,0:T(8,128)(2,1)}, bf16[4,264,1536]{2,1,0:T(8,128)(2,1)}, bf16[4,264,1536]{2,1,0:T(8,128)(2,1)}) custom-call(s32[1]{0:T(128)} %bitcast.29.first.turn, ...), custom_call_target="tpu_custom_call", output_to_operand_aliasing={{0}: (6, {}), {1}: (7, {}), {2}: (8, {})} | custom-call | flops 8053063680 | bytes 30000000 | tf_op jit(solution)/shard_map/expert_rows/pallas_call | solution.py:637
  498.6 20.7 %collective-permute-done.75 = bf16[128,1536]{1,0:T(8,128)(2,1)} collective-permute-done((bf16[128,1536]{1,0:T(8,128)(2,1)S(1)}, bf16[128,1536]{1,0:T(8,128)(2,1)}, u32[]{:S(2)}, u32[]{:S(2)}) %collective-permute-start.75) | collective-permute-done | bytes 393248 | tf_op jit(solution)/shard_map/ppermute | solution.py:835
  520.1 9.6 %mix_rows.7 = (bf16[4,256,1536]{2,1,0:T(8,128)(2,1)}, bf16[4,256,1536]{2,1,0:T(8,128)(2,1)}) custom-call(s32[1]{0:T(128)} %bitcast.29.first.turn, f32[8,8,1024]{2,1,0:T(8,128)S(1)} %copy-done.27, bf16[8,1280,128]{2,1,0:T(8,128)(2,1)S(1)} %copy-done.2, bf16[8,128,1536]{2,1,0:T(8,128)(2,1)} %convert_element_type.569.refs_0_.down), custom_call_target="tpu_custom_call" | custom-call | flops 3019898880 | bytes 20000000 | tf_op jit(solution)/shard_map/mix_rows/pallas_call | solution.py:704
  529.7 9.3 %mix_rows.6 = (bf16[4,256,1536]{2,1,0:T(8,128)(2,1)}, bf16[4,256,1536]{2,1,0:T(8,128)(2,1)}) custom-call(s32[1]{0:T(128)} %bitcast.29.first.turn, f32[8,8,1024]{2,1,0:T(8,128)S(1)} %copy-done.25, bf16[8,1280,128]{2,1,0:T(8,128)(2,1)S(1)} %copy-done.2, bf16[8,128,1536]{2,1,0:T(8,128)(2,1)} %convert_element_type.569.refs_0_.down), custom_call_target="tpu_custom_call" | custom-call | flops 3019898880 | bytes 20000000 | tf_op jit(solution)/shard_map/mix_rows/pallas_call | solution.py:704
  551.0 17.4 %weights_step.4 = (f32[2,8,1536,128]{3,2,1,0:T(8,128)}, f32[2,8,1536,128]{3,2,1,0:T(8,128)}, f32[2,8,1536,128]{3,2,1,0:T(8,128)}, f32[2,8,1536,128]{3,2,1,0:T(8,...) custom-call(s32[1]{0:T(128)} %bitcast.29.first.turn, ...), custom_call_target="tpu_custom_call" | custom-call | flops 3019898880 | bytes 52000000 | tf_op jit(solution)/shard_map/weights_step/pallas_call | solution.py:748
  568.4 4.5 collective-permute-done.81
  581.7 18.7 %weights_step.5 = (f32[2,8,1536,128]{3,2,1,0:T(8,128)}, f32[2,8,1536,128]{3,2,1,0:T(8,128)}, f32[2,8,1536,128]{3,2,1,0:T(8,128)}, f32[2,8,1536,128]{3,2,1,0:T(8,...) custom-call(s32[1]{0:T(128)} %get-tuple-element.968.turn, ...), custom_call_target="tpu_custom_call", output_to_operand_aliasing={{0}: (11, {}), {1}: (12, {}), {2}: (13, {}), {3}: (14, {}),... | custom-call | flops 3019898880 | bytes 52000000 | tf_op jit(solution)/shard_map/weights_step/pallas_call | solution.py:748
  608.7 13.1 %collective-permute-done.91 = bf16[256,1536]{1,0:T(8,128)(2,1)S(1)} collective-permute-done((bf16[256,1536]{1,0:T(8,128)(2,1)S(1)}, bf16[256,1536]{1,0:T(8,128)(2,1)S(1)}, u32[]{:S(2)}, u32[]{:S(2)}) %collective-permute-start.91) | collective-permute-done | bytes 786464 | tf_op jit(solution)/shard_map/ppermute | solution.py:835
  621.8 4.2 collective-permute-done.90
  637.6 18.2 %weights_step.6 = (f32[2,8,1536,128]{3,2,1,0:T(8,128)}, f32[2,8,1536,128]{3,2,1,0:T(8,128)}, f32[2,8,1536,128]{3,2,1,0:T(8,128)}, f32[2,8,1536,128]{3,2,1,0:T(8,...) custom-call(s32[1]{0:T(128)} %get-tuple-element.1044.turn, ...), custom_call_target="tpu_custom_call", output_to_operand_aliasing={{0}: (11, {}), {1}: (12, {}), {2}: (13, {}), {3}: (14, {}),... | custom-call | flops 3019898880 | bytes 52000000 | tf_op jit(solution)/shard_map/weights_step/pallas_call | solution.py:748
  656.4 3.7 add_convert_fusion.5
  680.8 10.8 %attend_back.1 = (bf16[1024,384]{1,0:T(8,128)(2,1)S(1)}, bf16[1024,128]{1,0:T(8,128)(2,1)S(1)}, bf16[1024,128]{1,0:T(8,128)(2,1)S(1)}) custom-call(s32[1]{0:T(128)} %copy.140.length, bf16[1024,384]{1,0:T(8,128)(2,1)S(1)} %copy-done.12, bf16[1024,128]{1,0:T(8,128)(2,1)S(1)} %copy-done.19, bf16[1024,128]{1,0:T(8,128)(2,1)S(1)} %copy-done.21, ...), custom_call_target="tpu_custom_call" | custom-call | tf_op jit(solution)/shard_map/attend_back/pallas_call | solution.py:378
  692.6 4.2 collective-permute-done.100
  700.9 8.9 %collective-permute-start.104 = (bf16[192,384]{1,0:T(8,128)(2,1)S(1)}, bf16[192,384]{1,0:T(8,128)(2,1)S(1)}, u32[]{:S(2)}, u32[]{:S(2)}) collective-permute-start(bf16[192,384]{1,0:T(8,128)(2,1)S(1)} %slice_bitcast_fusion.50), channel_id=1, source_target_pairs={{0,8},{4,12},{8,16},{12,20},{16,24},{20,28},{24,0},{28,4},{1,9},{5... | collective-permute-start | bytes 442376 | tf_op jit(solution)/shard_map/ppermute | solution.py:852
  723.4 18.3 %weights_step.7 = (f32[2,8,1536,128]{3,2,1,0:T(8,128)}, f32[2,8,1536,128]{3,2,1,0:T(8,128)}, f32[2,8,1536,128]{3,2,1,0:T(8,128)}, f32[2,8,1536,128]{3,2,1,0:T(8,...) custom-call(s32[1]{0:T(128)} %get-tuple-element.1184.turn, ...), custom_call_target="tpu_custom_call", output_to_operand_aliasing={{0}: (11, {}), {1}: (12, {}), {2}: (13, {}), {3}: (14, {}),... | custom-call | flops 3019898880 | bytes 52000000 | tf_op jit(solution)/shard_map/weights_step/pallas_call | solution.py:748
  751.4 16.0 %collective-permute-done.120 = f32[2,1536]{1,0:T(2,128)S(1)} collective-permute-done((f32[2,1536]{1,0:T(2,128)S(1)}, f32[2,1536]{1,0:T(2,128)S(1)}, u32[]{:S(2)}, u32[]{:S(2)}) %collective-permute-start.120) | collective-permute-done | bytes 12320 | tf_op jit(solution)/shard_map/ppermute | solution.py:835
  771.4 5.1 collective-permute-done.122
  785.9 14.7 %collective-permute-done.123 = f32[2,1536]{1,0:T(2,128)S(1)} collective-permute-done((f32[2,1536]{1,0:T(2,128)S(1)}, f32[2,1536]{1,0:T(2,128)S(1)}, u32[]{:S(2)}, u32[]{:S(2)}) %collective-permute-start.123) | collective-permute-done | bytes 12320 | tf_op jit(solution)/shard_map/ppermute | solution.py:835
  802.6 9.6 %collective-permute-done.113 = bf16[192,640]{1,0:T(8,128)(2,1)S(1)} collective-permute-done((bf16[192,640]{1,0:T(8,128)(2,1)S(1)}, bf16[192,640]{1,0:T(8,128)(2,1)S(1)}, u32[]{:S(2)}, u32[]{:S(2)}) %collective-permute-start.113) | collective-permute-done | bytes 245792 | tf_op jit(solution)/shard_map/ppermute | solution.py:852
  812.9 8.3 collective-permute-done.118
  823.3 6.3 collective-permute-done.117
  (732 shorter events, 298.0 us)
Async XLA Ops:
  4.5 30.9 %collective-permute-start.3 = (bf16[192,1152]{1,0:T(8,128)(2,1)S(1)}, bf16[192,1152]{1,0:T(8,128)(2,1)S(1)}, u32[]{:S(2)}, u32[]{:S(2)}) collective-permute-start(bf16[192,1152]{1,0:T(8,128)(2,1)S(1)} %pad_dynamic-update-slice_fusion.refs_4_), channel_id=1, source_target_pairs={{0,8},{4,12},{8,16},{12,20},{16,24},{20,28},{24,0},{28,4},{1,9},{5... | collective-permute-start | bytes 1327112 | tf_op jit(solution)/shard_map/ppermute | solution.py:852
  7.6 27.8 %collective-permute-start.4 = (bf16[192,1152]{1,0:T(8,128)(2,1)S(1)}, bf16[192,1152]{1,0:T(8,128)(2,1)}, u32[]{:S(2)}, u32[]{:S(2)}) collective-permute-start(bf16[192,1152]{1,0:T(8,128)(2,1)S(1)} %pad_dynamic-update-slice_fusion.refs_4_), channel_id=1, source_target_pairs={{0,4},{4,0},{8,12},{12,8},{16,20},{20,16},{24,28},{28,24},{1,5},{5... | collective-permute-start | bytes 1327112 | tf_op jit(solution)/shard_map/ppermute | solution.py:835
  9.1 55.8 %collective-permute-start.1 = (bf16[256,1536]{1,0:T(8,128)(2,1)}, bf16[256,1536]{1,0:T(8,128)(2,1)S(1)}, u32[]{:S(2)}, u32[]{:S(2)}) collective-permute-start(bf16[256,1536]{1,0:T(8,128)(2,1)} %refs_0_.4), channel_id=1, source_target_pairs={{0,2},{1,3},{2,0},{3,1},{4,6},{5,7},{6,4},{7,5},{8,10},{9,11},{10,... | collective-permute-start | bytes 2359304 | tf_op jit(solution)/shard_map/ppermute | solution.py:835
  10.6 65.5 %collective-permute-start = (bf16[256,1536]{1,0:T(8,128)(2,1)}, bf16[256,1536]{1,0:T(8,128)(2,1)}, u32[]{:S(2)}, u32[]{:S(2)}) collective-permute-start(bf16[256,1536]{1,0:T(8,128)(2,1)} %refs_0_.4), channel_id=1, source_target_pairs={{0,1},{1,0},{2,3},{3,2},{4,5},{5,4},{6,7},{7,6},{8,9},{9,8},{10,11... | collective-permute-start | bytes 2359304 | tf_op jit(solution)/shard_map/ppermute | solution.py:835
  167.6 27.8 %collective-permute-start.27 = (bf16[256,1536]{1,0:T(8,128)(2,1)S(1)}, bf16[256,1536]{1,0:T(8,128)(2,1)}, u32[]{:S(2)}, u32[]{:S(2)}) collective-permute-start(bf16[256,1536]{1,0:T(8,128)(2,1)S(1)} %multiply_convert_fusion), channel_id=1, source_target_pairs={{0,8},{4,12},{8,16},{12,20},{16,24},{20,28},{24,0},{28,4},{1,9},{5... | collective-permute-start | bytes 2359304 | tf_op jit(solution)/shard_map/ppermute | solution.py:852
  167.7 27.7 %collective-permute-start.28 = (bf16[256,1536]{1,0:T(8,128)(2,1)S(1)}, bf16[256,1536]{1,0:T(8,128)(2,1)S(1)}, u32[]{:S(2)}, u32[]{:S(2)}) collective-permute-start(bf16[256,1536]{1,0:T(8,128)(2,1)S(1)} %multiply_convert_fusion), channel_id=1, source_target_pairs={{0,2},{1,3},{2,0},{3,1},{4,6},{5,7},{6,4},{7,5},{8,10},{9,11},{10,... | collective-permute-start | bytes 2359304 | tf_op jit(solution)/shard_map/ppermute | solution.py:835
  168.8 26.7 %collective-permute-start.29 = (bf16[256,1536]{1,0:T(8,128)(2,1)S(1)}, bf16[256,1536]{1,0:T(8,128)(2,1)S(1)}, u32[]{:S(2)}, u32[]{:S(2)}) collective-permute-start(bf16[256,1536]{1,0:T(8,128)(2,1)S(1)} %multiply_convert_fusion), channel_id=1, source_target_pairs={{0,4},{4,0},{8,12},{12,8},{16,20},{20,16},{24,28},{28,24},{1,5},{5... | collective-permute-start | bytes 2359304 | tf_op jit(solution)/shard_map/ppermute | solution.py:835
  197.2 41.2 %collective-permute-start.32 = (bf16[4,264,1536]{2,1,0:T(8,128)(2,1)S(1)}, bf16[4,264,1536]{2,1,0:T(8,128)(2,1)S(1)}, u32[]{:S(2)}, u32[]{:S(2)}) collective-permute-start(bf16[4,264,1536]{2,1,0:T(8,128)(2,1)S(1)} %pad_maximum_fusion.2.own), channel_id=1, source_target_pairs={{0,1},{1,0},{2,3},{3,2},{4,5},{5,4},{6,7},{7,6},{8,9},{9,8},{10,11... | collective-permute-start | bytes 9732104 | tf_op jit(solution)/shard_map/ppermute | solution.py:835
  197.3 40.2 %collective-permute-start.30 = (bf16[264,1536]{1,0:T(8,128)(2,1)S(1)}, bf16[264,1536]{1,0:T(8,128)(2,1)S(1)}, u32[]{:S(2)}, u32[]{:S(2)}) collective-permute-start(bf16[264,1536]{1,0:T(8,128)(2,1)S(1)} %copy-done.110), channel_id=1, source_target_pairs={{0,2},{1,3},{2,0},{3,1},{4,6},{5,7},{6,4},{7,5},{8,10},{9,11},{10,... | collective-permute-start | bytes 2433032 | tf_op jit(solution)/shard_map/ppermute | solution.py:835
  198.6 38.9 %collective-permute-start.31 = (bf16[264,1536]{1,0:T(8,128)(2,1)S(1)}, bf16[264,1536]{1,0:T(8,128)(2,1)S(1)}, u32[]{:S(2)}, u32[]{:S(2)}) collective-permute-start(bf16[264,1536]{1,0:T(8,128)(2,1)S(1)} %copy-done.110), channel_id=1, source_target_pairs={{0,4},{4,0},{8,12},{12,8},{16,20},{20,16},{24,28},{28,24},{1,5},{5... | collective-permute-start | bytes 2433032 | tf_op jit(solution)/shard_map/ppermute | solution.py:835
  199.1 28.0 %collective-permute-start.34 = (bf16[128,1536]{1,0:T(8,128)(2,1)S(1)}, bf16[128,1536]{1,0:T(8,128)(2,1)S(1)}, u32[]{:S(2)}, u32[]{:S(2)}) collective-permute-start(bf16[128,1536]{1,0:T(8,128)(2,1)S(1)} %slice.440), channel_id=1, source_target_pairs={{0,4},{4,0},{8,12},{12,8},{16,20},{20,16},{24,28},{28,24},{1,5},{5... | collective-permute-start | bytes 1179656 | tf_op jit(solution)/shard_map/ppermute | solution.py:835
  200.7 36.8 %collective-permute-start.33 = (bf16[256,1536]{1,0:T(8,128)(2,1)}, bf16[256,1536]{1,0:T(8,128)(2,1)S(1)}, u32[]{:S(2)}, u32[]{:S(2)}) collective-permute-start(bf16[256,1536]{1,0:T(8,128)(2,1)} %collective-permute-done.27), channel_id=1, source_target_pairs={{0,8},{4,12},{8,16},{12,20},{16,24},{20,28},{24,0},{28,4},{1,9},{5... | collective-permute-start | bytes 2359304 | tf_op jit(solution)/shard_map/ppermute | solution.py:852
  240.1 29.1 %collective-permute-start.40 = (bf16[4,256,1536]{2,1,0:T(8,128)(2,1)S(1)}, bf16[4,256,1536]{2,1,0:T(8,128)(2,1)}, u32[]{:S(2)}, u32[]{:S(2)}) collective-permute-start(bf16[4,256,1536]{2,1,0:T(8,128)(2,1)S(1)} %pad_maximum_fusion.5.own_in), channel_id=1, source_target_pairs={{0,1},{1,0},{2,3},{3,2},{4,5},{5,4},{6,7},{7,6},{8,9},{9,8},{10,11... | collective-permute-start | bytes 9437192 | tf_op jit(solution)/shard_map/ppermute | solution.py:835
  240.1 29.1 %collective-permute-start.38 = (bf16[256,1536]{1,0:T(8,128)(2,1)}, bf16[256,1536]{1,0:T(8,128)(2,1)S(1)}, u32[]{:S(2)}, u32[]{:S(2)}) collective-permute-start(bf16[256,1536]{1,0:T(8,128)(2,1)} %collective-permute-done.27), channel_id=1, source_target_pairs={{0,2},{1,3},{2,0},{3,1},{4,6},{5,7},{6,4},{7,5},{8,10},{9,11},{10,... | collective-permute-start | bytes 2359304 | tf_op jit(solution)/shard_map/ppermute | solution.py:835
  240.9 28.3 %collective-permute-start.39 = (bf16[256,1536]{1,0:T(8,128)(2,1)}, bf16[256,1536]{1,0:T(8,128)(2,1)S(1)}, u32[]{:S(2)}, u32[]{:S(2)}) collective-permute-start(bf16[256,1536]{1,0:T(8,128)(2,1)} %collective-permute-done.27), channel_id=1, source_target_pairs={{0,4},{4,0},{8,12},{12,8},{16,20},{20,16},{24,28},{28,24},{1,5},{5... | collective-permute-start | bytes 2359304 | tf_op jit(solution)/shard_map/ppermute | solution.py:835
  241.9 27.4 %collective-permute-start.37 = (bf16[136,1536]{1,0:T(8,128)(2,1)S(1)}, bf16[136,1536]{1,0:T(8,128)(2,1)S(1)}, u32[]{:S(2)}, u32[]{:S(2)}) collective-permute-start(bf16[136,1536]{1,0:T(8,128)(2,1)S(1)} %slice.443), channel_id=1, source_target_pairs={{0,2},{1,3},{2,0},{3,1},{4,6},{5,7},{6,4},{7,5},{8,10},{9,11},{10,... | collective-permute-start | bytes 1253384 | tf_op jit(solution)/shard_map/ppermute | solution.py:835
  272.6 31.7 %collective-permute-start.41 = (bf16[4,264,1536]{2,1,0:T(8,128)(2,1)}, bf16[4,264,1536]{2,1,0:T(8,128)(2,1)}, u32[]{:S(2)}, u32[]{:S(2)}) collective-permute-start(bf16[4,264,1536]{2,1,0:T(8,128)(2,1)} %pad_maximum_fusion.3.own), channel_id=1, source_target_pairs={{0,1},{1,0},{2,3},{3,2},{4,5},{5,4},{6,7},{7,6},{8,9},{9,8},{10,11... | collective-permute-start | bytes 9732104 | tf_op jit(solution)/shard_map/ppermute | solution.py:835
  273.7 30.7 %collective-permute-start.42 = (bf16[256,1536]{1,0:T(8,128)(2,1)S(1)}, bf16[256,1536]{1,0:T(8,128)(2,1)}, u32[]{:S(2)}, u32[]{:S(2)}) collective-permute-start(bf16[256,1536]{1,0:T(8,128)(2,1)S(1)} %copy-done.115), channel_id=1, source_target_pairs={{0,8},{4,12},{8,16},{12,20},{16,24},{20,28},{24,0},{28,4},{1,9},{5... | collective-permute-start | bytes 2359304 | tf_op jit(solution)/shard_map/ppermute | solution.py:852
  276.4 27.9 %collective-permute-start.43 = (bf16[256,1536]{1,0:T(8,128)(2,1)S(1)}, bf16[256,1536]{1,0:T(8,128)(2,1)S(1)}, u32[]{:S(2)}, u32[]{:S(2)}) collective-permute-start(bf16[256,1536]{1,0:T(8,128)(2,1)S(1)} %copy-done.115), channel_id=1, source_target_pairs={{0,2},{1,3},{2,0},{3,1},{4,6},{5,7},{6,4},{7,5},{8,10},{9,11},{10,... | collective-permute-start | bytes 2359304 | tf_op jit(solution)/shard_map/ppermute | solution.py:835
  277.2 27.1 %collective-permute-start.44 = (bf16[256,1536]{1,0:T(8,128)(2,1)S(1)}, bf16[256,1536]{1,0:T(8,128)(2,1)S(1)}, u32[]{:S(2)}, u32[]{:S(2)}) collective-permute-start(bf16[256,1536]{1,0:T(8,128)(2,1)S(1)} %copy-done.115), channel_id=1, source_target_pairs={{0,4},{4,0},{8,12},{12,8},{16,20},{20,16},{24,28},{28,24},{1,5},{5... | collective-permute-start | bytes 2359304 | tf_op jit(solution)/shard_map/ppermute | solution.py:835
  307.8 29.3 %collective-permute-start.51 = (bf16[4,256,1536]{2,1,0:T(8,128)(2,1)S(1)}, bf16[4,256,1536]{2,1,0:T(8,128)(2,1)S(1)}, u32[]{:S(2)}, u32[]{:S(2)}) collective-permute-start(bf16[4,256,1536]{2,1,0:T(8,128)(2,1)S(1)} %pad_maximum_fusion.6.own_in), channel_id=1, source_target_pairs={{0,1},{1,0},{2,3},{3,2},{4,5},{5,4},{6,7},{7,6},{8,9},{9,8},{10,11... | collective-permute-start | bytes 9437192 | tf_op jit(solution)/shard_map/ppermute | solution.py:835
  307.8 29.2 %collective-permute-start.49 = (bf16[256,1536]{1,0:T(8,128)(2,1)}, bf16[256,1536]{1,0:T(8,128)(2,1)S(1)}, u32[]{:S(2)}, u32[]{:S(2)}) collective-permute-start(bf16[256,1536]{1,0:T(8,128)(2,1)} %collective-permute-done.42), channel_id=1, source_target_pairs={{0,2},{1,3},{2,0},{3,1},{4,6},{5,7},{6,4},{7,5},{8,10},{9,11},{10,... | collective-permute-start | bytes 2359304 | tf_op jit(solution)/shard_map/ppermute | solution.py:835
  308.7 28.4 %collective-permute-start.50 = (bf16[256,1536]{1,0:T(8,128)(2,1)}, bf16[256,1536]{1,0:T(8,128)(2,1)S(1)}, u32[]{:S(2)}, u32[]{:S(2)}) collective-permute-start(bf16[256,1536]{1,0:T(8,128)(2,1)} %collective-permute-done.42), channel_id=1, source_target_pairs={{0,4},{4,0},{8,12},{12,8},{16,20},{20,16},{24,28},{28,24},{1,5},{5... | collective-permute-start | bytes 2359304 | tf_op jit(solution)/shard_map/ppermute | solution.py:835
  365.0 40.1 %collective-permute-start.60 = (bf16[4,264,1536]{2,1,0:T(8,128)(2,1)}, bf16[4,264,1536]{2,1,0:T(8,128)(2,1)}, u32[]{:S(2)}, u32[]{:S(2)}) collective-permute-start(bf16[4,264,1536]{2,1,0:T(8,128)(2,1)} %get-tuple-element.840), channel_id=1, source_target_pairs={{0,1},{1,0},{2,3},{3,2},{4,5},{5,4},{6,7},{7,6},{8,9},{9,8},{10,11... | collective-permute-start | bytes 9732104 | tf_op jit(solution)/shard_map/ppermute | solution.py:835
  367.9 37.2 %collective-permute-start.59 = (bf16[4,256,1536]{2,1,0:T(8,128)(2,1)S(1)}, bf16[4,256,1536]{2,1,0:T(8,128)(2,1)}, u32[]{:S(2)}, u32[]{:S(2)}) collective-permute-start(bf16[4,256,1536]{2,1,0:T(8,128)(2,1)S(1)} %pad_maximum_fusion.7.own_in), channel_id=1, source_target_pairs={{0,1},{1,0},{2,3},{3,2},{4,5},{5,4},{6,7},{7,6},{8,9},{9,8},{10,11... | collective-permute-start | bytes 9437192 | tf_op jit(solution)/shard_map/ppermute | solution.py:835
  372.9 32.2 %collective-permute-start.62 = (bf16[136,1536]{1,0:T(8,128)(2,1)}, bf16[136,1536]{1,0:T(8,128)(2,1)}, u32[]{:S(2)}, u32[]{:S(2)}) collective-permute-start(bf16[136,1536]{1,0:T(8,128)(2,1)} %slice_bitcast_fusion.33), channel_id=1, source_target_pairs={{0,2},{1,3},{2,0},{3,1},{4,6},{5,7},{6,4},{7,5},{8,10},{9,11},{10,... | collective-permute-start | bytes 1253384 | tf_op jit(solution)/shard_map/ppermute | solution.py:835
  375.3 29.7 %collective-permute-start.57 = (bf16[128,1536]{1,0:T(8,128)(2,1)}, bf16[128,1536]{1,0:T(8,128)(2,1)S(1)}, u32[]{:S(2)}, u32[]{:S(2)}) collective-permute-start(bf16[128,1536]{1,0:T(8,128)(2,1)} %slice.450), channel_id=1, source_target_pairs={{0,4},{4,0},{8,12},{12,8},{16,20},{20,16},{24,28},{28,24},{1,5},{5... | collective-permute-start | bytes 1179656 | tf_op jit(solution)/shard_map/ppermute | solution.py:835
  409.7 30.2 %collective-permute-start.67 = (bf16[128,1536]{1,0:T(8,128)(2,1)}, bf16[128,1536]{1,0:T(8,128)(2,1)}, u32[]{:S(2)}, u32[]{:S(2)}) collective-permute-start(bf16[128,1536]{1,0:T(8,128)(2,1)} %get-tuple-element.1259), channel_id=1, source_target_pairs={{0,4},{4,0},{8,12},{12,8},{16,20},{20,16},{24,28},{28,24},{1,5},{5... | collective-permute-start | bytes 1179656 | tf_op jit(solution)/shard_map/ppermute | solution.py:835
  410.4 32.3 %collective-permute-start.68 = (bf16[128,1536]{1,0:T(8,128)(2,1)}, bf16[128,1536]{1,0:T(8,128)(2,1)}, u32[]{:S(2)}, u32[]{:S(2)}) collective-permute-start(bf16[128,1536]{1,0:T(8,128)(2,1)} %get-tuple-element.1258), channel_id=1, source_target_pairs={{0,2},{1,3},{2,0},{3,1},{4,6},{5,7},{6,4},{7,5},{8,10},{9,11},{10,... | collective-permute-start | bytes 1179656 | tf_op jit(solution)/shard_map/ppermute | solution.py:835
  414.3 36.4 %collective-permute-start.63 = (bf16[4,256,1536]{2,1,0:T(8,128)(2,1)}, bf16[4,256,1536]{2,1,0:T(8,128)(2,1)}, u32[]{:S(2)}, u32[]{:S(2)}) collective-permute-start(bf16[4,256,1536]{2,1,0:T(8,128)(2,1)} %pad_maximum_fusion.8.own_in), channel_id=1, source_target_pairs={{0,1},{1,0},{2,3},{3,2},{4,5},{5,4},{6,7},{7,6},{8,9},{9,8},{10,11... | collective-permute-start | bytes 9437192 | tf_op jit(solution)/shard_map/ppermute | solution.py:835
  414.3 36.4 %collective-permute-start.66 = (bf16[4,256,1536]{2,1,0:T(8,128)(2,1)}, bf16[4,256,1536]{2,1,0:T(8,128)(2,1)}, u32[]{:S(2)}, u32[]{:S(2)}) collective-permute-start(bf16[4,256,1536]{2,1,0:T(8,128)(2,1)} %get-tuple-element.873), channel_id=1, source_target_pairs={{0,1},{1,0},{2,3},{3,2},{4,5},{5,4},{6,7},{7,6},{8,9},{9,8},{10,11... | collective-permute-start | bytes 9437192 | tf_op jit(solution)/shard_map/ppermute | solution.py:835
  418.5 32.2 %collective-permute-start.65 = (bf16[136,1536]{1,0:T(8,128)(2,1)}, bf16[136,1536]{1,0:T(8,128)(2,1)}, u32[]{:S(2)}, u32[]{:S(2)}) collective-permute-start(bf16[136,1536]{1,0:T(8,128)(2,1)} %slice_bitcast_fusion.32), channel_id=1, source_target_pairs={{0,2},{1,3},{2,0},{3,1},{4,6},{5,7},{6,4},{7,5},{8,10},{9,11},{10,... | collective-permute-start | bytes 1253384 | tf_op jit(solution)/shard_map/ppermute | solution.py:835
  450.7 34.0 %collective-permute-start.69 = (bf16[4,264,1536]{2,1,0:T(8,128)(2,1)}, bf16[4,264,1536]{2,1,0:T(8,128)(2,1)}, u32[]{:S(2)}, u32[]{:S(2)}) collective-permute-start(bf16[4,264,1536]{2,1,0:T(8,128)(2,1)} %get-tuple-element.889), channel_id=1, source_target_pairs={{0,1},{1,0},{2,3},{3,2},{4,5},{5,4},{6,7},{7,6},{8,9},{9,8},{10,11... | collective-permute-start | bytes 9732104 | tf_op jit(solution)/shard_map/ppermute | solution.py:835
  454.5 26.6 %collective-permute-start.72 = (bf16[128,1536]{1,0:T(8,128)(2,1)}, bf16[128,1536]{1,0:T(8,128)(2,1)}, u32[]{:S(2)}, u32[]{:S(2)}) collective-permute-start(bf16[128,1536]{1,0:T(8,128)(2,1)} %get-tuple-element.1254), channel_id=1, source_target_pairs={{0,4},{4,0},{8,12},{12,8},{16,20},{20,16},{24,28},{28,24},{1,5},{5... | collective-permute-start | bytes 1179656 | tf_op jit(solution)/shard_map/ppermute | solution.py:835
  487.3 51.7 %collective-permute-start.79 = (bf16[264,1536]{1,0:T(8,128)(2,1)}, bf16[264,1536]{1,0:T(8,128)(2,1)}, u32[]{:S(2)}, u32[]{:S(2)}) collective-permute-start(bf16[264,1536]{1,0:T(8,128)(2,1)} %add_convert_fusion.11), channel_id=1, source_target_pairs={{0,8},{4,12},{8,16},{12,20},{16,24},{20,28},{24,0},{28,4},{1,9},{5... | collective-permute-start | bytes 2433032 | tf_op jit(solution)/shard_map/ppermute | solution.py:852
  491.5 47.6 %collective-permute-start.78 = (bf16[264,1536]{1,0:T(8,128)(2,1)}, bf16[264,1536]{1,0:T(8,128)(2,1)}, u32[]{:S(2)}, u32[]{:S(2)}) collective-permute-start(bf16[264,1536]{1,0:T(8,128)(2,1)} %pad_maximum_fusion.15), channel_id=1, source_target_pairs={{0,4},{4,0},{8,12},{12,8},{16,20},{20,16},{24,28},{28,24},{1,5},{5... | collective-permute-start | bytes 2433032 | tf_op jit(solution)/shard_map/ppermute | solution.py:835
  492.5 46.6 %collective-permute-start.74 = (bf16[4,264,1536]{2,1,0:T(8,128)(2,1)}, bf16[4,264,1536]{2,1,0:T(8,128)(2,1)S(1)}, u32[]{:S(2)}, u32[]{:S(2)}) collective-permute-start(bf16[4,264,1536]{2,1,0:T(8,128)(2,1)} %get-tuple-element.912), channel_id=1, source_target_pairs={{0,1},{1,0},{2,3},{3,2},{4,5},{5,4},{6,7},{7,6},{8,9},{9,8},{10,11... | collective-permute-start | bytes 9732104 | tf_op jit(solution)/shard_map/ppermute | solution.py:835
  493.6 45.5 %collective-permute-start.77 = (bf16[264,1536]{1,0:T(8,128)(2,1)}, bf16[264,1536]{1,0:T(8,128)(2,1)}, u32[]{:S(2)}, u32[]{:S(2)}) collective-permute-start(bf16[264,1536]{1,0:T(8,128)(2,1)} %pad_maximum_fusion.14), channel_id=1, source_target_pairs={{0,2},{1,3},{2,0},{3,1},{4,6},{5,7},{6,4},{7,5},{8,10},{9,11},{10,... | collective-permute-start | bytes 2433032 | tf_op jit(solution)/shard_map/ppermute | solution.py:835
  541.0 31.9 %collective-permute-start.83 = (bf16[264,1536]{1,0:T(8,128)(2,1)S(1)}, bf16[264,1536]{1,0:T(8,128)(2,1)S(1)}, u32[]{:S(2)}, u32[]{:S(2)}) collective-permute-start(bf16[264,1536]{1,0:T(8,128)(2,1)S(1)} %pad_maximum_fusion.17), channel_id=1, source_target_pairs={{0,4},{4,0},{8,12},{12,8},{16,20},{20,16},{24,28},{28,24},{1,5},{5... | collective-permute-start | bytes 2433032 | tf_op jit(solution)/shard_map/ppermute | solution.py:835
  542.0 30.8 %collective-permute-start.84 = (bf16[4,256,1536]{2,1,0:T(8,128)(2,1)}, bf16[4,256,1536]{2,1,0:T(8,128)(2,1)}, u32[]{:S(2)}, u32[]{:S(2)}) collective-permute-start(bf16[4,256,1536]{2,1,0:T(8,128)(2,1)} %get-tuple-element.957), channel_id=1, source_target_pairs={{0,1},{1,0},{2,3},{3,2},{4,5},{5,4},{6,7},{7,6},{8,9},{9,8},{10,11... | collective-permute-start | bytes 9437192 | tf_op jit(solution)/shard_map/ppermute | solution.py:835
  543.3 29.6 %collective-permute-start.82 = (bf16[264,1536]{1,0:T(8,128)(2,1)S(1)}, bf16[264,1536]{1,0:T(8,128)(2,1)}, u32[]{:S(2)}, u32[]{:S(2)}) collective-permute-start(bf16[264,1536]{1,0:T(8,128)(2,1)S(1)} %pad_maximum_fusion.16), channel_id=1, source_target_pairs={{0,2},{1,3},{2,0},{3,1},{4,6},{5,7},{6,4},{7,5},{8,10},{9,11},{10,... | collective-permute-start | bytes 2433032 | tf_op jit(solution)/shard_map/ppermute | solution.py:835
  572.9 27.9 %collective-permute-start.88 = (bf16[4,256,1536]{2,1,0:T(8,128)(2,1)}, bf16[4,256,1536]{2,1,0:T(8,128)(2,1)}, u32[]{:S(2)}, u32[]{:S(2)}) collective-permute-start(bf16[4,256,1536]{2,1,0:T(8,128)(2,1)} %get-tuple-element.993), channel_id=1, source_target_pairs={{0,1},{1,0},{2,3},{3,2},{4,5},{5,4},{6,7},{7,6},{8,9},{9,8},{10,11... | collective-permute-start | bytes 9437192 | tf_op jit(solution)/shard_map/ppermute | solution.py:835
  673.8 26.8 %collective-permute-start.102 = (bf16[256,1536]{1,0:T(8,128)(2,1)S(1)}, bf16[256,1536]{1,0:T(8,128)(2,1)S(1)}, u32[]{:S(2)}, u32[]{:S(2)}) collective-permute-start(bf16[256,1536]{1,0:T(8,128)(2,1)S(1)} %pad_maximum_fusion.23), channel_id=1, source_target_pairs={{0,2},{1,3},{2,0},{3,1},{4,6},{5,7},{6,4},{7,5},{8,10},{9,11},{10,... | collective-permute-start | bytes 2359304 | tf_op jit(solution)/shard_map/ppermute | solution.py:835
  746.8 30.2 %collective-permute-start.112 = (bf16[256,1536]{1,0:T(8,128)(2,1)S(1)}, bf16[256,1536]{1,0:T(8,128)(2,1)S(1)}, u32[]{:S(2)}, u32[]{:S(2)}) collective-permute-start(bf16[256,1536]{1,0:T(8,128)(2,1)S(1)} %pad_maximum_fusion.25), channel_id=1, source_target_pairs={{0,4},{4,0},{8,12},{12,8},{16,20},{20,16},{24,28},{28,24},{1,5},{5... | collective-permute-start | bytes 2359304 | tf_op jit(solution)/shard_map/ppermute | solution.py:835
  747.7 29.4 %collective-permute-start.111 = (bf16[256,1536]{1,0:T(8,128)(2,1)S(1)}, bf16[256,1536]{1,0:T(8,128)(2,1)S(1)}, u32[]{:S(2)}, u32[]{:S(2)}) collective-permute-start(bf16[256,1536]{1,0:T(8,128)(2,1)S(1)} %pad_maximum_fusion.24), channel_id=1, source_target_pairs={{0,2},{1,3},{2,0},{3,1},{4,6},{5,7},{6,4},{7,5},{8,10},{9,11},{10,... | collective-permute-start | bytes 2359304 | tf_op jit(solution)/shard_map/ppermute | solution.py:835
  778.6 33.5 %collective-permute-start.116 = (bf16[256,1536]{1,0:T(8,128)(2,1)S(1)}, bf16[256,1536]{1,0:T(8,128)(2,1)S(1)}, u32[]{:S(2)}, u32[]{:S(2)}) collective-permute-start(bf16[256,1536]{1,0:T(8,128)(2,1)S(1)} %add_convert_fusion.14), channel_id=1, source_target_pairs={{0,8},{4,12},{8,16},{12,20},{16,24},{20,28},{24,0},{28,4},{1,9},{5... | collective-permute-start | bytes 2359304 | tf_op jit(solution)/shard_map/ppermute | solution.py:852
  780.8 31.4 %collective-permute-start.115 = (bf16[256,1536]{1,0:T(8,128)(2,1)S(1)}, bf16[256,1536]{1,0:T(8,128)(2,1)S(1)}, u32[]{:S(2)}, u32[]{:S(2)}) collective-permute-start(bf16[256,1536]{1,0:T(8,128)(2,1)S(1)} %pad_maximum_fusion.27), channel_id=1, source_target_pairs={{0,4},{4,0},{8,12},{12,8},{16,20},{20,16},{24,28},{28,24},{1,5},{5... | collective-permute-start | bytes 2359304 | tf_op jit(solution)/shard_map/ppermute | solution.py:835
  781.3 30.8 %collective-permute-start.114 = (bf16[256,1536]{1,0:T(8,128)(2,1)S(1)}, bf16[256,1536]{1,0:T(8,128)(2,1)S(1)}, u32[]{:S(2)}, u32[]{:S(2)}) collective-permute-start(bf16[256,1536]{1,0:T(8,128)(2,1)S(1)} %pad_maximum_fusion.26), channel_id=1, source_target_pairs={{0,2},{1,3},{2,0},{3,1},{4,6},{5,7},{6,4},{7,5},{8,10},{9,11},{10,... | collective-permute-start | bytes 2359304 | tf_op jit(solution)/shard_map/ppermute | solution.py:835
  (230 other events, 2958.1 us)
where the time goes:
time: 840 us; the launch traced here: 832 us
  waiting for transfers between devices  276 us (33%)
  Pallas kernels  263 us (31%)
  other arithmetic  121 us (14%)
  starting transfers between devices  107 us (13%)
  local copies, waits for them, and re-layouts  57.1 us (7%)
    ppermute x103, waiting for transfers between devices, flip(): lax.ppermute(v, axis, [(i, i ^ bit) for i in range(lax.axis_size(axis))])  216 us
    ppermute x103, starting transfers between devices, flip(): lax.ppermute(v, axis, [(i, i ^ bit) for i in range(lax.axis_size(axis))])  80 us
    pallas_call x4, Pallas kernels, weights_step(): pl.pallas_call(functools.partial(weights_body, len(older)), grid=(count,...  72.5 us
    pallas_call x4, Pallas kernels, expert_rows(): pl.pallas_call(functools.partial(main_body, cap, plane, fresh), in_specs=...  70.4 us
    ppermute x21, waiting for transfers between devices, onward(): return lax.ppermute(v, 'dp', [(i, (i + 2 * planes) % n) for i in range(n)])  59.9 us
    convert_element_type x32, other arithmetic, plus(): functools.reduce(lambda a, b: a + b, [v.astype(F32) for v in vs]).astype(BF)  39.8 us
    pallas_call x4, Pallas kernels, mix_rows(): pl.pallas_call(functools.partial(mix_body, cap, plane), in_specs=[pl.Bloc...  37.6 us
    pallas_call x4, Pallas kernels, seed_rows(): pl.pallas_call(functools.partial(seed_body, cap, plane, fresh), in_specs=...  34.4 us
  transfers between devices with their start and end apart: 124, of which 39 were waited for; matrix products, arithmetic and copies ran while one was open for 14% of the time, Pallas kernels for 32%

commit v1 on v0

--- a/solution.py
+++ b/solution.py
@@ -157,20 +157,16 @@
             pltpu.VMEM((rows, width), BF),
             pltpu.SemaphoreType.DMA((len(xs) + len(ws),)),
         ],
-        compiler_params=params(32),
+        compiler_params=params(60),
         cost_estimate=cost(2 * rows * width * cols, 2e7),
         name="qkv",
     )(at, *xs, *ws, cos, sin)
 
 
-def project_body(cols, at, v, w, far, near):
-    def block(i, _):
-        for j, out in ((2, far), (0, near)):
-            rows = pl.ds(pl.multiple_of(at[j + i] * BLOCK, BLOCK), BLOCK)
-            out[i] = mm(v[rows, :], w[:, cols[0] : cols[1]], NT).astype(BF)
-        return 0
-
-    lax.fori_loop(0, 2, block, 0)
+def project_body(cols, at, v, w, *outs):
+    for i, out in enumerate(outs):
+        rows = pl.ds(pl.multiple_of(at[i] * BLOCK, BLOCK), BLOCK)
+        out[...] = mm(v[rows, :], w[:, cols[0] : cols[1]], NT).astype(BF)
 
 
 def project(at, v, w, cols):
@@ -180,8 +176,8 @@
     return pl.pallas_call(
         functools.partial(project_body, cols),
         in_specs=[pl.BlockSpec(memory_space=pltpu.SMEM), vm, vm],
-        out_specs=[vm] * 2,
-        out_shape=[jax.ShapeDtypeStruct((2, BLOCK, width), BF)] * 2,
+        out_specs=[vm] * 4,
+        out_shape=[jax.ShapeDtypeStruct((BLOCK, width), BF)] * 4,
         compiler_params=params(32),
         cost_estimate=cost(2 * rows * depth * width, 1e7),
         name="project",
@@ -719,6 +715,37 @@
     )(first, tab, a, down)
 
 
+def round_body(turn, up, down, wgu, low):
+    hidden = low.shape[1]
+    for part in range(2):
+        wgu[0, :, part * hidden : (part + 1) * hidden] = up[part, 0].astype(BF)
+    low[0] = down[0].astype(BF)
+
+
+def round_weights(turn, up, down):
+    local, hidden, width = down.shape
+    return pl.pallas_call(
+        round_body,
+        grid=(local,),
+        in_specs=[
+            pl.BlockSpec(memory_space=pltpu.SMEM),
+            pl.BlockSpec((2, 1, width, hidden), lambda e: (0, e, 0, 0)),
+            pl.BlockSpec((1, hidden, width), lambda e: (e, 0, 0)),
+        ],
+        out_specs=[
+            pl.BlockSpec((1, width, 2 * hidden), lambda e: (e, 0, 0)),
+            pl.BlockSpec((1, hidden, width), lambda e: (e, 0, 0)),
+        ],
+        out_shape=[
+            jax.ShapeDtypeStruct((local, width, 2 * hidden), BF),
+            jax.ShapeDtypeStruct((local, hidden, width), BF),
+        ],
+        compiler_params=params(32),
+        cost_estimate=cost(0, 28e6),
+        name="round_weights",
+    )(turn, up, down)
+
+
 def weights_body(older, turn, x, s, d, a, *refs):
     hidden = a.shape[2]
     ins, outs = refs[:6], refs[6 + older :]
@@ -860,19 +887,9 @@
     return lax.optimization_barrier(vs)
 
 
-def group_sum(far, near):
-    sent = across(plus(far[0], core(far[1])))
-    return plus(near[0], core(near[1])).astype(F32) + sent.astype(F32)
-
-
-HALF = BLOCK // 2
-
-
 class Spread:
     def __init__(self, own):
-        self.z, self.x, self.y, self.top, self.low, self.own, self.sib = (
-            {0: own}, {}, {}, {}, {}, {}, {},
-        )
+        self.z, self.x, self.y, self.d, self.own, self.sib = {0: own}, {}, {}, {}, {}, {}
 
     def on(self, r):
         self.z[r] = onward(self.z[r - 1])
@@ -883,55 +900,64 @@
     def y_(self, r):
         self.y[r] = side(self.z[r])
 
-    def wide(self, r):
-        self.x_(r), self.y_(r)
-
-    def corner(self, r):
-        self.top[r], self.low[r] = side(self.x[r][:HALF]), across(self.y[r][HALF:])
+    def x_on(self, r):
+        self.x[r] = onward(self.x[r - 1])
+
+    def y_on(self, r):
+        self.y[r] = onward(self.y[r - 1])
+
+    def d_(self, r):
+        self.d[r] = across(self.y[r]) if r % 2 else side(self.x[r])
 
     def cores(self, r):
-        z = self.z[r]
-        last = jnp.concatenate([self.top.pop(r), self.low.pop(r)], axis=0)
-        self.own[r] = jnp.stack([z, self.x.pop(r), self.y.pop(r), last])
+        self.own[r] = jnp.stack([self.z[r], self.x[r], self.y[r], self.d.pop(r)])
         self.sib[r] = core(self.own[r])
 
     def state(self):
-        return [self.z, self.x, self.y, self.top, self.low, self.own, self.sib]
+        return [self.z, self.x, self.y, self.d, self.own, self.sib]
 
     def put(self, state):
-        self.z, self.x, self.y, self.top, self.low, self.own, self.sib = state
+        self.z, self.x, self.y, self.d, self.own, self.sib = state
 
 
 class Reduce:
     def __init__(self):
-        self.own, self.sib, self.came, self.here, self.x, self.y, self.top, self.low = (
-            {} for _ in range(8)
-        )
-        self.wx, self.wy, self.total = {}, {}, {}
+        self.own, self.sib, self.parts, self.d = {}, {}, {}, {}
+        self.wx, self.wy, self.zx, self.zy, self.total = {}, {}, {}, {}, {}
 
     def cores(self, r):
-        self.came[r] = core(self.sib.pop(r))
-
-    def corner(self, r):
-        part = plus(self.own.pop(r), self.came.pop(r))
-        self.here[r], self.x[r], self.y[r] = part[0], part[1], part[2]
-        self.top[r], self.low[r] = side(part[3][:HALF]), across(part[3][HALF:])
+        own, came = self.own.pop(r), core(self.sib.pop(r))
+        self.parts[r] = [plus(own[i], came[i]) for i in range(4)]
+
+    def part(self, r, i):
+        vs = [self.parts[r][i]]
+        if i == (2 if r % 2 else 1) and r in self.d:
+            vs.append(self.d[r])
+        if r == 0 and i == 1:
+            vs.append(self.zx[1])
+        if r == 0 and i == 2:
+            vs.append(self.zy[1])
+        return vs
+
+    def d_(self, r):
+        v = plus(*self.part(r, 3))
+        self.d[r] = across(v) if r % 2 else side(v)
 
     def x_(self, r):
-        x = self.x.pop(r)
-        self.wx[r] = across(jnp.concatenate([plus(x[:HALF], self.top.pop(r)), x[HALF:]], axis=0))
+        self.wx[r] = across(plus(*self.part(r, 1)))
 
     def y_(self, r):
-        y = self.y.pop(r)
-        self.wy[r] = side(jnp.concatenate([y[:HALF], plus(y[HALF:], self.low.pop(r))], axis=0))
-
-    def wide(self, r):
-        self.x_(r), self.y_(r)
+        self.wy[r] = side(plus(*self.part(r, 2)))
+
+    def x_in(self, r):
+        self.zx[r] = onward(plus(*self.part(r, 1)), -1)
+
+    def y_in(self, r):
+        self.zy[r] = onward(plus(*self.part(r, 2)), -1)
 
     def plane(self, r):
-        vs = (self.here.pop(r), self.wx.pop(r), self.wy.pop(r))
-        if r in self.total:
-            vs = vs + (self.total.pop(r),)
+        vs = self.part(r, 0)
+        vs = vs + [w.pop(r) for w in (self.wx, self.wy, self.total) if r in w]
         return functools.reduce(lambda a, b: a + b, [v.astype(F32) for v in vs])
 
     def on(self, r, count):
@@ -939,14 +965,14 @@
 
     def state(self):
         return [
-            self.own, self.sib, self.came, self.here, self.x, self.y, self.top, self.low,
-            self.wx, self.wy, self.total,
+            self.own, self.sib, self.parts, self.d,
+            self.wx, self.wy, self.zx, self.zy, self.total,
         ]
 
     def put(self, state):
         (
-            self.own, self.sib, self.came, self.here, self.x, self.y, self.top, self.low,
-            self.wx, self.wy, self.total,
+            self.own, self.sib, self.parts, self.d,
+            self.wx, self.wy, self.zx, self.zy, self.total,
         ) = state
 
 
@@ -960,15 +986,6 @@
     order = [((me // 2) + planes - r) % planes for r in range(planes)]
     at = lambda a, r: lax.dynamic_index_in_dim(a, order[r], 0, keepdims=False)
     return tuple(jnp.stack([at(a, r) for r in range(planes)]) for a in (mine, other))
-
-
-def sum_all(v):
-    for axis in ("tensor", "dp"):
-        bit = 1
-        while bit < lax.axis_size(axis):
-            v = v + flip(v, axis, bit)
-            bit *= 2
-    return v
 
 
 def pack_weights(query_weight, keyvalue_matrix, outproj_weight, norm_gains):
@@ -1008,7 +1025,8 @@
     wide = qw + 2 * kw
     out_cols, in_cols = (wide, wide + qw), (0, wide)
 
-    w = [pack_weights(query_weight, keyvalue_matrix, outproj_weight, norm_gains)]
+    own_packed = pack_weights(query_weight, keyvalue_matrix, outproj_weight, norm_gains)
+    w = [own_packed]
     hx, hc = across(hidden_in), core(hidden_in)
     sides = []
     for r in range(count - 1):
@@ -1017,8 +1035,6 @@
         w[r + 1], sides[r] = meet(w[r + 1], sides[r])
     sides.append(side(w[-1]))
     hxc = core(hx)
-    upgate_low, down_low = up[0].astype(BF), down[0].astype(BF)
-    wgu = jnp.concatenate([upgate_low[0], upgate_low[1]], axis=-1)
     places = [(me + 2 * (count - r)) % (2 * count) for r in range(count)]
     weight_places = [p for r in range(count) for p in (places[r], places[r] ^ 1)]
     at = [tensor_index ^ j for j in range(4)] + weight_places
@@ -1033,29 +1049,31 @@
     table = jnp.pad(table, ((0, 0), (0, width - table.shape[1])))
     first = (me * local).astype(jnp.int32).reshape(1)
     c = Spread(jnp.concatenate([seeds, table], axis=0))
-    c.z[0], w[-1] = meet(c.z[0], w[-1])
-    c.x_(0), c.on(1)
-
-    (rows_of, w, sides, wgu, down_low, cos, sin, st) = meet(
-        [hidden_in, hc, hx, hxc], w, sides, wgu, down_low, cos, sin, c.state()
+    c.z[0], w[2], hx = meet(c.z[0], w[2], hx)
+    c.x_(0)
+    c.z[0], w[3] = meet(c.z[0], w[3])
+    c.on(1)
+
+    (rows_of, w, sides, cos, sin, st) = meet(
+        [hidden_in, hc, hx, hxc], w, sides, cos, sin, c.state()
     )
     c.put(st)
     weight_blocks = [b for r in range(count) for b in (w[r], sides[r])]
     attn_in, q, k, v, gains, packed = qkv(at, rows_of, weight_blocks, qw, kw, cos, sin)
-    c.y_(0), c.x_(1), c.on(2)
+    c.x_(1), c.y_(0), c.on(2)
     q, k, v, gains, st = meet(q, k, v, gains, c.state())
     c.put(st)
     gain_attn, gain_moe = gains[0:1], gains[1:2]
     heads, lse = attend(lengths, q, k, v, share)
-    c.corner(0), c.y_(1), c.on(3), c.x_(2)
+    c.x_(2), c.d_(0), c.on(3)
     heads, st = meet(heads, c.state())
     c.put(st)
-    far, near = project(at, heads, packed, out_cols)
-    far1 = core(far[1])
-    c.cores(0)
-    far, near, far1, st, first = meet(far, near, far1, c.state(), first)
+    near0, near1, far0, far1 = project(at, heads, packed, out_cols)
+    far1 = core(far1)
+    c.y_(1), c.cores(0)
+    near0, near1, far0, far1, st, first = meet(near0, near1, far0, far1, c.state(), first)
     c.put(st)
-    sent, near1 = across(plus(far[0], far1)), core(near[1])
+    sent, near1 = across(plus(far0, far1)), core(near1)
     us, tabs, kept_s = {}, {}, None
 
     def seed(r):
@@ -1064,11 +1082,11 @@
             r, count, first, c.own.pop(r), c.sib.pop(r), down_low, kept_s, capacity
         )
 
-    seed(0)
     c.y_(2)
-    sent, near, near1, us[0], tabs[0], st = meet(sent, near, near1, us[0], tabs[0], c.state())
+    wgu, down_low = round_weights(first, up[0], down[0])
+    sent, near0, near1, wgu, down_low, st = meet(sent, near0, near1, wgu, down_low, c.state())
     c.put(st)
-    attn_own = plus(near[0], near1).astype(F32) + sent.astype(F32)
+    attn_own = plus(near0, near1).astype(F32) + sent.astype(F32)
     hidden = hidden_in.astype(F32)
     middle = hidden + attn_own
     rms_moe, normed_moe = normed(middle)
@@ -1101,106 +1119,115 @@
 
     m.z[0], st = meet(m.z[0], c.state())
     c.put(st)
-    m.wide(0), m.on(1), c.corner(1)
+    m.x_(0), m.y_(0), m.on(1)
+    seed(0)
     step()
-    m.corner(0), c.wide(3), c.cores(1), m.on(2)
+    c.d_(1), m.d_(0), m.y_on(1)
     step()
-    m.wide(1), c.corner(2), m.cores(0)
-    seed(1)
+    m.d_(1), c.d_(2), m.on(2), c.cores(1), m.cores(0)
     step()
-    m.corner(1), m.wide(2), c.cores(2), m.on(3)
+    m.x_(2), m.y_(2), m.x_on(1), c.cores(2)
     expert(0)
     step()
-    c.corner(3), m.wide(3), m.cores(1)
+    c.x_(3), m.d_(2), m.on(3), m.cores(1), back.cores(0)
+    seed(1)
     seed(2)
+    step()
+    m.x_(3), c.y_(3), m.cores(2)
+    expert(1)
+    step()
+    c.d_(3), m.y_(3), back.cores(1)
+    expert(2)
+    step()
+    m.d_(3), back.d_(0), back.x_in(1), c.cores(3), back.cores(2)
     mixes(0)
     step()
-    m.corner(2), c.cores(3), back.cores(0), mix.cores(0)
-    expert(1)
-    step()
-    m.corner(3), m.cores(2), back.corner(0), back.cores(1)
+    back.d_(1), back.d_(2), back.on(1, count), m.cores(3), mix.cores(0)
     seed(3)
     mixes(1)
     step()
-    back.corner(1), m.cores(3), mix.corner(0), mix.cores(1)
-    expert(2)
-    step()
-    back.wide(1), back.cores(2), mix.corner(1)
+    back.x_(2), back.y_(2), back.y_in(1), mix.cores(1)
     expert(3)
     step()
-    back.on(1, count), back.wide(0), back.corner(2), back.cores(3)
+    mix.d_(1), mix.d_(0), back.on(2, count), back.cores(3)
     mixes(2)
+    step()
+    back.d_(3), mix.x_in(1), mix.cores(2)
     mixes(3)
     step()
-    back.wide(2), back.corner(3), mix.cores(2)
+    back.x_(3), back.y_(3), mix.y_in(1), mix.cores(3)
     weights(0, 2)
     step()
-    back.on(2, count), back.wide(3), mix.cores(3)
+    back.x_(0), back.y_(0), back.on(3, count)
     weights(2, 2)
-    step()
-    back.on(3, count), mix.wide(1)
     step()
     whole = back.plane(0)
     gate_grad, moe_grad = whole[BLOCK:, :BLOCK].T, whole[:BLOCK]
 
     seed_grad = cotangent.astype(F32) * live_rows[:, None].astype(F32)
-    gain_moe_part = jnp.sum(moe_grad * normed_moe, axis=0)
+    gain_sum = jnp.sum(moe_grad * normed_moe, axis=0, keepdims=True)
     middle_grad = seed_grad + norm_back(moe_grad, gain_moe, rms_moe, normed_moe)
     mid, turn, st = meet(middle_grad.astype(BF), turn, mix.state())
     mix.put(st)
     mx, mc = across(mid), core(mid)
-    mix.on(1, count), mix.y_(0)
+    mix.d_(2), mix.on(1, count)
     weights(4, 2)
-    mx, mc, turn, st, gain_moe_part = meet(mx, mc, turn, mix.state(), gain_moe_part)
+    mx, mc, turn, st, gain_sum = meet(mx, mc, turn, mix.state(), gain_sum)
     mix.put(st)
     mxc = core(mx)
-    mix.corner(2)
+    mix.x_(0), mix.y_(0)
+    gain_sum = gain_sum + flip(gain_sum, "tensor", 1)
     heads_grad, middle_low = heads_back(at, [mid, mc, mx, mxc], packed, out_cols)
     omine, oother = data_parts(mm(middle_low, heads, TN).astype(BF))
-    heads_grad, omine, oother, st = meet(heads_grad, omine, oother, mix.state())
+    heads_grad, omine, oother, gain_sum, st = meet(
+        heads_grad, omine, oother, gain_sum, mix.state()
+    )
     mix.put(st)
     dq, dk, dv = attend_back(lengths, q, k, v, heads, heads_grad, lse, cos, sin, share)
     ocame = side(oother)
-    mix.x_(0), mix.corner(3)
-    dq, dk, dv, ocame, omine, st = meet(dq, dk, dv, ocame, omine, mix.state())
+    mix.d_(3), mix.x_(2), mix.y_(2)
+    gain_sum = gain_sum + flip(gain_sum, "tensor", 2)
+    dq, dk, dv, ocame, omine, gain_sum, st = meet(dq, dk, dv, ocame, omine, gain_sum, mix.state())
     mix.put(st)
     dqkv = jnp.concatenate([dq, dk, dv], axis=1)
-    far, near = project(at, dqkv, packed, in_cols)
-    far1 = core(far[1])
+    near0, near1, far0, far1 = project(at, dqkv, packed, in_cols)
+    far1 = core(far1)
     osums = plus(omine, ocame)
-    oring = onward(osums[1])
+    ohere = [osums[0]] + [onward(osums[r], -r) for r in range(1, count)]
     qmine, qother = data_parts(mm(attn_in, dqkv, TN).astype(BF))
-    far, near, far1, oring, osums, qmine, qother, st = meet(
-        far, near, far1, oring, osums, qmine, qother, mix.state()
+    gain_sum = gain_sum + flip(gain_sum, "dp", 1)
+    near0, near1, far0, far1, ohere, qmine, qother, gain_sum, st = meet(
+        near0, near1, far0, far1, ohere, qmine, qother, gain_sum, mix.state()
     )
     mix.put(st)
-    sent, near1 = across(plus(far[0], far1)), core(near[1])
+    sent, near1 = across(plus(far0, far1)), core(near1)
     qcame = side(qother)
-    oring = onward(plus(osums[2], oring))
+    mix.on(2, count)
     weights(6, 2)
-    sent, near, near1, qcame, qmine, oring, turn, st = meet(
-        sent, near, near1, qcame, qmine, oring, turn, mix.state()
+    sent, near0, near1, qcame, qmine, turn, gain_sum, st = meet(
+        sent, near0, near1, qcame, qmine, turn, gain_sum, mix.state()
     )
     mix.put(st)
-    attn_grad = plus(near[0], near1).astype(F32) + sent.astype(F32)
+    attn_grad = plus(near0, near1).astype(F32) + sent.astype(F32)
     rms_attn, normed_attn = normed(hidden)
-    gain_attn_part = jnp.sum(attn_grad * normed_attn, axis=0)
     input_grad = middle_grad + norm_back(attn_grad, gain_attn, rms_attn, normed_attn)
-    gains_sum = sum_all(jnp.stack([gain_attn_part, gain_moe_part]))
     qsums = plus(qmine, qcame)
-    mix.wide(2)
-    oring = onward(plus(osums[3], oring))
-    qring = onward(qsums[1])
-    oring, qring, st = meet(oring, qring, mix.state())
-    mix.put(st)
-    mix.wide(3), mix.on(2, count)
-    qring = onward(plus(qsums[2], qring))
-    qring, st = meet(qring, mix.state())
+    qhere = [qsums[0]] + [onward(qsums[r], -r) for r in range(1, count)]
+    mix.x_(3), mix.y_(3)
+    qhere, gain_sum, st = meet(qhere, gain_sum, mix.state())
     mix.put(st)
     mix.on(3, count)
-    qring = onward(plus(qsums[3], qring))
-    outproj_sum = (osums[0].astype(F32) + oring.astype(F32)).T
-    qkv_sum = qsums[0].astype(F32) + qring.astype(F32)
+    gain_sum = gain_sum + flip(gain_sum, "dp", 2)
+    gain_sum = gain_sum + flip(gain_sum, "dp", 4)
+    outproj_sum = functools.reduce(lambda a, b: a + b, [o.astype(F32) for o in ohere]).T
+    qkv_sum = functools.reduce(lambda a, b: a + b, [q.astype(F32) for q in qhere])
+    own_gains = norm_gains.astype(BF).astype(F32)
+    gain_part = jnp.sum(own_packed[:, :wide].astype(F32) * qkv_sum, axis=1)[None, :]
+    gain_part = gain_part + flip(gain_part, "tensor", 1)
+    gain_part = gain_part + flip(gain_part, "tensor", 2)
+    own_cols = norm_gains.shape[1]
+    gain_moe_own = lax.dynamic_slice_in_dim(gain_sum, me * own_cols, own_cols, 1)
+    gains_sum = jnp.concatenate([gain_part / own_gains[0:1], gain_moe_own], axis=0)
     block_out = (middle + mix.plane(0)).astype(BF)
     return (
         block_out, input_grad, gate_grad, qkv_sum, outproj_sum, gains_sum,
@@ -1251,6 +1278,8 @@
     gain_attn_part = jnp.sum(attn_grad * normed_attn, axis=0)
     input_grad = middle_grad + norm_back(attn_grad, gain_attn, rms_attn, normed_attn)
     gains_sum = lax.psum(jnp.stack([gain_attn_part, gain_moe_part]), ("dp", "tensor"))
+    own_cols = norm_gains.shape[1]
+    gains_sum = lax.dynamic_slice_in_dim(gains_sum, lax.axis_index("dp") * own_cols, own_cols, 1)
     part = jnp.concatenate([mm(attn_in, dqkv, TN), mm(middle_low, heads, TN)], axis=1)
     summed = lax.psum_scatter(part, "dp", scatter_dimension=0, tiled=True)
     return (
@@ -1307,8 +1336,6 @@
         (upgate_weight, upgate_mean, upgate_sqmean),
         (downproj_weight, downproj_mean, downproj_sqmean),
     )
-    own_cols = norm_gains.shape[1]
-    gains_sum = lax.dynamic_slice_in_dim(gains_sum, lax.axis_index("dp") * own_cols, own_cols, 1)
     query_sum = qkv_sum[:, :qw]
     keyval_sum = jnp.stack([qkv_sum[:, qw : qw + kw], qkv_sum[:, qw + kw :]])
     return (

time: 840 us -> 714 us (0.85)
  waiting for transfers between devices: 276 us -> 189 us
  local copies, waits for them, and re-layouts: 57.1 us -> 31 us
  Pallas kernels: 263 us -> 279 us
  other arithmetic: 121 us -> 106 us
  starting transfers between devices: 107 us -> 93.4 us
    ppermute x103 -> x83, waiting for transfers between devices: 216 us -> 80.4 us  [flip(): lax.ppermute(v, axis, [(i, i ^ bit) for i in range(lax.axis_size(axis))])]
    ppermute x21 -> x27, waiting for transfers between devices: 59.9 us -> 109 us  [onward(): return lax.ppermute(v, 'dp', [(i, (i + 2 * planes) % n) for i in range(n)])]
    ppermute x103 -> x83, starting transfers between devices: 80 us -> 63.5 us  [flip(): lax.ppermute(v, axis, [(i, i ^ bit) for i in range(lax.axis_size(axis))])]
    slice x44 -> x0, local copies, waits for them, and re-layouts: 15.1 us -> none  [the longest x12 6.44 us: corner(): self.top[r], self.low[r] = (side(part[3][:HALF]), across(part[3][HALF:]))]
    convert_element_type x2 -> x0, other arithmetic: 13.6 us -> none  [few_groups(): upgate_low, down_low = (up[0].astype(BF), down[0].astype(BF))]
    squeeze x15 -> x2, local copies, waits for them, and re-layouts: 13.8 us -> 0.81 us  [the longest x1 0.72 us: few_groups(): ohere = [osums[0]] + [onward(osums[r], -r) for r in range(1, count)]]
    convert_element_type x32 -> x22, other arithmetic: 39.8 us -> 47.3 us  [plus(): functools.reduce(lambda a, b: a + b, [v.astype(F32) for v in vs]).astype(BF)]
    another operation x18 -> x9, other arithmetic: 22.6 us -> 17.3 us  [the longest x8 16.3 us: cores(): self.own[r] = jnp.stack([self.z[r], self.x[r], self.y[r], self.d.pop(r)])]
  transfers between devices with their start and end apart: 124 -> 110, of which waited for: 39 -> 31; matrix products, arithmetic and copies ran while one was open for 14% -> 13% of each run, Pallas kernels for 32% -> 39%
where the time goes in v1:
time: 714 us; the launch traced here: 708 us
  Pallas kernels  279 us (39%)
  waiting for transfers between devices  189 us (26%)
  other arithmetic  106 us (15%)
  starting transfers between devices  93.4 us (13%)
  local copies, waits for them, and re-layouts  31 us (4%)
    ppermute x27, waiting for transfers between devices, onward(): return lax.ppermute(v, 'dp', [(i, (i + 2 * planes) % n) for i in range(n)])  109 us
    ppermute x83, waiting for transfers between devices, flip(): lax.ppermute(v, axis, [(i, i ^ bit) for i in range(lax.axis_size(axis))])  80.4 us
    pallas_call x4, Pallas kernels, weights_step(): pl.pallas_call(functools.partial(weights_body, len(older)), grid=(count,...  72.3 us
    pallas_call x4, Pallas kernels, expert_rows(): pl.pallas_call(functools.partial(main_body, cap, plane, fresh), in_specs=...  70.7 us
    ppermute x83, starting transfers between devices, flip(): lax.ppermute(v, axis, [(i, i ^ bit) for i in range(lax.axis_size(axis))])  63.5 us
    convert_element_type x22, other arithmetic, plus(): functools.reduce(lambda a, b: a + b, [v.astype(F32) for v in vs]).astype(BF)  47.3 us
    pallas_call x4, Pallas kernels, mix_rows(): pl.pallas_call(functools.partial(mix_body, cap, plane), in_specs=[pl.Bloc...  37.9 us
    pallas_call x4, Pallas kernels, seed_rows(): pl.pallas_call(functools.partial(seed_body, cap, plane, fresh), in_specs=...  34.5 us
  transfers between devices with their start and end apart: 110, of which 31 were waited for; matrix products, arithmetic and copies ran while one was open for 13% of the time, Pallas kernels for 39%

profile of v1, /device:TPU:0, one launch (start us, length us, event | category | flops | bytes accessed | tf_op | source)
XLA Modules:
  0.0 708.0 jit_solution(17855512963471567359)
XLA Ops:
  17.4 6.1 collective-permute-done.1.refs_6_
  26.5 5.6 slot_targets.1
  41.0 8.3 %collective-permute-done.7.refs_10_ = bf16[192,1152]{1,0:T(8,128)(2,1)S(1)} collective-permute-done((bf16[192,1152]{1,0:T(8,128)(2,1)}, bf16[192,1152]{1,0:T(8,128)(2,1)S(1)}, u32[]{:S(2)}, u32[]{:S(2)}) %collective-permute-start.7) | collective-permute-done | bytes 442400 | tf_op jit(solution)/shard_map/ppermute | solution.py:879
  57.3 5.4 collective-permute-done.9.refs_11_
  62.7 6.7 collective-permute-done.10
  72.5 11.1 %qkv.1 = (bf16[1024,1536]{1,0:T(8,128)(2,1)}, bf16[1024,384]{1,0:T(8,128)(2,1)}, bf16[1024,128]{1,0:T(8,128)(2,1)}, bf16[1024,128]{1,0:T(8,128)(2,1)}, f32[8,1536]{1,0:T(8,128)}, /*index=5*/bf16[1536,1152]{1,0:T(8,128)(2,1)}) custom-call(s32[12]{0:T(128)} %stack.208.at, bf16[256,1536]{1,0:T(8,128)(2,1)} %refs_0_.4, bf16[256,1536]{1,0:T(8,128)(2,1)} %copy-done.122, ...), custom_call_target="tpu_custom_call" | custom-call | flops 3623878656 | bytes 20000000 | tf_op jit(solution)/shard_map/qkv/pallas_call | solution.py:142
  83.6 4.3 collective-permute-done.12
  93.4 13.9 %attend.1 = (bf16[1024,384]{1,0:T(8,128)(2,1)S(1)}, f32[3,8,1024]{2,1,0:T(8,128)S(1)}) custom-call(s32[1]{0:T(128)} %copy.194.length, bf16[1024,384]{1,0:T(8,128)(2,1)S(1)} %copy-done.10, bf16[1024,128]{1,0:T(8,128)(2,1)S(1)} %copy-done.15, bf16[1024,128]{1,0:T(8,128)(2,1)S(1)} %copy-done.17), custom_call_target="tpu_custom_call" | custom-call | tf_op jit(solution)/shard_map/attend/pallas_call | solution.py:273
  114.6 3.8 collective-permute-done.18
  118.4 13.7 %collective-permute-done.19 = bf16[264,1536]{1,0:T(8,128)(2,1)} collective-permute-done((bf16[264,1536]{1,0:T(8,128)(2,1)}, bf16[264,1536]{1,0:T(8,128)(2,1)}, u32[]{:S(2)}, u32[]{:S(2)}) %collective-permute-start.19) | collective-permute-done | bytes 811040 | tf_op jit(solution)/shard_map/ppermute | solution.py:862
  139.8 7.1 %round_weights.1 = (bf16[8,1536,256]{2,1,0:T(8,128)(2,1)S(1)}, bf16[8,128,1536]{2,1,0:T(8,128)(2,1)S(1)}) custom-call(s32[1]{0:T(128)} %bitcast.26.turn.first, f32[2,8,1536,128]{3,2,1,0:T(8,128)} %refs_0_.8, f32[8,128,1536]{2,1,0:T(8,128)S(1)} %copy-done), custom_call_target="tpu_custom_call" | custom-call | bytes 28000000 | tf_op jit(solution)/shard_map/round_weights/pallas_call | solution.py:727
  157.3 8.5 %seed_rows.4 = (bf16[8,1280,1536]{2,1,0:T(8,128)(2,1)}, f32[8,320,128]{2,1,0:T(8,128)S(1)}, f32[8,8,1024]{2,1,0:T(8,128)S(1)}) custom-call(s32[1]{0:T(128)} %bitcast.26.turn.first, bf16[4,264,1536]{2,1,0:T(8,128)(2,1)} %pad_maximum_fusion.own, bf16[4,264,1536]{2,1,0:T(8,128)(2,1)} %collective-permute-done.20.sib, bf16[8,128,1536]{2,1,0:T(8,128)(2,1)} %copy-done.4), custom_call_target="tpu_custom_call" | custom-call | flops 3019898880 | bytes 20000000 | tf_op jit(solution)/shard_map/seed_rows/pallas_call | solution.py:500
  165.9 9.2 %collective-permute-done.24 = bf16[256,1536]{1,0:T(8,128)(2,1)} collective-permute-done((bf16[256,1536]{1,0:T(8,128)(2,1)S(1)}, bf16[256,1536]{1,0:T(8,128)(2,1)}, u32[]{:S(2)}, u32[]{:S(2)}) %collective-permute-start.24) | collective-permute-done | bytes 786464 | tf_op jit(solution)/shard_map/ppermute | solution.py:879
  178.7 16.7 %collective-permute-done.28 = bf16[256,1536]{1,0:T(8,128)(2,1)S(1)} collective-permute-done((bf16[256,1536]{1,0:T(8,128)(2,1)S(1)}, bf16[256,1536]{1,0:T(8,128)(2,1)S(1)}, u32[]{:S(2)}, u32[]{:S(2)}) %collective-permute-start.28) | collective-permute-done | bytes 786464 | tf_op jit(solution)/shard_map/ppermute | solution.py:879
  202.4 20.2 %collective-permute-done.32 = bf16[256,1536]{1,0:T(8,128)(2,1)} collective-permute-done((bf16[256,1536]{1,0:T(8,128)(2,1)}, bf16[256,1536]{1,0:T(8,128)(2,1)}, u32[]{:S(2)}, u32[]{:S(2)}) %collective-permute-start.32) | collective-permute-done | bytes 786464 | tf_op jit(solution)/shard_map/ppermute | solution.py:879
  228.1 17.5 %expert_rows.4 = (bf16[8,1280,1536]{2,1,0:T(8,128)(2,1)}, bf16[8,1280,256]{2,1,0:T(8,128)(2,1)}, bf16[8,1280,128]{2,1,0:T(8,128)(2,1)}, bf16[4,264,1536]{2,1,0:T(8,128)(2,1)}, bf16[4,264,1536]{2,1,0:T(8,128)(2,1)}) custom-call(s32[1]{0:T(128)} %bitcast.26.turn.first, f32[8,8,1024]{2,1,0:T(8,128)} %copy-done.32, f32[8,320,128]{2,1,0:T(8,128)} %copy-done.31, ...), custom_call_target="tpu_custom_call" | custom-call | flops 8053063680 | bytes 30000000 | tf_op jit(solution)/shard_map/expert_rows/pallas_call | solution.py:633
  252.5 8.5 %seed_rows.5 = (bf16[8,1280,1536]{2,1,0:T(8,128)(2,1)}, f32[8,320,128]{2,1,0:T(8,128)S(1)}, f32[8,8,1024]{2,1,0:T(8,128)S(1)}) custom-call(s32[1]{0:T(128)} %bitcast.26.turn.first, bf16[4,264,1536]{2,1,0:T(8,128)(2,1)} %copy-done.38, bf16[4,264,1536]{2,1,0:T(8,128)(2,1)} %copy-done.56, ...), custom_call_target="tpu_custom_call", output_to_operand_aliasing={{0}: (4, {})} | custom-call | flops 3019898880 | bytes 20000000 | tf_op jit(solution)/shard_map/seed_rows/pallas_call | solution.py:500
  262.9 8.7 %seed_rows.6 = (bf16[8,1280,1536]{2,1,0:T(8,128)(2,1)}, f32[8,320,128]{2,1,0:T(8,128)S(1)}, f32[8,8,1024]{2,1,0:T(8,128)S(1)}) custom-call(s32[1]{0:T(128)} %bitcast.26.turn.first, bf16[4,264,1536]{2,1,0:T(8,128)(2,1)} %copy-done.40, bf16[4,264,1536]{2,1,0:T(8,128)(2,1)} %collective-permute-done.35.sib, ...), custom_call_target="tpu_custom_call", output_to_operand_aliasing={{0}: (4, {})} | custom-call | flops 3019898880 | bytes 20000000 | tf_op jit(solution)/shard_map/seed_rows/pallas_call | solution.py:500
  278.4 17.5 %expert_rows.5 = (bf16[8,1280,1536]{2,1,0:T(8,128)(2,1)}, bf16[8,1280,256]{2,1,0:T(8,128)(2,1)}, bf16[8,1280,128]{2,1,0:T(8,128)(2,1)}, bf16[4,264,1536]{2,1,0:T(8,128)(2,1)}, bf16[4,264,1536]{2,1,0:T(8,128)(2,1)}) custom-call(s32[1]{0:T(128)} %bitcast.26.turn.first, ...), custom_call_target="tpu_custom_call", output_to_operand_aliasing={{0}: (6, {}), {1}: (7, {}), {2}: (8, {})} | custom-call | flops 8053063680 | bytes 30000000 | tf_op jit(solution)/shard_map/expert_rows/pallas_call | solution.py:633
  300.0 17.8 %expert_rows.6 = (bf16[8,1280,1536]{2,1,0:T(8,128)(2,1)}, bf16[8,1280,256]{2,1,0:T(8,128)(2,1)}, bf16[8,1280,128]{2,1,0:T(8,128)(2,1)}, bf16[4,264,1536]{2,1,0:T(8,128)(2,1)}, bf16[4,264,1536]{2,1,0:T(8,128)(2,1)}) custom-call(s32[1]{0:T(128)} %bitcast.26.turn.first, ...), custom_call_target="tpu_custom_call", output_to_operand_aliasing={{0}: (6, {}), {1}: (7, {}), {2}: (8, {})} | custom-call | flops 8053063680 | bytes 30000000 | tf_op jit(solution)/shard_map/expert_rows/pallas_call | solution.py:633
  317.8 4.0 fusion.14
  325.2 3.8 collective-permute-start.54
  330.3 9.5 %mix_rows.4 = (bf16[4,256,1536]{2,1,0:T(8,128)(2,1)}, bf16[4,256,1536]{2,1,0:T(8,128)(2,1)}) custom-call(s32[1]{0:T(128)} %bitcast.26.turn.first, f32[8,8,1024]{2,1,0:T(8,128)S(1)} %copy-done.33, bf16[8,1280,128]{2,1,0:T(8,128)(2,1)S(1)} %copy-done.1, bf16[8,128,1536]{2,1,0:T(8,128)(2,1)} %copy-done.4), custom_call_target="tpu_custom_call" | custom-call | flops 3019898880 | bytes 20000000 | tf_op jit(solution)/shard_map/mix_rows/pallas_call | solution.py:700
  339.8 3.9 fusion.18
  343.7 4.6 collective-permute-done.51
  353.1 9.3 %mix_rows.5 = (bf16[4,256,1536]{2,1,0:T(8,128)(2,1)}, bf16[4,256,1536]{2,1,0:T(8,128)(2,1)}) custom-call(s32[1]{0:T(128)} %bitcast.26.turn.first, f32[8,8,1024]{2,1,0:T(8,128)S(1)} %copy-done.26, bf16[8,1280,128]{2,1,0:T(8,128)(2,1)S(1)} %copy-done.1, bf16[8,128,1536]{2,1,0:T(8,128)(2,1)} %copy-done.4), custom_call_target="tpu_custom_call" | custom-call | flops 3019898880 | bytes 20000000 | tf_op jit(solution)/shard_map/mix_rows/pallas_call | solution.py:700
  362.4 8.7 %seed_rows.7 = (bf16[8,1280,1536]{2,1,0:T(8,128)(2,1)}, f32[8,320,128]{2,1,0:T(8,128)S(1)}, f32[8,8,1024]{2,1,0:T(8,128)S(1)}) custom-call(s32[1]{0:T(128)} %bitcast.26.turn.first, bf16[4,264,1536]{2,1,0:T(8,128)(2,1)} %copy-done.39, bf16[4,264,1536]{2,1,0:T(8,128)(2,1)} %collective-permute-done.50.sib, ...), custom_call_target="tpu_custom_call", output_to_operand_aliasing={{0}: (4, {})} | custom-call | flops 3019898880 | bytes 20000000 | tf_op jit(solution)/shard_map/seed_rows/pallas_call | solution.py:500
  371.2 4.7 fusion.26
  378.3 3.8 collective-permute-start.62
  385.2 17.9 %expert_rows.7 = (bf16[8,1280,1536]{2,1,0:T(8,128)(2,1)}, bf16[8,1280,256]{2,1,0:T(8,128)(2,1)}, bf16[8,1280,128]{2,1,0:T(8,128)(2,1)}, bf16[4,264,1536]{2,1,0:T(8,128)(2,1)}, bf16[4,264,1536]{2,1,0:T(8,128)(2,1)}) custom-call(s32[1]{0:T(128)} %bitcast.26.turn.first, ...), custom_call_target="tpu_custom_call", output_to_operand_aliasing={{0}: (6, {}), {1}: (7, {}), {2}: (8, {})} | custom-call | flops 8053063680 | bytes 30000000 | tf_op jit(solution)/shard_map/expert_rows/pallas_call | solution.py:633
  403.2 3.9 fusion.30
  412.4 9.5 %mix_rows.6 = (bf16[4,256,1536]{2,1,0:T(8,128)(2,1)}, bf16[4,256,1536]{2,1,0:T(8,128)(2,1)}) custom-call(s32[1]{0:T(128)} %bitcast.26.turn.first, f32[8,8,1024]{2,1,0:T(8,128)S(1)} %copy-done.24, bf16[8,1280,128]{2,1,0:T(8,128)(2,1)S(1)} %copy-done.2, bf16[8,128,1536]{2,1,0:T(8,128)(2,1)} %copy-done.4), custom_call_target="tpu_custom_call" | custom-call | flops 3019898880 | bytes 20000000 | tf_op jit(solution)/shard_map/mix_rows/pallas_call | solution.py:700
  423.8 6.6 collective-permute-done.66
  436.6 9.7 %mix_rows.7 = (bf16[4,256,1536]{2,1,0:T(8,128)(2,1)}, bf16[4,256,1536]{2,1,0:T(8,128)(2,1)}) custom-call(s32[1]{0:T(128)} %bitcast.26.turn.first, f32[8,8,1024]{2,1,0:T(8,128)S(1)} %copy-done.28, bf16[8,1280,128]{2,1,0:T(8,128)(2,1)S(1)} %copy-done.2, bf16[8,128,1536]{2,1,0:T(8,128)(2,1)} %copy-done.4), custom_call_target="tpu_custom_call" | custom-call | flops 3019898880 | bytes 20000000 | tf_op jit(solution)/shard_map/mix_rows/pallas_call | solution.py:700
  448.6 6.2 collective-permute-done.70
  457.0 3.6 collective-permute-start.74
  462.9 17.6 %weights_step.4 = (f32[2,8,1536,128]{3,2,1,0:T(8,128)}, f32[2,8,1536,128]{3,2,1,0:T(8,128)}, f32[2,8,1536,128]{3,2,1,0:T(8,128)}, f32[2,8,1536,128]{3,2,1,0:T(8,...) custom-call(s32[1]{0:T(128)} %bitcast.26.turn.first, ...), custom_call_target="tpu_custom_call" | custom-call | flops 3019898880 | bytes 52000000 | tf_op jit(solution)/shard_map/weights_step/pallas_call | solution.py:775
  480.5 4.1 fusion.38
  492.8 18.2 %weights_step.5 = (f32[2,8,1536,128]{3,2,1,0:T(8,128)}, f32[2,8,1536,128]{3,2,1,0:T(8,128)}, f32[2,8,1536,128]{3,2,1,0:T(8,128)}, f32[2,8,1536,128]{3,2,1,0:T(8,...) custom-call(s32[1]{0:T(128)} %get-tuple-element.1027.turn, ...), custom_call_target="tpu_custom_call", output_to_operand_aliasing={{0}: (11, {}), {1}: (12, {}), {2}: (13, {}), {3}: (14, {}),... | custom-call | flops 3019898880 | bytes 52000000 | tf_op jit(solution)/shard_map/weights_step/pallas_call | solution.py:775
  518.2 18.4 %weights_step.6 = (f32[2,8,1536,128]{3,2,1,0:T(8,128)}, f32[2,8,1536,128]{3,2,1,0:T(8,128)}, f32[2,8,1536,128]{3,2,1,0:T(8,128)}, f32[2,8,1536,128]{3,2,1,0:T(8,...) custom-call(s32[1]{0:T(128)} %get-tuple-element.1083.turn, ...), custom_call_target="tpu_custom_call", output_to_operand_aliasing={{0}: (11, {}), {1}: (12, {}), {2}: (13, {}), {3}: (14, {}),... | custom-call | flops 3019898880 | bytes 52000000 | tf_op jit(solution)/shard_map/weights_step/pallas_call | solution.py:775
  552.6 8.9 %collective-permute-done.85 = bf16[256,1536]{1,0:T(8,128)(2,1)S(1)} collective-permute-done((bf16[256,1536]{1,0:T(8,128)(2,1)S(1)}, bf16[256,1536]{1,0:T(8,128)(2,1)S(1)}, u32[]{:S(2)}, u32[]{:S(2)}) %collective-permute-start.85) | collective-permute-done | bytes 786464 | tf_op jit(solution)/shard_map/ppermute | solution.py:862
  573.6 17.6 %attend_back.1 = (bf16[1024,384]{1,0:T(8,128)(2,1)S(1)}, bf16[1024,128]{1,0:T(8,128)(2,1)S(1)}, bf16[1024,128]{1,0:T(8,128)(2,1)S(1)}) custom-call(s32[1]{0:T(128)} %copy.194.length, bf16[1024,384]{1,0:T(8,128)(2,1)S(1)} %copy-done.11, bf16[1024,128]{1,0:T(8,128)(2,1)S(1)} %copy-done.16, bf16[1024,128]{1,0:T(8,128)(2,1)S(1)} %copy-done.18, ...), custom_call_target="tpu_custom_call" | custom-call | tf_op jit(solution)/shard_map/attend_back/pallas_call | solution.py:374
  591.2 11.8 %collective-permute-done.87 = f32[1,1536]{1,0:T(1,128)S(1)} collective-permute-done((f32[1,1536]{1,0:T(1,128)S(1)}, f32[1,1536]{1,0:T(1,128)S(1)}, u32[]{:S(2)}, u32[]{:S(2)}) %collective-permute-start.87) | collective-permute-done | bytes 6176 | tf_op jit(solution)/shard_map/ppermute | solution.py:862
  616.1 3.6 collective-permute-done.93
  626.6 18.1 %weights_step.7 = (f32[2,8,1536,128]{3,2,1,0:T(8,128)}, f32[2,8,1536,128]{3,2,1,0:T(8,128)}, f32[2,8,1536,128]{3,2,1,0:T(8,128)}, f32[2,8,1536,128]{3,2,1,0:T(8,...) custom-call(s32[1]{0:T(128)} %get-tuple-element.1218.turn, ...), custom_call_target="tpu_custom_call", output_to_operand_aliasing={{0}: (11, {}), {1}: (12, {}), {2}: (13, {}), {3}: (14, {}),... | custom-call | flops 3019898880 | bytes 52000000 | tf_op jit(solution)/shard_map/weights_step/pallas_call | solution.py:775
  651.3 3.6 collective-permute-start.100
  661.3 15.8 %collective-permute-done.101 = bf16[192,640]{1,0:T(8,128)(2,1)S(1)} collective-permute-done((bf16[192,640]{1,0:T(8,128)(2,1)S(1)}, bf16[192,640]{1,0:T(8,128)(2,1)S(1)}, u32[]{:S(2)}, u32[]{:S(2)}) %collective-permute-start.101) | collective-permute-done | bytes 245792 | tf_op jit(solution)/shard_map/ppermute | solution.py:879
  692.7 10.7 %collective-permute-done.109 = f32[1,1536]{1,0:T(1,128)S(1)} collective-permute-done((f32[1,1536]{1,0:T(1,128)S(1)}, f32[1,1536]{1,0:T(1,128)S(1)}, u32[]{:S(2)}, u32[]{:S(2)}) %collective-permute-start.109) | collective-permute-done | bytes 6176 | tf_op jit(solution)/shard_map/ppermute | solution.py:862
  (562 shorter events, 235.4 us)
Async XLA Ops:
  12.4 27.0 %collective-permute-start.5 = (bf16[256,1536]{1,0:T(8,128)(2,1)S(1)}, bf16[256,1536]{1,0:T(8,128)(2,1)}, u32[]{:S(2)}, u32[]{:S(2)}) collective-permute-start(bf16[256,1536]{1,0:T(8,128)(2,1)S(1)} %copy-done.44), channel_id=1, source_target_pairs={{0,2},{1,3},{2,0},{3,1},{4,6},{5,7},{6,4},{7,5},{8,10},{9,11},{10,... | collective-permute-start | bytes 2359304 | tf_op jit(solution)/shard_map/ppermute | solution.py:862
  197.4 25.2 %collective-permute-start.31 = (bf16[4,264,1536]{2,1,0:T(8,128)(2,1)S(1)}, bf16[4,264,1536]{2,1,0:T(8,128)(2,1)S(1)}, u32[]{:S(2)}, u32[]{:S(2)}) collective-permute-start(bf16[4,264,1536]{2,1,0:T(8,128)(2,1)S(1)} %pad_maximum_fusion.1.own), channel_id=1, source_target_pairs={{0,1},{1,0},{2,3},{3,2},{4,5},{5,4},{6,7},{7,6},{8,9},{9,8},{10,11... | collective-permute-start | bytes 9732104 | tf_op jit(solution)/shard_map/ppermute | solution.py:862
  200.2 22.4 %collective-permute-start.34 = (bf16[4,256,1536]{2,1,0:T(8,128)(2,1)S(1)}, bf16[4,256,1536]{2,1,0:T(8,128)(2,1)S(1)}, u32[]{:S(2)}, u32[]{:S(2)}) collective-permute-start(bf16[4,256,1536]{2,1,0:T(8,128)(2,1)S(1)} %pad_maximum_fusion.4.own_in), channel_id=1, source_target_pairs={{0,1},{1,0},{2,3},{3,2},{4,5},{5,4},{6,7},{7,6},{8,9},{9,8},{10,11... | collective-permute-start | bytes 9437192 | tf_op jit(solution)/shard_map/ppermute | solution.py:862
  200.3 22.3 %collective-permute-start.30 = (bf16[264,1536]{1,0:T(8,128)(2,1)S(1)}, bf16[264,1536]{1,0:T(8,128)(2,1)S(1)}, u32[]{:S(2)}, u32[]{:S(2)}) collective-permute-start(bf16[264,1536]{1,0:T(8,128)(2,1)S(1)} %copy-done.81), channel_id=1, source_target_pairs={{0,4},{4,0},{8,12},{12,8},{16,20},{20,16},{24,28},{28,24},{1,5},{5... | collective-permute-start | bytes 2433032 | tf_op jit(solution)/shard_map/ppermute | solution.py:862
  200.9 21.7 %collective-permute-start.32 = (bf16[256,1536]{1,0:T(8,128)(2,1)}, bf16[256,1536]{1,0:T(8,128)(2,1)}, u32[]{:S(2)}, u32[]{:S(2)}) collective-permute-start(bf16[256,1536]{1,0:T(8,128)(2,1)} %collective-permute-done.24), channel_id=1, source_target_pairs={{0,8},{4,12},{8,16},{12,20},{16,24},{20,28},{24,0},{28,4},{1,9},{5... | collective-permute-start | bytes 2359304 | tf_op jit(solution)/shard_map/ppermute | solution.py:879
  225.3 22.5 %collective-permute-start.35 = (bf16[4,264,1536]{2,1,0:T(8,128)(2,1)S(1)}, bf16[4,264,1536]{2,1,0:T(8,128)(2,1)}, u32[]{:S(2)}, u32[]{:S(2)}) collective-permute-start(bf16[4,264,1536]{2,1,0:T(8,128)(2,1)S(1)} %pad_maximum_fusion.2.own), channel_id=1, source_target_pairs={{0,1},{1,0},{2,3},{3,2},{4,5},{5,4},{6,7},{7,6},{8,9},{9,8},{10,11... | collective-permute-start | bytes 9732104 | tf_op jit(solution)/shard_map/ppermute | solution.py:862
  225.6 22.3 %collective-permute-start.36 = (bf16[256,1536]{1,0:T(8,128)(2,1)}, bf16[256,1536]{1,0:T(8,128)(2,1)}, u32[]{:S(2)}, u32[]{:S(2)}) collective-permute-start(bf16[256,1536]{1,0:T(8,128)(2,1)} %collective-permute-done.25), channel_id=1, source_target_pairs={{0,8},{4,12},{8,16},{12,20},{16,24},{20,28},{24,0},{28,4},{1,9},{5... | collective-permute-start | bytes 2359304 | tf_op jit(solution)/shard_map/ppermute | solution.py:879
  226.0 21.8 %collective-permute-start.37 = (bf16[256,1536]{1,0:T(8,128)(2,1)}, bf16[256,1536]{1,0:T(8,128)(2,1)}, u32[]{:S(2)}, u32[]{:S(2)}) collective-permute-start(bf16[256,1536]{1,0:T(8,128)(2,1)} %collective-permute-done.32), channel_id=1, source_target_pairs={{0,2},{1,3},{2,0},{3,1},{4,6},{5,7},{6,4},{7,5},{8,10},{9,11},{10,... | collective-permute-start | bytes 2359304 | tf_op jit(solution)/shard_map/ppermute | solution.py:862
  247.9 23.8 %collective-permute-start.43 = (bf16[4,264,1536]{2,1,0:T(8,128)(2,1)}, bf16[4,264,1536]{2,1,0:T(8,128)(2,1)S(1)}, u32[]{:S(2)}, u32[]{:S(2)}) collective-permute-start(bf16[4,264,1536]{2,1,0:T(8,128)(2,1)} %get-tuple-element.811), channel_id=1, source_target_pairs={{0,1},{1,0},{2,3},{3,2},{4,5},{5,4},{6,7},{7,6},{8,9},{9,8},{10,11... | collective-permute-start | bytes 9732104 | tf_op jit(solution)/shard_map/ppermute | solution.py:862
  250.0 24.0 %collective-permute-start.42 = (bf16[4,256,1536]{2,1,0:T(8,128)(2,1)S(1)}, bf16[4,256,1536]{2,1,0:T(8,128)(2,1)}, u32[]{:S(2)}, u32[]{:S(2)}) collective-permute-start(bf16[4,256,1536]{2,1,0:T(8,128)(2,1)S(1)} %pad_maximum_fusion.5.own_in), channel_id=1, source_target_pairs={{0,1},{1,0},{2,3},{3,2},{4,5},{5,4},{6,7},{7,6},{8,9},{9,8},{10,11... | collective-permute-start | bytes 9437192 | tf_op jit(solution)/shard_map/ppermute | solution.py:862
  250.6 23.5 %collective-permute-start.39 = (bf16[264,1536]{1,0:T(8,128)(2,1)}, bf16[264,1536]{1,0:T(8,128)(2,1)S(1)}, u32[]{:S(2)}, u32[]{:S(2)}) collective-permute-start(bf16[264,1536]{1,0:T(8,128)(2,1)} %collective-permute-done.15), channel_id=1, source_target_pairs={{0,2},{1,3},{2,0},{3,1},{4,6},{5,7},{6,4},{7,5},{8,10},{9,11},{10,... | collective-permute-start | bytes 2433032 | tf_op jit(solution)/shard_map/ppermute | solution.py:862
  252.1 21.9 %collective-permute-start.40 = (bf16[256,1536]{1,0:T(8,128)(2,1)}, bf16[256,1536]{1,0:T(8,128)(2,1)}, u32[]{:S(2)}, u32[]{:S(2)}) collective-permute-start(bf16[256,1536]{1,0:T(8,128)(2,1)} %collective-permute-done.32), channel_id=1, source_target_pairs={{0,8},{4,12},{8,16},{12,20},{16,24},{20,28},{24,0},{28,4},{1,9},{5... | collective-permute-start | bytes 2359304 | tf_op jit(solution)/shard_map/ppermute | solution.py:879
  252.1 21.9 %collective-permute-start.41 = (bf16[256,1536]{1,0:T(8,128)(2,1)}, bf16[256,1536]{1,0:T(8,128)(2,1)S(1)}, u32[]{:S(2)}, u32[]{:S(2)}) collective-permute-start(bf16[256,1536]{1,0:T(8,128)(2,1)} %collective-permute-done.37), channel_id=1, source_target_pairs={{0,4},{4,0},{8,12},{12,8},{16,20},{20,16},{24,28},{28,24},{1,5},{5... | collective-permute-start | bytes 2359304 | tf_op jit(solution)/shard_map/ppermute | solution.py:862
  297.9 23.9 %collective-permute-start.47 = (bf16[264,1536]{1,0:T(8,128)(2,1)}, bf16[264,1536]{1,0:T(8,128)(2,1)}, u32[]{:S(2)}, u32[]{:S(2)}) collective-permute-start(bf16[264,1536]{1,0:T(8,128)(2,1)} %collective-permute-done.44), channel_id=1, source_target_pairs={{0,2},{1,3},{2,0},{3,1},{4,6},{5,7},{6,4},{7,5},{8,10},{9,11},{10,... | collective-permute-start | bytes 2433032 | tf_op jit(solution)/shard_map/ppermute | solution.py:862
  298.7 23.1 %collective-permute-start.48 = (bf16[256,1536]{1,0:T(8,128)(2,1)}, bf16[256,1536]{1,0:T(8,128)(2,1)}, u32[]{:S(2)}, u32[]{:S(2)}) collective-permute-start(bf16[256,1536]{1,0:T(8,128)(2,1)} %collective-permute-done.40), channel_id=1, source_target_pairs={{0,4},{4,0},{8,12},{12,8},{16,20},{20,16},{24,28},{28,24},{1,5},{5... | collective-permute-start | bytes 2359304 | tf_op jit(solution)/shard_map/ppermute | solution.py:862
  323.9 24.4 %collective-permute-start.50 = (bf16[4,264,1536]{2,1,0:T(8,128)(2,1)S(1)}, bf16[4,264,1536]{2,1,0:T(8,128)(2,1)}, u32[]{:S(2)}, u32[]{:S(2)}) collective-permute-start(bf16[4,264,1536]{2,1,0:T(8,128)(2,1)S(1)} %pad_maximum_fusion.3.own), channel_id=1, source_target_pairs={{0,1},{1,0},{2,3},{3,2},{4,5},{5,4},{6,7},{7,6},{8,9},{9,8},{10,11... | collective-permute-start | bytes 9732104 | tf_op jit(solution)/shard_map/ppermute | solution.py:862
  324.4 23.8 %collective-permute-start.53 = (bf16[264,1536]{1,0:T(8,128)(2,1)S(1)}, bf16[264,1536]{1,0:T(8,128)(2,1)}, u32[]{:S(2)}, u32[]{:S(2)}) collective-permute-start(bf16[264,1536]{1,0:T(8,128)(2,1)S(1)} %copy-done.84), channel_id=1, source_target_pairs={{0,4},{4,0},{8,12},{12,8},{16,20},{20,16},{24,28},{28,24},{1,5},{5... | collective-permute-start | bytes 2433032 | tf_op jit(solution)/shard_map/ppermute | solution.py:862
  325.2 23.1 %collective-permute-start.54 = (bf16[264,1536]{1,0:T(8,128)(2,1)S(1)}, bf16[264,1536]{1,0:T(8,128)(2,1)}, u32[]{:S(2)}, u32[]{:S(2)}) collective-permute-start(bf16[264,1536]{1,0:T(8,128)(2,1)S(1)} %get-tuple-element.878), channel_id=1, source_target_pairs={{0,24},{4,28},{8,0},{12,4},{16,8},{20,12},{24,16},{28,20},{1,25},{... | collective-permute-start | bytes 2433032 | tf_op jit(solution)/shard_map/ppermute | solution.py:879
  348.3 22.9 %collective-permute-start.59 = (bf16[4,256,1536]{2,1,0:T(8,128)(2,1)}, bf16[4,256,1536]{2,1,0:T(8,128)(2,1)}, u32[]{:S(2)}, u32[]{:S(2)}) collective-permute-start(bf16[4,256,1536]{2,1,0:T(8,128)(2,1)} %get-tuple-element.914), channel_id=1, source_target_pairs={{0,1},{1,0},{2,3},{3,2},{4,5},{5,4},{6,7},{7,6},{8,9},{9,8},{10,11... | collective-permute-start | bytes 9437192 | tf_op jit(solution)/shard_map/ppermute | solution.py:862
  350.5 25.4 %collective-permute-start.55 = (bf16[4,256,1536]{2,1,0:T(8,128)(2,1)S(1)}, bf16[4,256,1536]{2,1,0:T(8,128)(2,1)}, u32[]{:S(2)}, u32[]{:S(2)}) collective-permute-start(bf16[4,256,1536]{2,1,0:T(8,128)(2,1)S(1)} %pad_maximum_fusion.7.own_in), channel_id=1, source_target_pairs={{0,1},{1,0},{2,3},{3,2},{4,5},{5,4},{6,7},{7,6},{8,9},{9,8},{10,11... | collective-permute-start | bytes 9437192 | tf_op jit(solution)/shard_map/ppermute | solution.py:862
  351.0 24.9 %collective-permute-start.56 = (bf16[264,1536]{1,0:T(8,128)(2,1)}, bf16[264,1536]{1,0:T(8,128)(2,1)}, u32[]{:S(2)}, u32[]{:S(2)}) collective-permute-start(bf16[264,1536]{1,0:T(8,128)(2,1)} %get-tuple-element.904), channel_id=1, source_target_pairs={{0,2},{1,3},{2,0},{3,1},{4,6},{5,7},{6,4},{7,5},{8,10},{9,11},{10,... | collective-permute-start | bytes 2433032 | tf_op jit(solution)/shard_map/ppermute | solution.py:862
  352.3 23.6 %collective-permute-start.57 = (bf16[264,1536]{1,0:T(8,128)(2,1)}, bf16[264,1536]{1,0:T(8,128)(2,1)S(1)}, u32[]{:S(2)}, u32[]{:S(2)}) collective-permute-start(bf16[264,1536]{1,0:T(8,128)(2,1)} %get-tuple-element.908), channel_id=1, source_target_pairs={{0,4},{4,0},{8,12},{12,8},{16,20},{20,16},{24,28},{28,24},{1,5},{5... | collective-permute-start | bytes 2433032 | tf_op jit(solution)/shard_map/ppermute | solution.py:862
  353.1 22.8 %collective-permute-start.58 = (bf16[264,1536]{1,0:T(8,128)(2,1)}, bf16[264,1536]{1,0:T(8,128)(2,1)}, u32[]{:S(2)}, u32[]{:S(2)}) collective-permute-start(bf16[264,1536]{1,0:T(8,128)(2,1)} %get-tuple-element.902), channel_id=1, source_target_pairs={{0,8},{4,12},{8,16},{12,20},{16,24},{20,28},{24,0},{28,4},{1,9},{5... | collective-permute-start | bytes 2433032 | tf_op jit(solution)/shard_map/ppermute | solution.py:879
  375.9 27.3 %collective-permute-start.63 = (bf16[4,256,1536]{2,1,0:T(8,128)(2,1)}, bf16[4,256,1536]{2,1,0:T(8,128)(2,1)}, u32[]{:S(2)}, u32[]{:S(2)}) collective-permute-start(bf16[4,256,1536]{2,1,0:T(8,128)(2,1)} %get-tuple-element.943), channel_id=1, source_target_pairs={{0,1},{1,0},{2,3},{3,2},{4,5},{5,4},{6,7},{7,6},{8,9},{9,8},{10,11... | collective-permute-start | bytes 9437192 | tf_op jit(solution)/shard_map/ppermute | solution.py:862
  378.3 28.8 %collective-permute-start.62 = (bf16[264,1536]{1,0:T(8,128)(2,1)}, bf16[264,1536]{1,0:T(8,128)(2,1)}, u32[]{:S(2)}, u32[]{:S(2)}) collective-permute-start(bf16[264,1536]{1,0:T(8,128)(2,1)} %add_convert_fusion.10), channel_id=1, source_target_pairs={{0,24},{4,28},{8,0},{12,4},{16,8},{20,12},{24,16},{28,20},{1,25},{... | collective-permute-start | bytes 2433032 | tf_op jit(solution)/shard_map/ppermute | solution.py:879
  383.2 23.9 %collective-permute-start.60 = (bf16[264,1536]{1,0:T(8,128)(2,1)}, bf16[264,1536]{1,0:T(8,128)(2,1)}, u32[]{:S(2)}, u32[]{:S(2)}) collective-permute-start(bf16[264,1536]{1,0:T(8,128)(2,1)} %add_convert_fusion.11), channel_id=1, source_target_pairs={{0,2},{1,3},{2,0},{3,1},{4,6},{5,7},{6,4},{7,5},{8,10},{9,11},{10,... | collective-permute-start | bytes 2433032 | tf_op jit(solution)/shard_map/ppermute | solution.py:862
  384.5 22.6 %collective-permute-start.61 = (bf16[264,1536]{1,0:T(8,128)(2,1)}, bf16[264,1536]{1,0:T(8,128)(2,1)}, u32[]{:S(2)}, u32[]{:S(2)}) collective-permute-start(bf16[264,1536]{1,0:T(8,128)(2,1)} %get-tuple-element.932), channel_id=1, source_target_pairs={{0,4},{4,0},{8,12},{12,8},{16,20},{20,16},{24,28},{28,24},{1,5},{5... | collective-permute-start | bytes 2433032 | tf_op jit(solution)/shard_map/ppermute | solution.py:862
  410.3 22.3 %collective-permute-start.65 = (bf16[264,1536]{1,0:T(8,128)(2,1)}, bf16[264,1536]{1,0:T(8,128)(2,1)S(1)}, u32[]{:S(2)}, u32[]{:S(2)}) collective-permute-start(bf16[264,1536]{1,0:T(8,128)(2,1)} %add_convert_fusion.5), channel_id=1, source_target_pairs={{0,8},{4,12},{8,16},{12,20},{16,24},{20,28},{24,0},{28,4},{1,9},{5... | collective-permute-start | bytes 2433032 | tf_op jit(solution)/shard_map/ppermute | solution.py:879
  454.8 25.7 %collective-permute-start.73 = (bf16[4,256,1536]{2,1,0:T(8,128)(2,1)}, bf16[4,256,1536]{2,1,0:T(8,128)(2,1)}, u32[]{:S(2)}, u32[]{:S(2)}) collective-permute-start(bf16[4,256,1536]{2,1,0:T(8,128)(2,1)} %get-tuple-element.1023), channel_id=1, source_target_pairs={{0,1},{1,0},{2,3},{3,2},{4,5},{5,4},{6,7},{7,6},{8,9},{9,8},{10,11... | collective-permute-start | bytes 9437192 | tf_op jit(solution)/shard_map/ppermute | solution.py:862
  457.0 27.6 %collective-permute-start.74 = (bf16[256,1536]{1,0:T(8,128)(2,1)}, bf16[256,1536]{1,0:T(8,128)(2,1)}, u32[]{:S(2)}, u32[]{:S(2)}) collective-permute-start(bf16[256,1536]{1,0:T(8,128)(2,1)} %add_convert_fusion.33), channel_id=1, source_target_pairs={{0,24},{4,28},{8,0},{12,4},{16,8},{20,12},{24,16},{28,20},{1,25},{... | collective-permute-start | bytes 2359304 | tf_op jit(solution)/shard_map/ppermute | solution.py:879
  460.8 23.8 %collective-permute-start.72 = (bf16[264,1536]{1,0:T(8,128)(2,1)S(1)}, bf16[264,1536]{1,0:T(8,128)(2,1)}, u32[]{:S(2)}, u32[]{:S(2)}) collective-permute-start(bf16[264,1536]{1,0:T(8,128)(2,1)S(1)} %add_convert_fusion.4), channel_id=1, source_target_pairs={{0,4},{4,0},{8,12},{12,8},{16,20},{20,16},{24,28},{28,24},{1,5},{5... | collective-permute-start | bytes 2433032 | tf_op jit(solution)/shard_map/ppermute | solution.py:862
  462.2 22.5 %collective-permute-start.71 = (bf16[264,1536]{1,0:T(8,128)(2,1)}, bf16[264,1536]{1,0:T(8,128)(2,1)}, u32[]{:S(2)}, u32[]{:S(2)}) collective-permute-start(bf16[264,1536]{1,0:T(8,128)(2,1)} %get-tuple-element.1006), channel_id=1, source_target_pairs={{0,2},{1,3},{2,0},{3,1},{4,6},{5,7},{6,4},{7,5},{8,10},{9,11},{10,... | collective-permute-start | bytes 2433032 | tf_op jit(solution)/shard_map/ppermute | solution.py:862
  487.4 23.6 %collective-permute-start.77 = (bf16[264,1536]{1,0:T(8,128)(2,1)}, bf16[264,1536]{1,0:T(8,128)(2,1)S(1)}, u32[]{:S(2)}, u32[]{:S(2)}) collective-permute-start(bf16[264,1536]{1,0:T(8,128)(2,1)} %add_convert_fusion.1), channel_id=1, source_target_pairs={{0,8},{4,12},{8,16},{12,20},{16,24},{20,28},{24,0},{28,4},{1,9},{5... | collective-permute-start | bytes 2433032 | tf_op jit(solution)/shard_map/ppermute | solution.py:879
  488.9 22.1 %collective-permute-start.76 = (bf16[264,1536]{1,0:T(8,128)(2,1)S(1)}, bf16[264,1536]{1,0:T(8,128)(2,1)S(1)}, u32[]{:S(2)}, u32[]{:S(2)}) collective-permute-start(bf16[264,1536]{1,0:T(8,128)(2,1)S(1)} %add_convert_fusion.2), channel_id=1, source_target_pairs={{0,4},{4,0},{8,12},{12,8},{16,20},{20,16},{24,28},{28,24},{1,5},{5... | collective-permute-start | bytes 2433032 | tf_op jit(solution)/shard_map/ppermute | solution.py:862
  518.2 21.8 %collective-permute-start.81 = (bf16[256,1536]{1,0:T(8,128)(2,1)}, bf16[256,1536]{1,0:T(8,128)(2,1)}, u32[]{:S(2)}, u32[]{:S(2)}) collective-permute-start(bf16[256,1536]{1,0:T(8,128)(2,1)} %get-tuple-element.1096), channel_id=1, source_target_pairs={{0,8},{4,12},{8,16},{12,20},{16,24},{20,28},{24,0},{28,4},{1,9},{5... | collective-permute-start | bytes 2359304 | tf_op jit(solution)/shard_map/ppermute | solution.py:879
  566.8 36.2 %collective-permute-start.89 = (bf16[256,1536]{1,0:T(8,128)(2,1)}, bf16[256,1536]{1,0:T(8,128)(2,1)}, u32[]{:S(2)}, u32[]{:S(2)}) collective-permute-start(bf16[256,1536]{1,0:T(8,128)(2,1)} %add_convert_fusion.30), channel_id=1, source_target_pairs={{0,2},{1,3},{2,0},{3,1},{4,6},{5,7},{6,4},{7,5},{8,10},{9,11},{10,... | collective-permute-start | bytes 2359304 | tf_op jit(solution)/shard_map/ppermute | solution.py:862
  567.7 35.3 %collective-permute-start.88 = (bf16[256,1536]{1,0:T(8,128)(2,1)}, bf16[256,1536]{1,0:T(8,128)(2,1)}, u32[]{:S(2)}, u32[]{:S(2)}) collective-permute-start(bf16[256,1536]{1,0:T(8,128)(2,1)} %get-tuple-element.1143), channel_id=1, source_target_pairs={{0,2},{1,3},{2,0},{3,1},{4,6},{5,7},{6,4},{7,5},{8,10},{9,11},{10,... | collective-permute-start | bytes 2359304 | tf_op jit(solution)/shard_map/ppermute | solution.py:862
  568.9 34.2 %collective-permute-start.90 = (bf16[256,1536]{1,0:T(8,128)(2,1)}, bf16[256,1536]{1,0:T(8,128)(2,1)}, u32[]{:S(2)}, u32[]{:S(2)}) collective-permute-start(bf16[256,1536]{1,0:T(8,128)(2,1)} %get-tuple-element.1139), channel_id=1, source_target_pairs={{0,4},{4,0},{8,12},{12,8},{16,20},{20,16},{24,28},{28,24},{1,5},{5... | collective-permute-start | bytes 2359304 | tf_op jit(solution)/shard_map/ppermute | solution.py:862
  569.8 33.2 %collective-permute-start.86 = (bf16[4,192,384]{2,1,0:T(8,128)(2,1)}, bf16[4,192,384]{2,1,0:T(8,128)(2,1)}, u32[]{:S(2)}, u32[]{:S(2)}) collective-permute-start(bf16[4,192,384]{2,1,0:T(8,128)(2,1)} %pad_maximum_fusion.12), channel_id=1, source_target_pairs={{0,4},{4,0},{8,12},{12,8},{16,20},{20,16},{24,28},{28,24},{1,5},{5... | collective-permute-start | bytes 1769480 | tf_op jit(solution)/shard_map/ppermute | solution.py:862
  571.5 31.5 %collective-permute-start.87 = (f32[1,1536]{1,0:T(1,128)S(1)}, f32[1,1536]{1,0:T(1,128)S(1)}, u32[]{:S(2)}, u32[]{:S(2)}) collective-permute-start(f32[1,1536]{1,0:T(1,128)S(1)} %add.673), channel_id=1, source_target_pairs={{0,2},{1,3},{2,0},{3,1},{4,6},{5,7},{6,4},{7,5},{8,10},{9,11},{10,... | collective-permute-start | bytes 18440 | tf_op jit(solution)/shard_map/ppermute | solution.py:862
  622.7 24.4 %collective-permute-start.99 = (bf16[256,1536]{1,0:T(8,128)(2,1)}, bf16[256,1536]{1,0:T(8,128)(2,1)}, u32[]{:S(2)}, u32[]{:S(2)}) collective-permute-start(bf16[256,1536]{1,0:T(8,128)(2,1)} %add_convert_fusion.28), channel_id=1, source_target_pairs={{0,8},{4,12},{8,16},{12,20},{16,24},{20,28},{24,0},{28,4},{1,9},{5... | collective-permute-start | bytes 2359304 | tf_op jit(solution)/shard_map/ppermute | solution.py:879
  623.0 24.1 %collective-permute-start.98 = (bf16[4,192,640]{2,1,0:T(8,128)(2,1)S(1)}, bf16[4,192,640]{2,1,0:T(8,128)(2,1)}, u32[]{:S(2)}, u32[]{:S(2)}) collective-permute-start(bf16[4,192,640]{2,1,0:T(8,128)(2,1)S(1)} %pad_maximum_fusion.9), channel_id=1, source_target_pairs={{0,4},{4,0},{8,12},{12,8},{16,20},{20,16},{24,28},{28,24},{1,5},{5... | collective-permute-start | bytes 2949128 | tf_op jit(solution)/shard_map/ppermute | solution.py:862
  624.4 22.7 %collective-permute-start.96 = (bf16[256,1536]{1,0:T(8,128)(2,1)S(1)}, bf16[256,1536]{1,0:T(8,128)(2,1)S(1)}, u32[]{:S(2)}, u32[]{:S(2)}) collective-permute-start(bf16[256,1536]{1,0:T(8,128)(2,1)S(1)} %add_convert_fusion.29), channel_id=1, source_target_pairs={{0,2},{1,3},{2,0},{3,1},{4,6},{5,7},{6,4},{7,5},{8,10},{9,11},{10,... | collective-permute-start | bytes 2359304 | tf_op jit(solution)/shard_map/ppermute | solution.py:862
  625.2 21.8 %collective-permute-start.97 = (bf16[256,1536]{1,0:T(8,128)(2,1)S(1)}, bf16[256,1536]{1,0:T(8,128)(2,1)S(1)}, u32[]{:S(2)}, u32[]{:S(2)}) collective-permute-start(bf16[256,1536]{1,0:T(8,128)(2,1)S(1)} %get-tuple-element.1173), channel_id=1, source_target_pairs={{0,1},{1,0},{2,3},{3,2},{4,5},{5,4},{6,7},{7,6},{8,9},{9,8},{10,11... | collective-permute-start | bytes 2359304 | tf_op jit(solution)/shard_map/ppermute | solution.py:862
  648.4 28.7 %collective-permute-start.104 = (bf16[256,1536]{1,0:T(8,128)(2,1)S(1)}, bf16[256,1536]{1,0:T(8,128)(2,1)S(1)}, u32[]{:S(2)}, u32[]{:S(2)}) collective-permute-start(bf16[256,1536]{1,0:T(8,128)(2,1)S(1)} %add_convert_fusion.27), channel_id=1, source_target_pairs={{0,4},{4,0},{8,12},{12,8},{16,20},{20,16},{24,28},{28,24},{1,5},{5... | collective-permute-start | bytes 2359304 | tf_op jit(solution)/shard_map/ppermute | solution.py:862
  654.9 22.2 %collective-permute-start.101 = (bf16[192,640]{1,0:T(8,128)(2,1)S(1)}, bf16[192,640]{1,0:T(8,128)(2,1)S(1)}, u32[]{:S(2)}, u32[]{:S(2)}) collective-permute-start(bf16[192,640]{1,0:T(8,128)(2,1)S(1)} %get-tuple-element.1368), channel_id=1, source_target_pairs={{0,16},{4,20},{8,24},{12,28},{16,0},{20,4},{24,8},{28,12},{1,17},{... | collective-permute-start | bytes 737288 | tf_op jit(solution)/shard_map/ppermute | solution.py:879
  655.4 21.7 %collective-permute-start.102 = (bf16[192,640]{1,0:T(8,128)(2,1)S(1)}, bf16[192,640]{1,0:T(8,128)(2,1)S(1)}, u32[]{:S(2)}, u32[]{:S(2)}) collective-permute-start(bf16[192,640]{1,0:T(8,128)(2,1)S(1)} %get-tuple-element.1367), channel_id=1, source_target_pairs={{0,8},{4,12},{8,16},{12,20},{16,24},{20,28},{24,0},{28,4},{1,9},{5... | collective-permute-start | bytes 737288 | tf_op jit(solution)/shard_map/ppermute | solution.py:879
  681.3 23.5 %collective-permute-start.105 = (bf16[256,1536]{1,0:T(8,128)(2,1)}, bf16[256,1536]{1,0:T(8,128)(2,1)}, u32[]{:S(2)}, u32[]{:S(2)}) collective-permute-start(bf16[256,1536]{1,0:T(8,128)(2,1)} %add_convert_fusion.26), channel_id=1, source_target_pairs={{0,8},{4,12},{8,16},{12,20},{16,24},{20,28},{24,0},{28,4},{1,9},{5... | collective-permute-start | bytes 2359304 | tf_op jit(solution)/shard_map/ppermute | solution.py:879
  (190 other events, 2306.4 us)

commit v2 on v1

--- a/solution.py
+++ b/solution.py
@@ -439,6 +439,11 @@
     ]
 
 
+def wait_pair(i, own, buf, sem):
+    for n in (2 * i, 2 * i + 1):
+        pltpu.make_async_copy(own.at[0, pl.ds(0, BLOCK), :], buf.at[n], sem.at[n]).wait()
+
+
 def gather_pair(i, buf, hots, out, local, cap):
     width = buf.shape[2]
     cut = width // 3
@@ -456,14 +461,15 @@
     s_out, u_out, tab, buf, s_scr, d_scr, t_scr, sem, t_sem = refs[1 if fresh else 2 :]
     local = d_scr.shape[0]
     copies = load_plane(own, sib, buf, sem)
+    tables = []
     for n in range(NB):
         ref = (own if n < 4 else sib).at[n % 4, pl.ds(BLOCK, TOP), :]
-        copies.append(pltpu.make_async_copy(ref, t_scr.at[n], t_sem.at[n]))
+        tables.append(pltpu.make_async_copy(ref, t_scr.at[n], t_sem.at[n]))
     weights = pltpu.make_async_copy(down, d_scr, sem.at[NB + 2])
-    for c in copies:
+    for c in tables + copies:
         c.start()
     weights.start()
-    for c in copies:
+    for c in tables:
         c.wait()
     for n in range(NB):
         tab[n] = t_scr[n, :, : 4 * BLOCK].astype(F32)
@@ -473,6 +479,7 @@
         for j in range(2):
             slot, _g = local_slots(tab[2 * i + j], first[0], local)
             hots.append(one_hot(slot, cap).astype(BF))
+        wait_pair(i, own, buf, sem)
         gather_pair(i, buf, hots, s_scr, local, cap)
         return 0
 
@@ -534,8 +541,6 @@
     for c in copies:
         c.start()
     weights.start()
-    for c in copies:
-        c.wait()
 
     def gather(i, _):
         hots = []
@@ -552,6 +557,7 @@
                 g_scr[e, pl.ds(b * cap, cap), :] = weight[e * cap : (e + 1) * cap, :]
             hots.append(hot.astype(BF))
             p_scr[b] = hots[-1]
+        wait_pair(i, own_in, buf, sem)
         gather_pair(i, buf, hots, x_scr, local, cap)
         return 0
 
@@ -662,13 +668,22 @@
     )(first, tab, u, own, sib, wgu, *more)
 
 
-def mix_body(cap, plane, first, tab, a, down, own, sib, y_scr, m_scr, a_scr, sem, out_sem):
+def mix_body(cap, plane, first, tab, a, down_in, own, sib, y_scr, a_scr, down, sem):
     local = down.shape[0]
     slots = local * cap
     rows = NB * cap
-    load = pltpu.make_async_copy(a.at[:, pl.ds(plane * rows, rows), :], a_scr, sem)
+    load = pltpu.make_async_copy(a.at[:, pl.ds(plane * rows, rows), :], a_scr, sem.at[0])
+    half = local // 2
+    cuts = [pl.ds(0, half), pl.ds(half, local - half)] if half else [pl.ds(0, local)]
+    weights = [
+        pltpu.make_async_copy(down_in.at[c], down.at[c], sem.at[1 + i]) for i, c in enumerate(cuts)
+    ]
     load.start()
+    for w in weights:
+        w.start()
     load.wait()
+    for w in weights:
+        w.wait()
 
     def expert(e, _):
         y_scr[e] = mm(a_scr[e], down[e])
@@ -682,15 +697,10 @@
             slot, _g = local_slots(tab[b], first[0], local)
             hot = one_hot(slot, cap).astype(BF)
             yb = y_scr[:, pl.ds(b * cap, cap), :].reshape(slots, -1).astype(BF)
-            m_scr[b] = mm(hot, yb, TN).astype(BF)
-            pltpu.make_async_copy(m_scr.at[b], out.at[i], out_sem.at[b]).start()
+            out[i] = mm(hot, yb, TN).astype(BF)
             return 0
 
         lax.fori_loop(0, 4, combine, 0, unroll=2)
-    for half, out in ((1, sib), (0, own)):
-        for i in range(4):
-            b = 4 * half + i
-            pltpu.make_async_copy(m_scr.at[b], out.at[i], out_sem.at[b]).wait()
 
 
 def mix_rows(plane, first, tab, a, down, cap):
@@ -699,17 +709,16 @@
     vm = pl.BlockSpec(memory_space=pltpu.VMEM)
     return pl.pallas_call(
         functools.partial(mix_body, cap, plane),
-        in_specs=[pl.BlockSpec(memory_space=pltpu.SMEM), vm, ANY, vm],
-        out_specs=[ANY, ANY],
+        in_specs=[pl.BlockSpec(memory_space=pltpu.SMEM), vm, ANY, ANY],
+        out_specs=[vm, vm],
         out_shape=[jax.ShapeDtypeStruct((4, BLOCK, width), BF)] * 2,
         scratch_shapes=[
             pltpu.VMEM((local, rows, width), F32),
-            pltpu.VMEM((NB, BLOCK, width), BF),
             pltpu.VMEM((local, rows, hidden), BF),
-            pltpu.SemaphoreType.DMA(()),
-            pltpu.SemaphoreType.DMA((NB,)),
+            pltpu.VMEM((local, hidden, width), BF),
+            pltpu.SemaphoreType.DMA((3,)),
         ],
-        compiler_params=params(50),
+        compiler_params=params(34),
         cost_estimate=cost(2 * rows * local * (BLOCK + hidden) * width, 2e7),
         name="mix_rows",
     )(first, tab, a, down)
@@ -1082,7 +1091,7 @@
             r, count, first, c.own.pop(r), c.sib.pop(r), down_low, kept_s, capacity
         )
 
-    c.y_(2)
+    c.d_(2), c.y_on(2)
     wgu, down_low = round_weights(first, up[0], down[0])
     sent, near0, near1, wgu, down_low, st = meet(sent, near0, near1, wgu, down_low, c.state())
     c.put(st)
@@ -1124,110 +1133,106 @@
     step()
     c.d_(1), m.d_(0), m.y_on(1)
     step()
-    m.d_(1), c.d_(2), m.on(2), c.cores(1), m.cores(0)
+    m.d_(1), c.y_(3), m.on(2), c.cores(1), m.cores(0)
     step()
     m.x_(2), m.y_(2), m.x_on(1), c.cores(2)
     expert(0)
     step()
-    c.x_(3), m.d_(2), m.on(3), m.cores(1), back.cores(0)
+    c.d_(3), m.d_(2), m.on(3), m.cores(1)
     seed(1)
     seed(2)
     step()
-    m.x_(3), c.y_(3), m.cores(2)
+    m.x_(3), m.y_(3), c.x_on(3), m.cores(2), back.cores(0)
     expert(1)
     step()
-    c.d_(3), m.y_(3), back.cores(1)
+    m.d_(3), back.d_(0), back.cores(1), c.cores(3)
     expert(2)
     step()
-    m.d_(3), back.d_(0), back.x_in(1), c.cores(3), back.cores(2)
+    back.d_(1), back.x_in(1), back.cores(2), m.cores(3)
+    seed(3)
     mixes(0)
     step()
-    back.d_(1), back.d_(2), back.on(1, count), m.cores(3), mix.cores(0)
-    seed(3)
+    back.d_(2), back.on(1, count), mix.cores(0)
+    expert(3)
+    step()
+    back.x_(2), back.y_(2), back.y_in(1), back.cores(3)
     mixes(1)
     step()
-    back.x_(2), back.y_(2), back.y_in(1), mix.cores(1)
-    expert(3)
-    step()
-    mix.d_(1), mix.d_(0), back.on(2, count), back.cores(3)
+    back.d_(3), mix.d_(0), back.on(2, count), mix.cores(1)
     mixes(2)
     step()
-    back.d_(3), mix.x_in(1), mix.cores(2)
+    back.x_(3), back.y_(3), mix.x_in(1), mix.cores(2)
     mixes(3)
     step()
-    back.x_(3), back.y_(3), mix.y_in(1), mix.cores(3)
+    back.x_(0), back.y_(0), back.on(3, count), mix.cores(3)
     weights(0, 2)
-    step()
-    back.x_(0), back.y_(0), back.on(3, count)
-    weights(2, 2)
     step()
     whole = back.plane(0)
     gate_grad, moe_grad = whole[BLOCK:, :BLOCK].T, whole[:BLOCK]
 
     seed_grad = cotangent.astype(F32) * live_rows[:, None].astype(F32)
-    gain_sum = jnp.sum(moe_grad * normed_moe, axis=0, keepdims=True)
+    gain_part = jnp.sum(moe_grad * normed_moe, axis=0)
     middle_grad = seed_grad + norm_back(moe_grad, gain_moe, rms_moe, normed_moe)
     mid, turn, st = meet(middle_grad.astype(BF), turn, mix.state())
     mix.put(st)
     mx, mc = across(mid), core(mid)
     mix.d_(2), mix.on(1, count)
-    weights(4, 2)
-    mx, mc, turn, st, gain_sum = meet(mx, mc, turn, mix.state(), gain_sum)
+    weights(2, 2)
+    mx, mc, turn, st, gain_part = meet(mx, mc, turn, mix.state(), gain_part)
     mix.put(st)
     mxc = core(mx)
-    mix.x_(0), mix.y_(0)
-    gain_sum = gain_sum + flip(gain_sum, "tensor", 1)
+    mix.d_(1)
     heads_grad, middle_low = heads_back(at, [mid, mc, mx, mxc], packed, out_cols)
-    omine, oother = data_parts(mm(middle_low, heads, TN).astype(BF))
-    heads_grad, omine, oother, gain_sum, st = meet(
-        heads_grad, omine, oother, gain_sum, mix.state()
-    )
+    outproj_part = mm(middle_low, heads, TN).astype(BF)
+    heads_grad, outproj_part, st = meet(heads_grad, outproj_part, mix.state())
     mix.put(st)
     dq, dk, dv = attend_back(lengths, q, k, v, heads, heads_grad, lse, cos, sin, share)
+    omine, oother = data_parts(outproj_part)
     ocame = side(oother)
-    mix.d_(3), mix.x_(2), mix.y_(2)
-    gain_sum = gain_sum + flip(gain_sum, "tensor", 2)
-    dq, dk, dv, ocame, omine, gain_sum, st = meet(dq, dk, dv, ocame, omine, gain_sum, mix.state())
+    mix.d_(3), mix.x_(2), mix.y_(2), mix.y_in(1)
+    dq, dk, dv, ocame, omine, st = meet(dq, dk, dv, ocame, omine, mix.state())
     mix.put(st)
+    osums = plus(omine, ocame)
+    ohere = [osums[0]] + [onward(osums[r], -r) for r in range(1, count)]
     dqkv = jnp.concatenate([dq, dk, dv], axis=1)
     near0, near1, far0, far1 = project(at, dqkv, packed, in_cols)
     far1 = core(far1)
-    osums = plus(omine, ocame)
-    ohere = [osums[0]] + [onward(osums[r], -r) for r in range(1, count)]
-    qmine, qother = data_parts(mm(attn_in, dqkv, TN).astype(BF))
-    gain_sum = gain_sum + flip(gain_sum, "dp", 1)
-    near0, near1, far0, far1, ohere, qmine, qother, gain_sum, st = meet(
-        near0, near1, far0, far1, ohere, qmine, qother, gain_sum, mix.state()
+    qkv_part = mm(attn_in, dqkv, TN)
+    gain_attn_part = jnp.sum(packed[:, :wide].astype(F32) * qkv_part, axis=1) / gain_attn[0]
+    gain_rows = jnp.stack([gain_attn_part, gain_part]).reshape(2, 2 * count, -1)
+    gain_rows = jnp.pad(gain_rows.transpose(1, 0, 2), ((0, 0), (0, 6), (0, wide - gain_rows.shape[2])))
+    qkv_part = qkv_part.astype(BF).reshape(2 * count, -1, wide)
+    qkv_part = jnp.concatenate([qkv_part, gain_rows.astype(BF)], axis=1)
+    qmine, qother = data_parts(qkv_part.reshape(-1, wide))
+    near0, near1, far0, far1, qmine, qother, ohere, st = meet(
+        near0, near1, far0, far1, qmine, qother, ohere, mix.state()
     )
     mix.put(st)
     sent, near1 = across(plus(far0, far1)), core(near1)
     qcame = side(qother)
     mix.on(2, count)
-    weights(6, 2)
-    sent, near0, near1, qcame, qmine, turn, gain_sum, st = meet(
-        sent, near0, near1, qcame, qmine, turn, gain_sum, mix.state()
+    weights(4, 2)
+    sent, near0, near1, qcame, qmine, turn, st = meet(
+        sent, near0, near1, qcame, qmine, turn, mix.state()
     )
     mix.put(st)
     attn_grad = plus(near0, near1).astype(F32) + sent.astype(F32)
     rms_attn, normed_attn = normed(hidden)
     input_grad = middle_grad + norm_back(attn_grad, gain_attn, rms_attn, normed_attn)
     qsums = plus(qmine, qcame)
-    qhere = [qsums[0]] + [onward(qsums[r], -r) for r in range(1, count)]
+    here = [qsums[0]] + [onward(qsums[r], -r) for r in range(1, count)]
     mix.x_(3), mix.y_(3)
-    qhere, gain_sum, st = meet(qhere, gain_sum, mix.state())
+    weights(6, 2)
+    here, turn, st = meet(here, turn, mix.state())
     mix.put(st)
-    mix.on(3, count)
-    gain_sum = gain_sum + flip(gain_sum, "dp", 2)
-    gain_sum = gain_sum + flip(gain_sum, "dp", 4)
+    mix.on(3, count), mix.x_(0), mix.y_(0)
+    here = functools.reduce(lambda a, b: a + b, [h.astype(F32) for h in here])
+    own_rows = norm_gains.shape[1]
+    qkv_sum = here[:own_rows]
     outproj_sum = functools.reduce(lambda a, b: a + b, [o.astype(F32) for o in ohere]).T
-    qkv_sum = functools.reduce(lambda a, b: a + b, [q.astype(F32) for q in qhere])
-    own_gains = norm_gains.astype(BF).astype(F32)
-    gain_part = jnp.sum(own_packed[:, :wide].astype(F32) * qkv_sum, axis=1)[None, :]
-    gain_part = gain_part + flip(gain_part, "tensor", 1)
-    gain_part = gain_part + flip(gain_part, "tensor", 2)
-    own_cols = norm_gains.shape[1]
-    gain_moe_own = lax.dynamic_slice_in_dim(gain_sum, me * own_cols, own_cols, 1)
-    gains_sum = jnp.concatenate([gain_part / own_gains[0:1], gain_moe_own], axis=0)
+    gains_sum = here[own_rows : own_rows + 2, :own_rows]
+    gains_sum = gains_sum + flip(gains_sum, "tensor", 1)
+    gains_sum = gains_sum + flip(gains_sum, "tensor", 2)
     block_out = (middle + mix.plane(0)).astype(BF)
     return (
         block_out, input_grad, gate_grad, qkv_sum, outproj_sum, gains_sum,

time: 714 us -> 710 us (level)
    ppermute x27 -> x29, waiting for transfers between devices: 109 us -> 70.6 us  [onward(): return lax.ppermute(v, 'dp', [(i, (i + 2 * planes) % n) for i in range(n)])]
    ppermute x83 -> x76, waiting for transfers between devices: 80.4 us -> 111 us  [flip(): lax.ppermute(v, axis, [(i, i ^ bit) for i in range(lax.axis_size(axis))])]
    pallas_call x4, Pallas kernels: 37.9 us -> 28.3 us  [mix_rows(): pl.pallas_call(functools.partial(mix_body, cap, plane), in_specs=[pl.Bloc...]
    pallas_call x1, Pallas kernels: 17.6 us -> 26.6 us  [attend_back(): pl.pallas_call(functools.partial(attend_back_body, share), grid_spec=pltp...]
    ppermute x27 -> x29, starting transfers between devices: 29.9 us -> 38.8 us  [onward(): return lax.ppermute(v, 'dp', [(i, (i + 2 * planes) % n) for i in range(n)])]
    ppermute x83 -> x76, starting transfers between devices: 63.5 us -> 59 us  [flip(): lax.ppermute(v, axis, [(i, i ^ bit) for i in range(lax.axis_size(axis))])]
    unnamed x261 -> x292, local copies, waits for them, and re-layouts: 21.3 us -> 23 us
  transfers between devices with their start and end apart: 110 -> 105, of which waited for: 31 -> 39; matrix products, arithmetic and copies ran while one was open for 13% -> 12% of each run, Pallas kernels for 39% -> 39%
where the time goes in v2:
time: 710 us; the launch traced here: 701 us
  Pallas kernels  278 us (39%)
  waiting for transfers between devices  182 us (26%)
  other arithmetic  103 us (15%)
  starting transfers between devices  97.7 us (14%)
  local copies, waits for them, and re-layouts  30.7 us (4%)
    ppermute x76, waiting for transfers between devices, flip(): lax.ppermute(v, axis, [(i, i ^ bit) for i in range(lax.axis_size(axis))])  111 us
    pallas_call x4, Pallas kernels, weights_step(): pl.pallas_call(functools.partial(weights_body, len(older)), grid=(count,...  72.7 us
    ppermute x29, waiting for transfers between devices, onward(): return lax.ppermute(v, 'dp', [(i, (i + 2 * planes) % n) for i in range(n)])  70.6 us
    pallas_call x4, Pallas kernels, expert_rows(): pl.pallas_call(functools.partial(main_body, cap, plane, fresh), in_specs=...  67.6 us
    ppermute x76, starting transfers between devices, flip(): lax.ppermute(v, axis, [(i, i ^ bit) for i in range(lax.axis_size(axis))])  59 us
    convert_element_type x22, other arithmetic, plus(): functools.reduce(lambda a, b: a + b, [v.astype(F32) for v in vs]).astype(BF)  47.6 us
    ppermute x29, starting transfers between devices, onward(): return lax.ppermute(v, 'dp', [(i, (i + 2 * planes) % n) for i in range(n)])  38.8 us
    pallas_call x4, Pallas kernels, seed_rows(): pl.pallas_call(functools.partial(seed_body, cap, plane, fresh), in_specs=...  35.6 us
  transfers between devices with their start and end apart: 105, of which 39 were waited for; matrix products, arithmetic and copies ran while one was open for 12% of the time, Pallas kernels for 39%

profile of v2, /device:TPU:0, one launch (start us, length us, event | category | flops | bytes accessed | tf_op | source)
XLA Modules:
  0.0 701.2 jit_solution(13224863491512955196)
XLA Ops:
  14.1 3.7 collective-permute-done.2.refs_5_
  17.8 3.4 collective-permute-done.1.refs_6_
  22.4 5.6 slot_targets.1
  38.7 6.0 collective-permute-done.8.refs_9_
  54.4 5.6 collective-permute-done.9.refs_11_
  60.0 5.4 collective-permute-done.10
  68.1 11.1 %qkv.1 = (bf16[1024,1536]{1,0:T(8,128)(2,1)}, bf16[1024,384]{1,0:T(8,128)(2,1)}, bf16[1024,128]{1,0:T(8,128)(2,1)}, bf16[1024,128]{1,0:T(8,128)(2,1)}, f32[8,1536]{1,0:T(8,128)}, /*index=5*/bf16[1536,1152]{1,0:T(8,128)(2,1)}) custom-call(s32[12]{0:T(128)} %stack.217.at, bf16[256,1536]{1,0:T(8,128)(2,1)} %refs_0_.4, bf16[256,1536]{1,0:T(8,128)(2,1)} %copy-done.136, ...), custom_call_target="tpu_custom_call" | custom-call | flops 3623878656 | bytes 20000000 | tf_op jit(solution)/shard_map/qkv/pallas_call | solution.py:142
  89.5 13.9 %attend.1 = (bf16[1024,384]{1,0:T(8,128)(2,1)S(1)}, f32[3,8,1024]{2,1,0:T(8,128)S(1)}) custom-call(s32[1]{0:T(128)} %copy.144.length, bf16[1024,384]{1,0:T(8,128)(2,1)S(1)} %copy-done.18, bf16[1024,128]{1,0:T(8,128)(2,1)S(1)} %copy-done.23, bf16[1024,128]{1,0:T(8,128)(2,1)S(1)} %copy-done.25), custom_call_target="tpu_custom_call" | custom-call | tf_op jit(solution)/shard_map/attend/pallas_call | solution.py:273
  115.1 13.7 %collective-permute-done.19 = bf16[264,1536]{1,0:T(8,128)(2,1)} collective-permute-done((bf16[264,1536]{1,0:T(8,128)(2,1)}, bf16[264,1536]{1,0:T(8,128)(2,1)}, u32[]{:S(2)}, u32[]{:S(2)}) %collective-permute-start.19) | collective-permute-done | bytes 811040 | tf_op jit(solution)/shard_map/ppermute | solution.py:871
  136.7 7.1 %round_weights.1 = (bf16[8,1536,256]{2,1,0:T(8,128)(2,1)S(1)}, bf16[8,128,1536]{2,1,0:T(8,128)(2,1)S(1)}) custom-call(s32[1]{0:T(128)} %bitcast.26.turn.first, f32[2,8,1536,128]{3,2,1,0:T(8,128)} %refs_0_.8, f32[8,128,1536]{2,1,0:T(8,128)S(1)} %copy-done), custom_call_target="tpu_custom_call" | custom-call | bytes 28000000 | tf_op jit(solution)/shard_map/round_weights/pallas_call | solution.py:736
  146.5 4.4 collective-permute-done.21
  156.3 8.9 %seed_rows.4 = (bf16[8,1280,1536]{2,1,0:T(8,128)(2,1)}, f32[8,320,128]{2,1,0:T(8,128)S(1)}, f32[8,8,1024]{2,1,0:T(8,128)S(1)}) custom-call(s32[1]{0:T(128)} %bitcast.26.turn.first, bf16[4,264,1536]{2,1,0:T(8,128)(2,1)} %pad_maximum_fusion.own, bf16[4,264,1536]{2,1,0:T(8,128)(2,1)} %collective-permute-done.20.sib, bf16[8,128,1536]{2,1,0:T(8,128)(2,1)} %copy-done.4), custom_call_target="tpu_custom_call" | custom-call | flops 3019898880 | bytes 20000000 | tf_op jit(solution)/shard_map/seed_rows/pallas_call | solution.py:507
  165.3 6.9 collective-permute-done.27
  177.6 15.2 %collective-permute-done.30 = bf16[256,1536]{1,0:T(8,128)(2,1)S(1)} collective-permute-done((bf16[256,1536]{1,0:T(8,128)(2,1)}, bf16[256,1536]{1,0:T(8,128)(2,1)S(1)}, u32[]{:S(2)}, u32[]{:S(2)}) %collective-permute-start.30) | collective-permute-done | bytes 786464 | tf_op jit(solution)/shard_map/ppermute | solution.py:871
  201.9 20.3 %collective-permute-done.33 = bf16[256,1536]{1,0:T(8,128)(2,1)} collective-permute-done((bf16[256,1536]{1,0:T(8,128)(2,1)}, bf16[256,1536]{1,0:T(8,128)(2,1)}, u32[]{:S(2)}, u32[]{:S(2)}) %collective-permute-start.33) | collective-permute-done | bytes 786464 | tf_op jit(solution)/shard_map/ppermute | solution.py:888
  228.0 16.8 %expert_rows.4 = (bf16[8,1280,1536]{2,1,0:T(8,128)(2,1)}, bf16[8,1280,256]{2,1,0:T(8,128)(2,1)}, bf16[8,1280,128]{2,1,0:T(8,128)(2,1)}, bf16[4,264,1536]{2,1,0:T(8,128)(2,1)}, bf16[4,264,1536]{2,1,0:T(8,128)(2,1)}) custom-call(s32[1]{0:T(128)} %bitcast.26.turn.first, f32[8,8,1024]{2,1,0:T(8,128)} %copy-done.45, f32[8,320,128]{2,1,0:T(8,128)} %copy-done.44, ...), custom_call_target="tpu_custom_call" | custom-call | flops 8053063680 | bytes 30000000 | tf_op jit(solution)/shard_map/expert_rows/pallas_call | solution.py:639
  251.6 11.4 %collective-permute-start.41 = (bf16[256,1536]{1,0:T(8,128)(2,1)}, bf16[256,1536]{1,0:T(8,128)(2,1)}, u32[]{:S(2)}, u32[]{:S(2)}) collective-permute-start(bf16[256,1536]{1,0:T(8,128)(2,1)} %collective-permute-done.33), channel_id=1, source_target_pairs={{0,8},{4,12},{8,16},{12,20},{16,24},{20,28},{24,0},{28,4},{1,9},{5... | collective-permute-start | bytes 2359304 | tf_op jit(solution)/shard_map/ppermute | solution.py:888
  263.6 8.8 %seed_rows.5 = (bf16[8,1280,1536]{2,1,0:T(8,128)(2,1)}, f32[8,320,128]{2,1,0:T(8,128)S(1)}, f32[8,8,1024]{2,1,0:T(8,128)S(1)}) custom-call(s32[1]{0:T(128)} %bitcast.26.turn.first, bf16[4,264,1536]{2,1,0:T(8,128)(2,1)} %copy-done.51, bf16[4,264,1536]{2,1,0:T(8,128)(2,1)} %copy-done.69, ...), custom_call_target="tpu_custom_call", output_to_operand_aliasing={{0}: (4, {})} | custom-call | flops 3019898880 | bytes 20000000 | tf_op jit(solution)/shard_map/seed_rows/pallas_call | solution.py:507
  274.2 8.8 %seed_rows.6 = (bf16[8,1280,1536]{2,1,0:T(8,128)(2,1)}, f32[8,320,128]{2,1,0:T(8,128)S(1)}, f32[8,8,1024]{2,1,0:T(8,128)S(1)}) custom-call(s32[1]{0:T(128)} %bitcast.26.turn.first, bf16[4,264,1536]{2,1,0:T(8,128)(2,1)} %copy-done.53, bf16[4,264,1536]{2,1,0:T(8,128)(2,1)} %collective-permute-done.36.sib, ...), custom_call_target="tpu_custom_call", output_to_operand_aliasing={{0}: (4, {})} | custom-call | flops 3019898880 | bytes 20000000 | tf_op jit(solution)/shard_map/seed_rows/pallas_call | solution.py:507
  290.8 16.8 %expert_rows.5 = (bf16[8,1280,1536]{2,1,0:T(8,128)(2,1)}, bf16[8,1280,256]{2,1,0:T(8,128)(2,1)}, bf16[8,1280,128]{2,1,0:T(8,128)(2,1)}, bf16[4,264,1536]{2,1,0:T(8,128)(2,1)}, bf16[4,264,1536]{2,1,0:T(8,128)(2,1)}) custom-call(s32[1]{0:T(128)} %bitcast.26.turn.first, ...), custom_call_target="tpu_custom_call", output_to_operand_aliasing={{0}: (6, {}), {1}: (7, {}), {2}: (8, {})} | custom-call | flops 8053063680 | bytes 30000000 | tf_op jit(solution)/shard_map/expert_rows/pallas_call | solution.py:639
  307.7 5.0 fusion.10
  316.7 17.0 %expert_rows.6 = (bf16[8,1280,1536]{2,1,0:T(8,128)(2,1)}, bf16[8,1280,256]{2,1,0:T(8,128)(2,1)}, bf16[8,1280,128]{2,1,0:T(8,128)(2,1)}, bf16[4,264,1536]{2,1,0:T(8,128)(2,1)}, bf16[4,264,1536]{2,1,0:T(8,128)(2,1)}) custom-call(s32[1]{0:T(128)} %bitcast.26.turn.first, ...), custom_call_target="tpu_custom_call", output_to_operand_aliasing={{0}: (6, {}), {1}: (7, {}), {2}: (8, {})} | custom-call | flops 8053063680 | bytes 30000000 | tf_op jit(solution)/shard_map/expert_rows/pallas_call | solution.py:639
  333.7 5.1 fusion.14
  345.7 7.4 %mix_rows.4 = (bf16[4,256,1536]{2,1,0:T(8,128)(2,1)S(1)}, bf16[4,256,1536]{2,1,0:T(8,128)(2,1)}) custom-call(s32[1]{0:T(128)} %bitcast.26.turn.first, f32[8,8,1024]{2,1,0:T(8,128)S(1)} %copy-done.46, bf16[8,1280,128]{2,1,0:T(8,128)(2,1)S(1)} %copy-done.1, bf16[8,128,1536]{2,1,0:T(8,128)(2,1)S(1)} %copy-done.5), custom_call_target="tpu_custom_call" | custom-call | flops 3019898880 | bytes 20000000 | tf_op jit(solution)/shard_map/mix_rows/pallas_call | solution.py:710
  354.7 9.0 %seed_rows.7 = (bf16[8,1280,1536]{2,1,0:T(8,128)(2,1)}, f32[8,320,128]{2,1,0:T(8,128)S(1)}, f32[8,8,1024]{2,1,0:T(8,128)S(1)}) custom-call(s32[1]{0:T(128)} %bitcast.26.turn.first, bf16[4,264,1536]{2,1,0:T(8,128)(2,1)} %copy-done.52, bf16[4,264,1536]{2,1,0:T(8,128)(2,1)} %collective-permute-done.49.sib, ...), custom_call_target="tpu_custom_call", output_to_operand_aliasing={{0}: (4, {})} | custom-call | flops 3019898880 | bytes 20000000 | tf_op jit(solution)/shard_map/seed_rows/pallas_call | solution.py:507
  363.8 4.7 fusion.18
  370.3 16.9 %expert_rows.7 = (bf16[8,1280,1536]{2,1,0:T(8,128)(2,1)}, bf16[8,1280,256]{2,1,0:T(8,128)(2,1)}, bf16[8,1280,128]{2,1,0:T(8,128)(2,1)}, bf16[4,264,1536]{2,1,0:T(8,128)(2,1)}, bf16[4,264,1536]{2,1,0:T(8,128)(2,1)}) custom-call(s32[1]{0:T(128)} %bitcast.26.turn.first, ...), custom_call_target="tpu_custom_call", output_to_operand_aliasing={{0}: (6, {}), {1}: (7, {}), {2}: (8, {})} | custom-call | flops 8053063680 | bytes 30000000 | tf_op jit(solution)/shard_map/expert_rows/pallas_call | solution.py:639
  387.3 4.0 fusion.26
  399.9 6.7 mix_rows.5
  407.7 5.7 collective-permute-done.61
  422.2 6.9 mix_rows.6
  431.4 7.0 collective-permute-done.67
  438.4 5.0 collective-permute-done.65
  447.7 7.3 %mix_rows.7 = (bf16[4,256,1536]{2,1,0:T(8,128)(2,1)S(1)}, bf16[4,256,1536]{2,1,0:T(8,128)(2,1)}) custom-call(s32[1]{0:T(128)} %bitcast.26.turn.first, f32[8,8,1024]{2,1,0:T(8,128)S(1)} %copy-done.39, bf16[8,1280,128]{2,1,0:T(8,128)(2,1)S(1)} %copy-done.2, bf16[8,128,1536]{2,1,0:T(8,128)(2,1)S(1)} %copy-done.6), custom_call_target="tpu_custom_call" | custom-call | flops 3019898880 | bytes 20000000 | tf_op jit(solution)/shard_map/mix_rows/pallas_call | solution.py:710
  457.8 5.8 collective-permute-done.71
  473.4 17.8 %weights_step.4 = (f32[2,8,1536,128]{3,2,1,0:T(8,128)}, f32[2,8,1536,128]{3,2,1,0:T(8,128)}, f32[2,8,1536,128]{3,2,1,0:T(8,128)}, f32[2,8,1536,128]{3,2,1,0:T(8,...) custom-call(s32[1]{0:T(128)} %bitcast.26.turn.first, ...), custom_call_target="tpu_custom_call" | custom-call | flops 3019898880 | bytes 52000000 | tf_op jit(solution)/shard_map/weights_step/pallas_call | solution.py:784
  491.2 4.1 fusion.38
  502.6 18.4 %weights_step.5 = (f32[2,8,1536,128]{3,2,1,0:T(8,128)}, f32[2,8,1536,128]{3,2,1,0:T(8,128)}, f32[2,8,1536,128]{3,2,1,0:T(8,128)}, f32[2,8,1536,128]{3,2,1,0:T(8,...) custom-call(s32[1]{0:T(128)} %get-tuple-element.1037.turn, ...), custom_call_target="tpu_custom_call", output_to_operand_aliasing={{0}: (11, {}), {1}: (12, {}), {2}: (13, {}), {3}: (14, {}),... | custom-call | flops 3019898880 | bytes 52000000 | tf_op jit(solution)/shard_map/weights_step/pallas_call | solution.py:784
  527.3 4.4 heads_back.1
  533.6 9.1 %collective-permute-done.81 = bf16[256,1536]{1,0:T(8,128)(2,1)} collective-permute-done((bf16[256,1536]{1,0:T(8,128)(2,1)}, bf16[256,1536]{1,0:T(8,128)(2,1)}, u32[]{:S(2)}, u32[]{:S(2)}) %collective-permute-start.81) | collective-permute-done | bytes 786464 | tf_op jit(solution)/shard_map/ppermute | solution.py:871
  548.5 3.5 collective-permute-start.86
  557.8 26.6 %attend_back.1 = (bf16[1024,384]{1,0:T(8,128)(2,1)S(1)}, bf16[1024,128]{1,0:T(8,128)(2,1)S(1)}, bf16[1024,128]{1,0:T(8,128)(2,1)S(1)}) custom-call(s32[1]{0:T(128)} %copy.144.length, bf16[1024,384]{1,0:T(8,128)(2,1)S(1)} %copy-done.19, bf16[1024,128]{1,0:T(8,128)(2,1)S(1)} %copy-done.24, bf16[1024,128]{1,0:T(8,128)(2,1)S(1)} %copy-done.26, ...), custom_call_target="tpu_custom_call" | custom-call | tf_op jit(solution)/shard_map/attend_back/pallas_call | solution.py:374
  589.8 4.0 fusion.87
  605.2 5.4 collective-permute-done.89
  619.7 18.1 %weights_step.6 = (f32[2,8,1536,128]{3,2,1,0:T(8,128)}, f32[2,8,1536,128]{3,2,1,0:T(8,128)}, f32[2,8,1536,128]{3,2,1,0:T(8,128)}, f32[2,8,1536,128]{3,2,1,0:T(8,...) custom-call(s32[1]{0:T(128)} %get-tuple-element.1136.turn, ...), custom_call_target="tpu_custom_call", output_to_operand_aliasing={{0}: (11, {}), {1}: (12, {}), {2}: (13, {}), {3}: (14, {}),... | custom-call | flops 3019898880 | bytes 52000000 | tf_op jit(solution)/shard_map/weights_step/pallas_call | solution.py:784
  644.9 3.4 collective-permute-start.95
  653.4 18.3 %weights_step.7 = (f32[2,8,1536,128]{3,2,1,0:T(8,128)}, f32[2,8,1536,128]{3,2,1,0:T(8,128)}, f32[2,8,1536,128]{3,2,1,0:T(8,128)}, f32[2,8,1536,128]{3,2,1,0:T(8,...) custom-call(s32[1]{0:T(128)} %get-tuple-element.1194.turn, ...), custom_call_target="tpu_custom_call", output_to_operand_aliasing={{0}: (11, {}), {1}: (12, {}), {2}: (13, {}), {3}: (14, {}),... | custom-call | flops 3019898880 | bytes 52000000 | tf_op jit(solution)/shard_map/weights_step/pallas_call | solution.py:784
  683.3 15.4 %collective-permute-done.104 = f32[2,192]{1,0:T(2,128)S(1)} collective-permute-done((f32[2,192]{1,0:T(2,128)S(1)}, f32[2,192]{1,0:T(2,128)S(1)}, u32[]{:S(2)}, u32[]{:S(2)}) %collective-permute-start.104) | collective-permute-done | bytes 1568 | tf_op jit(solution)/shard_map/ppermute | solution.py:871
  (579 shorter events, 241.0 us)
Async XLA Ops:
  9.2 27.9 %collective-permute-start.5 = (bf16[256,1536]{1,0:T(8,128)(2,1)}, bf16[256,1536]{1,0:T(8,128)(2,1)}, u32[]{:S(2)}, u32[]{:S(2)}) collective-permute-start(bf16[256,1536]{1,0:T(8,128)(2,1)} %refs_0_.4), channel_id=1, source_target_pairs={{0,2},{1,3},{2,0},{3,1},{4,6},{5,7},{6,4},{7,5},{8,10},{9,11},{10,... | collective-permute-start | bytes 2359304 | tf_op jit(solution)/shard_map/ppermute | solution.py:871
  128.9 22.1 %collective-permute-start.24 = (bf16[264,1536]{1,0:T(8,128)(2,1)}, bf16[264,1536]{1,0:T(8,128)(2,1)S(1)}, u32[]{:S(2)}, u32[]{:S(2)}) collective-permute-start(bf16[264,1536]{1,0:T(8,128)(2,1)} %collective-permute-done.16), channel_id=1, source_target_pairs={{0,4},{4,0},{8,12},{12,8},{16,20},{20,16},{24,28},{28,24},{1,5},{5... | collective-permute-start | bytes 2433032 | tf_op jit(solution)/shard_map/ppermute | solution.py:871
  130.4 21.9 %collective-permute-start.23 = (bf16[264,1536]{1,0:T(8,128)(2,1)}, bf16[264,1536]{1,0:T(8,128)(2,1)S(1)}, u32[]{:S(2)}, u32[]{:S(2)}) collective-permute-start(bf16[264,1536]{1,0:T(8,128)(2,1)} %collective-permute-done.19), channel_id=1, source_target_pairs={{0,8},{4,12},{8,16},{12,20},{16,24},{20,28},{24,0},{28,4},{1,9},{5... | collective-permute-start | bytes 2433032 | tf_op jit(solution)/shard_map/ppermute | solution.py:888
  197.5 24.7 %collective-permute-start.32 = (bf16[4,264,1536]{2,1,0:T(8,128)(2,1)S(1)}, bf16[4,264,1536]{2,1,0:T(8,128)(2,1)S(1)}, u32[]{:S(2)}, u32[]{:S(2)}) collective-permute-start(bf16[4,264,1536]{2,1,0:T(8,128)(2,1)S(1)} %pad_maximum_fusion.1.own), channel_id=1, source_target_pairs={{0,1},{1,0},{2,3},{3,2},{4,5},{5,4},{6,7},{7,6},{8,9},{9,8},{10,11... | collective-permute-start | bytes 9732104 | tf_op jit(solution)/shard_map/ppermute | solution.py:871
  199.9 22.4 %collective-permute-start.35 = (bf16[4,256,1536]{2,1,0:T(8,128)(2,1)S(1)}, bf16[4,256,1536]{2,1,0:T(8,128)(2,1)S(1)}, u32[]{:S(2)}, u32[]{:S(2)}) collective-permute-start(bf16[4,256,1536]{2,1,0:T(8,128)(2,1)S(1)} %pad_maximum_fusion.4.own_in), channel_id=1, source_target_pairs={{0,1},{1,0},{2,3},{3,2},{4,5},{5,4},{6,7},{7,6},{8,9},{9,8},{10,11... | collective-permute-start | bytes 9437192 | tf_op jit(solution)/shard_map/ppermute | solution.py:871
  200.1 22.1 %collective-permute-start.31 = (bf16[264,1536]{1,0:T(8,128)(2,1)S(1)}, bf16[264,1536]{1,0:T(8,128)(2,1)S(1)}, u32[]{:S(2)}, u32[]{:S(2)}) collective-permute-start(bf16[264,1536]{1,0:T(8,128)(2,1)S(1)} %copy-done.87), channel_id=1, source_target_pairs={{0,4},{4,0},{8,12},{12,8},{16,20},{20,16},{24,28},{28,24},{1,5},{5... | collective-permute-start | bytes 2433032 | tf_op jit(solution)/shard_map/ppermute | solution.py:871
  200.6 21.6 %collective-permute-start.33 = (bf16[256,1536]{1,0:T(8,128)(2,1)}, bf16[256,1536]{1,0:T(8,128)(2,1)}, u32[]{:S(2)}, u32[]{:S(2)}) collective-permute-start(bf16[256,1536]{1,0:T(8,128)(2,1)} %collective-permute-done.25), channel_id=1, source_target_pairs={{0,8},{4,12},{8,16},{12,20},{16,24},{20,28},{24,0},{28,4},{1,9},{5... | collective-permute-start | bytes 2359304 | tf_op jit(solution)/shard_map/ppermute | solution.py:888
  225.8 22.1 %collective-permute-start.36 = (bf16[4,264,1536]{2,1,0:T(8,128)(2,1)S(1)}, bf16[4,264,1536]{2,1,0:T(8,128)(2,1)}, u32[]{:S(2)}, u32[]{:S(2)}) collective-permute-start(bf16[4,264,1536]{2,1,0:T(8,128)(2,1)S(1)} %pad_maximum_fusion.2.own), channel_id=1, source_target_pairs={{0,1},{1,0},{2,3},{3,2},{4,5},{5,4},{6,7},{7,6},{8,9},{9,8},{10,11... | collective-permute-start | bytes 9732104 | tf_op jit(solution)/shard_map/ppermute | solution.py:871
  225.9 22.0 %collective-permute-start.37 = (bf16[256,1536]{1,0:T(8,128)(2,1)}, bf16[256,1536]{1,0:T(8,128)(2,1)}, u32[]{:S(2)}, u32[]{:S(2)}) collective-permute-start(bf16[256,1536]{1,0:T(8,128)(2,1)} %collective-permute-done.26), channel_id=1, source_target_pairs={{0,8},{4,12},{8,16},{12,20},{16,24},{20,28},{24,0},{28,4},{1,9},{5... | collective-permute-start | bytes 2359304 | tf_op jit(solution)/shard_map/ppermute | solution.py:888
  226.0 22.0 %collective-permute-start.39 = (bf16[256,1536]{1,0:T(8,128)(2,1)}, bf16[256,1536]{1,0:T(8,128)(2,1)}, u32[]{:S(2)}, u32[]{:S(2)}) collective-permute-start(bf16[256,1536]{1,0:T(8,128)(2,1)} %collective-permute-done.33), channel_id=1, source_target_pairs={{0,4},{4,0},{8,12},{12,8},{16,20},{20,16},{24,28},{28,24},{1,5},{5... | collective-permute-start | bytes 2359304 | tf_op jit(solution)/shard_map/ppermute | solution.py:871
  250.1 34.6 %collective-permute-start.43 = (bf16[4,256,1536]{2,1,0:T(8,128)(2,1)S(1)}, bf16[4,256,1536]{2,1,0:T(8,128)(2,1)S(1)}, u32[]{:S(2)}, u32[]{:S(2)}) collective-permute-start(bf16[4,256,1536]{2,1,0:T(8,128)(2,1)S(1)} %pad_maximum_fusion.5.own_in), channel_id=1, source_target_pairs={{0,1},{1,0},{2,3},{3,2},{4,5},{5,4},{6,7},{7,6},{8,9},{9,8},{10,11... | collective-permute-start | bytes 9437192 | tf_op jit(solution)/shard_map/ppermute | solution.py:871
  250.2 34.5 %collective-permute-start.40 = (bf16[264,1536]{1,0:T(8,128)(2,1)S(1)}, bf16[264,1536]{1,0:T(8,128)(2,1)S(1)}, u32[]{:S(2)}, u32[]{:S(2)}) collective-permute-start(bf16[264,1536]{1,0:T(8,128)(2,1)S(1)} %collective-permute-done.31), channel_id=1, source_target_pairs={{0,2},{1,3},{2,0},{3,1},{4,6},{5,7},{6,4},{7,5},{8,10},{9,11},{10,... | collective-permute-start | bytes 2433032 | tf_op jit(solution)/shard_map/ppermute | solution.py:871
  251.6 33.1 %collective-permute-start.41 = (bf16[256,1536]{1,0:T(8,128)(2,1)}, bf16[256,1536]{1,0:T(8,128)(2,1)}, u32[]{:S(2)}, u32[]{:S(2)}) collective-permute-start(bf16[256,1536]{1,0:T(8,128)(2,1)} %collective-permute-done.33), channel_id=1, source_target_pairs={{0,8},{4,12},{8,16},{12,20},{16,24},{20,28},{24,0},{28,4},{1,9},{5... | collective-permute-start | bytes 2359304 | tf_op jit(solution)/shard_map/ppermute | solution.py:888
  262.9 21.7 %collective-permute-start.42 = (bf16[256,1536]{1,0:T(8,128)(2,1)}, bf16[256,1536]{1,0:T(8,128)(2,1)S(1)}, u32[]{:S(2)}, u32[]{:S(2)}) collective-permute-start(bf16[256,1536]{1,0:T(8,128)(2,1)} %collective-permute-done.38), channel_id=1, source_target_pairs={{0,4},{4,0},{8,12},{12,8},{16,20},{20,16},{24,28},{28,24},{1,5},{5... | collective-permute-start | bytes 2359304 | tf_op jit(solution)/shard_map/ppermute | solution.py:871
  284.7 23.0 %collective-permute-start.48 = (bf16[4,264,1536]{2,1,0:T(8,128)(2,1)}, bf16[4,264,1536]{2,1,0:T(8,128)(2,1)}, u32[]{:S(2)}, u32[]{:S(2)}) collective-permute-start(bf16[4,264,1536]{2,1,0:T(8,128)(2,1)} %get-tuple-element.828), channel_id=1, source_target_pairs={{0,1},{1,0},{2,3},{3,2},{4,5},{5,4},{6,7},{7,6},{8,9},{9,8},{10,11... | collective-permute-start | bytes 9732104 | tf_op jit(solution)/shard_map/ppermute | solution.py:871
  288.0 24.8 %collective-permute-start.47 = (bf16[4,256,1536]{2,1,0:T(8,128)(2,1)S(1)}, bf16[4,256,1536]{2,1,0:T(8,128)(2,1)}, u32[]{:S(2)}, u32[]{:S(2)}) collective-permute-start(bf16[4,256,1536]{2,1,0:T(8,128)(2,1)S(1)} %pad_maximum_fusion.6.own_in), channel_id=1, source_target_pairs={{0,1},{1,0},{2,3},{3,2},{4,5},{5,4},{6,7},{7,6},{8,9},{9,8},{10,11... | collective-permute-start | bytes 9437192 | tf_op jit(solution)/shard_map/ppermute | solution.py:871
  288.0 24.7 %collective-permute-start.46 = (bf16[256,1536]{1,0:T(8,128)(2,1)}, bf16[256,1536]{1,0:T(8,128)(2,1)}, u32[]{:S(2)}, u32[]{:S(2)}) collective-permute-start(bf16[256,1536]{1,0:T(8,128)(2,1)} %collective-permute-done.41), channel_id=1, source_target_pairs={{0,4},{4,0},{8,12},{12,8},{16,20},{20,16},{24,28},{28,24},{1,5},{5... | collective-permute-start | bytes 2359304 | tf_op jit(solution)/shard_map/ppermute | solution.py:871
  288.7 24.1 %collective-permute-start.45 = (bf16[256,1536]{1,0:T(8,128)(2,1)}, bf16[256,1536]{1,0:T(8,128)(2,1)}, u32[]{:S(2)}, u32[]{:S(2)}) collective-permute-start(bf16[256,1536]{1,0:T(8,128)(2,1)} %collective-permute-done.41), channel_id=1, source_target_pairs={{0,2},{1,3},{2,0},{3,1},{4,6},{5,7},{6,4},{7,5},{8,10},{9,11},{10,... | collective-permute-start | bytes 2359304 | tf_op jit(solution)/shard_map/ppermute | solution.py:871
  290.3 22.4 %collective-permute-start.44 = (bf16[264,1536]{1,0:T(8,128)(2,1)}, bf16[264,1536]{1,0:T(8,128)(2,1)}, u32[]{:S(2)}, u32[]{:S(2)}) collective-permute-start(bf16[264,1536]{1,0:T(8,128)(2,1)} %collective-permute-done.16), channel_id=1, source_target_pairs={{0,8},{4,12},{8,16},{12,20},{16,24},{20,28},{24,0},{28,4},{1,9},{5... | collective-permute-start | bytes 2433032 | tf_op jit(solution)/shard_map/ppermute | solution.py:888
  314.3 24.5 %collective-permute-start.49 = (bf16[4,264,1536]{2,1,0:T(8,128)(2,1)S(1)}, bf16[4,264,1536]{2,1,0:T(8,128)(2,1)}, u32[]{:S(2)}, u32[]{:S(2)}) collective-permute-start(bf16[4,264,1536]{2,1,0:T(8,128)(2,1)S(1)} %pad_maximum_fusion.3.own), channel_id=1, source_target_pairs={{0,1},{1,0},{2,3},{3,2},{4,5},{5,4},{6,7},{7,6},{8,9},{9,8},{10,11... | collective-permute-start | bytes 9732104 | tf_op jit(solution)/shard_map/ppermute | solution.py:871
  314.9 24.0 %collective-permute-start.50 = (bf16[256,1536]{1,0:T(8,128)(2,1)}, bf16[256,1536]{1,0:T(8,128)(2,1)}, u32[]{:S(2)}, u32[]{:S(2)}) collective-permute-start(bf16[256,1536]{1,0:T(8,128)(2,1)} %collective-permute-done.46), channel_id=1, source_target_pairs={{0,2},{1,3},{2,0},{3,1},{4,6},{5,7},{6,4},{7,5},{8,10},{9,11},{10,... | collective-permute-start | bytes 2359304 | tf_op jit(solution)/shard_map/ppermute | solution.py:871
  315.2 23.6 %collective-permute-start.52 = (bf16[264,1536]{1,0:T(8,128)(2,1)}, bf16[264,1536]{1,0:T(8,128)(2,1)}, u32[]{:S(2)}, u32[]{:S(2)}) collective-permute-start(bf16[264,1536]{1,0:T(8,128)(2,1)} %get-tuple-element.852), channel_id=1, source_target_pairs={{0,4},{4,0},{8,12},{12,8},{16,20},{20,16},{24,28},{28,24},{1,5},{5... | collective-permute-start | bytes 2433032 | tf_op jit(solution)/shard_map/ppermute | solution.py:871
  338.8 24.9 %collective-permute-start.54 = (bf16[4,264,1536]{2,1,0:T(8,128)(2,1)}, bf16[4,264,1536]{2,1,0:T(8,128)(2,1)}, u32[]{:S(2)}, u32[]{:S(2)}) collective-permute-start(bf16[4,264,1536]{2,1,0:T(8,128)(2,1)} %get-tuple-element.877), channel_id=1, source_target_pairs={{0,1},{1,0},{2,3},{3,2},{4,5},{5,4},{6,7},{7,6},{8,9},{9,8},{10,11... | collective-permute-start | bytes 9732104 | tf_op jit(solution)/shard_map/ppermute | solution.py:871
  341.2 27.4 %collective-permute-start.53 = (bf16[4,256,1536]{2,1,0:T(8,128)(2,1)S(1)}, bf16[4,256,1536]{2,1,0:T(8,128)(2,1)}, u32[]{:S(2)}, u32[]{:S(2)}) collective-permute-start(bf16[4,256,1536]{2,1,0:T(8,128)(2,1)S(1)} %pad_maximum_fusion.7.own_in), channel_id=1, source_target_pairs={{0,1},{1,0},{2,3},{3,2},{4,5},{5,4},{6,7},{7,6},{8,9},{9,8},{10,11... | collective-permute-start | bytes 9437192 | tf_op jit(solution)/shard_map/ppermute | solution.py:871
  341.7 26.8 %collective-permute-start.56 = (bf16[264,1536]{1,0:T(8,128)(2,1)}, bf16[264,1536]{1,0:T(8,128)(2,1)}, u32[]{:S(2)}, u32[]{:S(2)}) collective-permute-start(bf16[264,1536]{1,0:T(8,128)(2,1)} %get-tuple-element.873), channel_id=1, source_target_pairs={{0,24},{4,28},{8,0},{12,4},{16,8},{20,12},{24,16},{28,20},{1,25},{... | collective-permute-start | bytes 2433032 | tf_op jit(solution)/shard_map/ppermute | solution.py:888
  345.1 23.5 %collective-permute-start.55 = (bf16[264,1536]{1,0:T(8,128)(2,1)}, bf16[264,1536]{1,0:T(8,128)(2,1)}, u32[]{:S(2)}, u32[]{:S(2)}) collective-permute-start(bf16[264,1536]{1,0:T(8,128)(2,1)} %get-tuple-element.875), channel_id=1, source_target_pairs={{0,2},{1,3},{2,0},{3,1},{4,6},{5,7},{6,4},{7,5},{8,10},{9,11},{10,... | collective-permute-start | bytes 2433032 | tf_op jit(solution)/shard_map/ppermute | solution.py:871
  368.6 22.7 %collective-permute-start.58 = (bf16[264,1536]{1,0:T(8,128)(2,1)}, bf16[264,1536]{1,0:T(8,128)(2,1)}, u32[]{:S(2)}, u32[]{:S(2)}) collective-permute-start(bf16[264,1536]{1,0:T(8,128)(2,1)} %get-tuple-element.897), channel_id=1, source_target_pairs={{0,8},{4,12},{8,16},{12,20},{16,24},{20,28},{24,0},{28,4},{1,9},{5... | collective-permute-start | bytes 2433032 | tf_op jit(solution)/shard_map/ppermute | solution.py:888
  369.4 21.8 %collective-permute-start.57 = (bf16[264,1536]{1,0:T(8,128)(2,1)}, bf16[264,1536]{1,0:T(8,128)(2,1)}, u32[]{:S(2)}, u32[]{:S(2)}) collective-permute-start(bf16[264,1536]{1,0:T(8,128)(2,1)} %get-tuple-element.902), channel_id=1, source_target_pairs={{0,4},{4,0},{8,12},{12,8},{16,20},{20,16},{24,28},{28,24},{1,5},{5... | collective-permute-start | bytes 2433032 | tf_op jit(solution)/shard_map/ppermute | solution.py:871
  421.4 22.1 %collective-permute-start.65 = (bf16[264,1536]{1,0:T(8,128)(2,1)S(1)}, bf16[264,1536]{1,0:T(8,128)(2,1)S(1)}, u32[]{:S(2)}, u32[]{:S(2)}) collective-permute-start(bf16[264,1536]{1,0:T(8,128)(2,1)S(1)} %add_convert_fusion.5), channel_id=1, source_target_pairs={{0,8},{4,12},{8,16},{12,20},{16,24},{20,28},{24,0},{28,4},{1,9},{5... | collective-permute-start | bytes 2433032 | tf_op jit(solution)/shard_map/ppermute | solution.py:888
  421.4 22.0 %collective-permute-start.64 = (bf16[264,1536]{1,0:T(8,128)(2,1)S(1)}, bf16[264,1536]{1,0:T(8,128)(2,1)S(1)}, u32[]{:S(2)}, u32[]{:S(2)}) collective-permute-start(bf16[264,1536]{1,0:T(8,128)(2,1)S(1)} %get-tuple-element.945), channel_id=1, source_target_pairs={{0,2},{1,3},{2,0},{3,1},{4,6},{5,7},{6,4},{7,5},{8,10},{9,11},{10,... | collective-permute-start | bytes 2433032 | tf_op jit(solution)/shard_map/ppermute | solution.py:871
  466.0 25.2 %collective-permute-start.75 = (bf16[4,256,1536]{2,1,0:T(8,128)(2,1)}, bf16[4,256,1536]{2,1,0:T(8,128)(2,1)}, u32[]{:S(2)}, u32[]{:S(2)}) collective-permute-start(bf16[4,256,1536]{2,1,0:T(8,128)(2,1)} %get-tuple-element.1012), channel_id=1, source_target_pairs={{0,1},{1,0},{2,3},{3,2},{4,5},{5,4},{6,7},{7,6},{8,9},{9,8},{10,11... | collective-permute-start | bytes 9437192 | tf_op jit(solution)/shard_map/ppermute | solution.py:871
  467.1 28.2 %collective-permute-start.73 = (bf16[264,1536]{1,0:T(8,128)(2,1)}, bf16[264,1536]{1,0:T(8,128)(2,1)S(1)}, u32[]{:S(2)}, u32[]{:S(2)}) collective-permute-start(bf16[264,1536]{1,0:T(8,128)(2,1)} %add_convert_fusion.2), channel_id=1, source_target_pairs={{0,4},{4,0},{8,12},{12,8},{16,20},{20,16},{24,28},{28,24},{1,5},{5... | collective-permute-start | bytes 2433032 | tf_op jit(solution)/shard_map/ppermute | solution.py:871
  471.1 24.2 %collective-permute-start.72 = (bf16[264,1536]{1,0:T(8,128)(2,1)}, bf16[264,1536]{1,0:T(8,128)(2,1)S(1)}, u32[]{:S(2)}, u32[]{:S(2)}) collective-permute-start(bf16[264,1536]{1,0:T(8,128)(2,1)} %add_convert_fusion.3), channel_id=1, source_target_pairs={{0,2},{1,3},{2,0},{3,1},{4,6},{5,7},{6,4},{7,5},{8,10},{9,11},{10,... | collective-permute-start | bytes 2433032 | tf_op jit(solution)/shard_map/ppermute | solution.py:871
  473.1 22.2 %collective-permute-start.74 = (bf16[264,1536]{1,0:T(8,128)(2,1)}, bf16[264,1536]{1,0:T(8,128)(2,1)}, u32[]{:S(2)}, u32[]{:S(2)}) collective-permute-start(bf16[264,1536]{1,0:T(8,128)(2,1)} %add_convert_fusion.1), channel_id=1, source_target_pairs={{0,8},{4,12},{8,16},{12,20},{16,24},{20,28},{24,0},{28,4},{1,9},{5... | collective-permute-start | bytes 2433032 | tf_op jit(solution)/shard_map/ppermute | solution.py:888
  544.9 40.5 %collective-permute-start.84 = (bf16[256,1536]{1,0:T(8,128)(2,1)}, bf16[256,1536]{1,0:T(8,128)(2,1)}, u32[]{:S(2)}, u32[]{:S(2)}) collective-permute-start(bf16[256,1536]{1,0:T(8,128)(2,1)} %add_convert_fusion.33), channel_id=1, source_target_pairs={{0,2},{1,3},{2,0},{3,1},{4,6},{5,7},{6,4},{7,5},{8,10},{9,11},{10,... | collective-permute-start | bytes 2359304 | tf_op jit(solution)/shard_map/ppermute | solution.py:871
  548.5 36.9 %collective-permute-start.86 = (bf16[256,1536]{1,0:T(8,128)(2,1)}, bf16[256,1536]{1,0:T(8,128)(2,1)}, u32[]{:S(2)}, u32[]{:S(2)}) collective-permute-start(bf16[256,1536]{1,0:T(8,128)(2,1)} %add_convert_fusion.32), channel_id=1, source_target_pairs={{0,24},{4,28},{8,0},{12,4},{16,8},{20,12},{24,16},{28,20},{1,25},{... | collective-permute-start | bytes 2359304 | tf_op jit(solution)/shard_map/ppermute | solution.py:888
  552.0 33.4 %collective-permute-start.85 = (bf16[256,1536]{1,0:T(8,128)(2,1)}, bf16[256,1536]{1,0:T(8,128)(2,1)}, u32[]{:S(2)}, u32[]{:S(2)}) collective-permute-start(bf16[256,1536]{1,0:T(8,128)(2,1)} %get-tuple-element.1095), channel_id=1, source_target_pairs={{0,4},{4,0},{8,12},{12,8},{16,20},{20,16},{24,28},{28,24},{1,5},{5... | collective-permute-start | bytes 2359304 | tf_op jit(solution)/shard_map/ppermute | solution.py:871
  552.5 32.9 %collective-permute-start.83 = (bf16[256,1536]{1,0:T(8,128)(2,1)}, bf16[256,1536]{1,0:T(8,128)(2,1)}, u32[]{:S(2)}, u32[]{:S(2)}) collective-permute-start(bf16[256,1536]{1,0:T(8,128)(2,1)} %get-tuple-element.1099), channel_id=1, source_target_pairs={{0,2},{1,3},{2,0},{3,1},{4,6},{5,7},{6,4},{7,5},{8,10},{9,11},{10,... | collective-permute-start | bytes 2359304 | tf_op jit(solution)/shard_map/ppermute | solution.py:871
  555.7 29.7 %collective-permute-start.82 = (bf16[4,192,384]{2,1,0:T(8,128)(2,1)}, bf16[4,192,384]{2,1,0:T(8,128)(2,1)}, u32[]{:S(2)}, u32[]{:S(2)}) collective-permute-start(bf16[4,192,384]{2,1,0:T(8,128)(2,1)} %pad_maximum_fusion.11), channel_id=1, source_target_pairs={{0,4},{4,0},{8,12},{12,8},{16,20},{20,16},{24,28},{28,24},{1,5},{5... | collective-permute-start | bytes 1769480 | tf_op jit(solution)/shard_map/ppermute | solution.py:871
  613.6 26.4 %collective-permute-start.94 = (bf16[256,1536]{1,0:T(8,128)(2,1)}, bf16[256,1536]{1,0:T(8,128)(2,1)}, u32[]{:S(2)}, u32[]{:S(2)}) collective-permute-start(bf16[256,1536]{1,0:T(8,128)(2,1)} %add_convert_fusion.30), channel_id=1, source_target_pairs={{0,8},{4,12},{8,16},{12,20},{16,24},{20,28},{24,0},{28,4},{1,9},{5... | collective-permute-start | bytes 2359304 | tf_op jit(solution)/shard_map/ppermute | solution.py:888
  616.7 24.1 %collective-permute-start.93 = (bf16[4,200,640]{2,1,0:T(8,128)(2,1)}, bf16[4,200,640]{2,1,0:T(8,128)(2,1)}, u32[]{:S(2)}, u32[]{:S(2)}) collective-permute-start(bf16[4,200,640]{2,1,0:T(8,128)(2,1)} %pad_maximum_fusion.9), channel_id=1, source_target_pairs={{0,4},{4,0},{8,12},{12,8},{16,20},{20,16},{24,28},{28,24},{1,5},{5... | collective-permute-start | bytes 3072008 | tf_op jit(solution)/shard_map/ppermute | solution.py:871
  617.1 22.9 %collective-permute-start.91 = (bf16[256,1536]{1,0:T(8,128)(2,1)S(1)}, bf16[256,1536]{1,0:T(8,128)(2,1)S(1)}, u32[]{:S(2)}, u32[]{:S(2)}) collective-permute-start(bf16[256,1536]{1,0:T(8,128)(2,1)S(1)} %add_convert_fusion.31), channel_id=1, source_target_pairs={{0,2},{1,3},{2,0},{3,1},{4,6},{5,7},{6,4},{7,5},{8,10},{9,11},{10,... | collective-permute-start | bytes 2359304 | tf_op jit(solution)/shard_map/ppermute | solution.py:871
  644.2 27.6 %collective-permute-start.97 = (bf16[200,640]{1,0:T(8,128)(2,1)}, bf16[200,640]{1,0:T(8,128)(2,1)S(1)}, u32[]{:S(2)}, u32[]{:S(2)}) collective-permute-start(bf16[200,640]{1,0:T(8,128)(2,1)} %get-tuple-element.1287), channel_id=1, source_target_pairs={{0,8},{4,12},{8,16},{12,20},{16,24},{20,28},{24,0},{28,4},{1,9},{5... | collective-permute-start | bytes 768008 | tf_op jit(solution)/shard_map/ppermute | solution.py:888
  644.6 27.2 %collective-permute-start.96 = (bf16[200,640]{1,0:T(8,128)(2,1)S(1)}, bf16[200,640]{1,0:T(8,128)(2,1)}, u32[]{:S(2)}, u32[]{:S(2)}) collective-permute-start(bf16[200,640]{1,0:T(8,128)(2,1)S(1)} %get-tuple-element.1288), channel_id=1, source_target_pairs={{0,16},{4,20},{8,24},{12,28},{16,0},{20,4},{24,8},{28,12},{1,17},{... | collective-permute-start | bytes 768008 | tf_op jit(solution)/shard_map/ppermute | solution.py:888
  644.9 26.8 %collective-permute-start.95 = (bf16[200,640]{1,0:T(8,128)(2,1)S(1)}, bf16[200,640]{1,0:T(8,128)(2,1)}, u32[]{:S(2)}, u32[]{:S(2)}) collective-permute-start(bf16[200,640]{1,0:T(8,128)(2,1)S(1)} %get-tuple-element.1289), channel_id=1, source_target_pairs={{0,24},{4,28},{8,0},{12,4},{16,8},{20,12},{24,16},{28,20},{1,25},{... | collective-permute-start | bytes 768008 | tf_op jit(solution)/shard_map/ppermute | solution.py:888
  649.6 22.1 %collective-permute-start.99 = (bf16[256,1536]{1,0:T(8,128)(2,1)S(1)}, bf16[256,1536]{1,0:T(8,128)(2,1)S(1)}, u32[]{:S(2)}, u32[]{:S(2)}) collective-permute-start(bf16[256,1536]{1,0:T(8,128)(2,1)S(1)} %add_convert_fusion.29), channel_id=1, source_target_pairs={{0,4},{4,0},{8,12},{12,8},{16,20},{20,16},{24,28},{28,24},{1,5},{5... | collective-permute-start | bytes 2359304 | tf_op jit(solution)/shard_map/ppermute | solution.py:871
  675.0 24.3 %collective-permute-start.102 = (bf16[256,1536]{1,0:T(8,128)(2,1)S(1)}, bf16[256,1536]{1,0:T(8,128)(2,1)S(1)}, u32[]{:S(2)}, u32[]{:S(2)}) collective-permute-start(bf16[256,1536]{1,0:T(8,128)(2,1)S(1)} %add_convert_fusion.26), channel_id=1, source_target_pairs={{0,8},{4,12},{8,16},{12,20},{16,24},{20,28},{24,0},{28,4},{1,9},{5... | collective-permute-start | bytes 2359304 | tf_op jit(solution)/shard_map/ppermute | solution.py:888
  677.0 22.3 %collective-permute-start.101 = (bf16[256,1536]{1,0:T(8,128)(2,1)S(1)}, bf16[256,1536]{1,0:T(8,128)(2,1)S(1)}, u32[]{:S(2)}, u32[]{:S(2)}) collective-permute-start(bf16[256,1536]{1,0:T(8,128)(2,1)S(1)} %add_convert_fusion.27), channel_id=1, source_target_pairs={{0,4},{4,0},{8,12},{12,8},{16,20},{20,16},{24,28},{28,24},{1,5},{5... | collective-permute-start | bytes 2359304 | tf_op jit(solution)/shard_map/ppermute | solution.py:871
  (200 other events, 2223.9 us)

commit v3 on v2

--- a/solution.py
+++ b/solution.py
@@ -1152,7 +1152,7 @@
     seed(3)
     mixes(0)
     step()
-    back.d_(2), back.on(1, count), mix.cores(0)
+    back.x_(0), back.d_(2), back.on(1, count), mix.cores(0)
     expert(3)
     step()
     back.x_(2), back.y_(2), back.y_in(1), back.cores(3)
@@ -1163,9 +1163,10 @@
     step()
     back.x_(3), back.y_(3), mix.x_in(1), mix.cores(2)
     mixes(3)
+    weights(0, 1)
     step()
-    back.x_(0), back.y_(0), back.on(3, count), mix.cores(3)
-    weights(0, 2)
+    mix.d_(1), back.y_(0), back.on(3, count), mix.cores(3)
+    weights(1, 1)
     step()
     whole = back.plane(0)
     gate_grad, moe_grad = whole[BLOCK:, :BLOCK].T, whole[:BLOCK]
@@ -1181,7 +1182,6 @@
     mx, mc, turn, st, gain_part = meet(mx, mc, turn, mix.state(), gain_part)
     mix.put(st)
     mxc = core(mx)
-    mix.d_(1)
     heads_grad, middle_low = heads_back(at, [mid, mc, mx, mxc], packed, out_cols)
     outproj_part = mm(middle_low, heads, TN).astype(BF)
     heads_grad, outproj_part, st = meet(heads_grad, outproj_part, mix.state())
@@ -1222,10 +1222,11 @@
     qsums = plus(qmine, qcame)
     here = [qsums[0]] + [onward(qsums[r], -r) for r in range(1, count)]
     mix.x_(3), mix.y_(3)
-    weights(6, 2)
+    weights(6, 1)
     here, turn, st = meet(here, turn, mix.state())
     mix.put(st)
     mix.on(3, count), mix.x_(0), mix.y_(0)
+    weights(7, 1)
     here = functools.reduce(lambda a, b: a + b, [h.astype(F32) for h in here])
     own_rows = norm_gains.shape[1]
     qkv_sum = here[:own_rows]

time: 710 us -> 688 us (0.969)
  waiting for transfers between devices: 182 us -> 161 us
    ppermute x76, waiting for transfers between devices: 111 us -> 61.6 us  [flip(): lax.ppermute(v, axis, [(i, i ^ bit) for i in range(lax.axis_size(axis))])]
    ppermute x29, waiting for transfers between devices: 70.6 us -> 99.7 us  [onward(): return lax.ppermute(v, 'dp', [(i, (i + 2 * planes) % n) for i in range(n)])]
    pallas_call x1, Pallas kernels: 26.6 us -> 17.8 us  [attend_back(): pl.pallas_call(functools.partial(attend_back_body, share), grid_spec=pltp...]
    pallas_call x4 -> x6, Pallas kernels: 72.7 us -> 76.4 us  [weights_step(): pl.pallas_call(functools.partial(weights_body, len(older)), grid=(count,...]
    unnamed x292 -> x298, local copies, waits for them, and re-layouts: 23 us -> 25.6 us
  transfers between devices with their start and end apart: 105 -> 105, of which waited for: 39 -> 33; matrix products, arithmetic and copies ran while one was open for 12% -> 13% of each run, Pallas kernels for 39% -> 39%
where the time goes in v3:
time: 688 us; the launch traced here: 684 us
  Pallas kernels  274 us (40%)
  waiting for transfers between devices  161 us (23%)
  other arithmetic  107 us (16%)
  starting transfers between devices  97.8 us (14%)
  local copies, waits for them, and re-layouts  33.9 us (5%)
    ppermute x29, waiting for transfers between devices, onward(): return lax.ppermute(v, 'dp', [(i, (i + 2 * planes) % n) for i in range(n)])  99.7 us
    pallas_call x6, Pallas kernels, weights_step(): pl.pallas_call(functools.partial(weights_body, len(older)), grid=(count,...  76.4 us
    pallas_call x4, Pallas kernels, expert_rows(): pl.pallas_call(functools.partial(main_body, cap, plane, fresh), in_specs=...  67.8 us
    ppermute x76, waiting for transfers between devices, flip(): lax.ppermute(v, axis, [(i, i ^ bit) for i in range(lax.axis_size(axis))])  61.6 us
    ppermute x76, starting transfers between devices, flip(): lax.ppermute(v, axis, [(i, i ^ bit) for i in range(lax.axis_size(axis))])  60 us
    convert_element_type x22, other arithmetic, plus(): functools.reduce(lambda a, b: a + b, [v.astype(F32) for v in vs]).astype(BF)  49.6 us
    ppermute x29, starting transfers between devices, onward(): return lax.ppermute(v, 'dp', [(i, (i + 2 * planes) % n) for i in range(n)])  37.8 us
    pallas_call x4, Pallas kernels, seed_rows(): pl.pallas_call(functools.partial(seed_body, cap, plane, fresh), in_specs=...  35.2 us
  transfers between devices with their start and end apart: 105, of which 33 were waited for; matrix products, arithmetic and copies ran while one was open for 13% of the time, Pallas kernels for 39%

profile of v3, /device:TPU:0, one launch (start us, length us, event | category | flops | bytes accessed | tf_op | source)
XLA Modules:
  0.0 683.8 jit_solution(7912534613711793908)
XLA Ops:
  14.1 5.8 collective-permute-done.1.refs_6_
  23.1 5.6 slot_targets.1
  37.4 8.2 %collective-permute-done.7.refs_10_ = bf16[192,1152]{1,0:T(8,128)(2,1)S(1)} collective-permute-done((bf16[192,1152]{1,0:T(8,128)(2,1)}, bf16[192,1152]{1,0:T(8,128)(2,1)S(1)}, u32[]{:S(2)}, u32[]{:S(2)}) %collective-permute-start.7) | collective-permute-done | bytes 442400 | tf_op jit(solution)/shard_map/ppermute | solution.py:888
  53.5 4.9 collective-permute-done.9.refs_11_
  58.4 6.6 collective-permute-done.10
  68.0 11.2 %qkv.1 = (bf16[1024,1536]{1,0:T(8,128)(2,1)}, bf16[1024,384]{1,0:T(8,128)(2,1)}, bf16[1024,128]{1,0:T(8,128)(2,1)}, bf16[1024,128]{1,0:T(8,128)(2,1)}, f32[8,1536]{1,0:T(8,128)}, /*index=5*/bf16[1536,1152]{1,0:T(8,128)(2,1)}) custom-call(s32[12]{0:T(128)} %stack.217.at, bf16[256,1536]{1,0:T(8,128)(2,1)} %refs_0_.6, bf16[256,1536]{1,0:T(8,128)(2,1)} %copy-done.139, ...), custom_call_target="tpu_custom_call" | custom-call | flops 3623878656 | bytes 20000000 | tf_op jit(solution)/shard_map/qkv/pallas_call | solution.py:142
  79.2 4.3 collective-permute-done.12
  88.8 13.9 %attend.1 = (bf16[1024,384]{1,0:T(8,128)(2,1)S(1)}, f32[3,8,1024]{2,1,0:T(8,128)S(1)}) custom-call(s32[1]{0:T(128)} %copy.176.length, bf16[1024,384]{1,0:T(8,128)(2,1)S(1)} %copy-done.20, bf16[1024,128]{1,0:T(8,128)(2,1)S(1)} %copy-done.25, bf16[1024,128]{1,0:T(8,128)(2,1)S(1)} %copy-done.27), custom_call_target="tpu_custom_call" | custom-call | tf_op jit(solution)/shard_map/attend/pallas_call | solution.py:273
  110.5 3.9 collective-permute-done.18
  114.4 13.7 %collective-permute-done.19 = bf16[264,1536]{1,0:T(8,128)(2,1)} collective-permute-done((bf16[264,1536]{1,0:T(8,128)(2,1)}, bf16[264,1536]{1,0:T(8,128)(2,1)}, u32[]{:S(2)}, u32[]{:S(2)}) %collective-permute-start.19) | collective-permute-done | bytes 811040 | tf_op jit(solution)/shard_map/ppermute | solution.py:871
  136.0 7.1 %round_weights.1 = (bf16[8,1536,256]{2,1,0:T(8,128)(2,1)S(1)}, bf16[8,128,1536]{2,1,0:T(8,128)(2,1)S(1)}) custom-call(s32[1]{0:T(128)} %bitcast.26.turn.first, f32[2,8,1536,128]{3,2,1,0:T(8,128)} %refs_0_.12, f32[8,128,1536]{2,1,0:T(8,128)S(1)} %copy-done), custom_call_target="tpu_custom_call" | custom-call | bytes 28000000 | tf_op jit(solution)/shard_map/round_weights/pallas_call | solution.py:736
  156.8 8.8 %seed_rows.4 = (bf16[8,1280,1536]{2,1,0:T(8,128)(2,1)}, f32[8,320,128]{2,1,0:T(8,128)S(1)}, f32[8,8,1024]{2,1,0:T(8,128)S(1)}) custom-call(s32[1]{0:T(128)} %bitcast.26.turn.first, bf16[4,264,1536]{2,1,0:T(8,128)(2,1)} %pad_maximum_fusion.own, bf16[4,264,1536]{2,1,0:T(8,128)(2,1)} %collective-permute-done.20.sib, bf16[8,128,1536]{2,1,0:T(8,128)(2,1)} %copy-done.4), custom_call_target="tpu_custom_call" | custom-call | flops 3019898880 | bytes 20000000 | tf_op jit(solution)/shard_map/seed_rows/pallas_call | solution.py:507
  165.6 7.1 %collective-permute-done.25 = bf16[256,1536]{1,0:T(8,128)(2,1)S(1)} collective-permute-done((bf16[256,1536]{1,0:T(8,128)(2,1)S(1)}, bf16[256,1536]{1,0:T(8,128)(2,1)S(1)}, u32[]{:S(2)}, u32[]{:S(2)}) %collective-permute-start.25) | collective-permute-done | bytes 786464 | tf_op jit(solution)/shard_map/ppermute | solution.py:888
  176.6 15.9 %collective-permute-done.29 = bf16[256,1536]{1,0:T(8,128)(2,1)S(1)} collective-permute-done((bf16[256,1536]{1,0:T(8,128)(2,1)S(1)}, bf16[256,1536]{1,0:T(8,128)(2,1)S(1)}, u32[]{:S(2)}, u32[]{:S(2)}) %collective-permute-start.29) | collective-permute-done | bytes 786464 | tf_op jit(solution)/shard_map/ppermute | solution.py:888
  199.0 20.6 %collective-permute-done.33 = bf16[256,1536]{1,0:T(8,128)(2,1)} collective-permute-done((bf16[256,1536]{1,0:T(8,128)(2,1)S(1)}, bf16[256,1536]{1,0:T(8,128)(2,1)}, u32[]{:S(2)}, u32[]{:S(2)}) %collective-permute-start.33) | collective-permute-done | bytes 786464 | tf_op jit(solution)/shard_map/ppermute | solution.py:888
  225.4 16.9 %expert_rows.4 = (bf16[8,1280,1536]{2,1,0:T(8,128)(2,1)}, bf16[8,1280,256]{2,1,0:T(8,128)(2,1)}, bf16[8,1280,128]{2,1,0:T(8,128)(2,1)}, bf16[4,264,1536]{2,1,0:T(8,128)(2,1)}, bf16[4,264,1536]{2,1,0:T(8,128)(2,1)}) custom-call(s32[1]{0:T(128)} %bitcast.26.turn.first, f32[8,8,1024]{2,1,0:T(8,128)} %copy-done.47, f32[8,320,128]{2,1,0:T(8,128)} %copy-done.46, ...), custom_call_target="tpu_custom_call" | custom-call | flops 8053063680 | bytes 30000000 | tf_op jit(solution)/shard_map/expert_rows/pallas_call | solution.py:639
  246.9 11.4 %collective-permute-start.41 = (bf16[256,1536]{1,0:T(8,128)(2,1)}, bf16[256,1536]{1,0:T(8,128)(2,1)}, u32[]{:S(2)}, u32[]{:S(2)}) collective-permute-start(bf16[256,1536]{1,0:T(8,128)(2,1)} %collective-permute-done.33), channel_id=1, source_target_pairs={{0,8},{4,12},{8,16},{12,20},{16,24},{20,28},{24,0},{28,4},{1,9},{5... | collective-permute-start | bytes 2359304 | tf_op jit(solution)/shard_map/ppermute | solution.py:888
  259.9 8.7 %seed_rows.5 = (bf16[8,1280,1536]{2,1,0:T(8,128)(2,1)}, f32[8,320,128]{2,1,0:T(8,128)S(1)}, f32[8,8,1024]{2,1,0:T(8,128)S(1)}) custom-call(s32[1]{0:T(128)} %bitcast.26.turn.first, bf16[4,264,1536]{2,1,0:T(8,128)(2,1)} %copy-done.53, bf16[4,264,1536]{2,1,0:T(8,128)(2,1)} %copy-done.71, ...), custom_call_target="tpu_custom_call", output_to_operand_aliasing={{0}: (4, {})} | custom-call | flops 3019898880 | bytes 20000000 | tf_op jit(solution)/shard_map/seed_rows/pallas_call | solution.py:507
  270.4 8.7 %seed_rows.6 = (bf16[8,1280,1536]{2,1,0:T(8,128)(2,1)}, f32[8,320,128]{2,1,0:T(8,128)S(1)}, f32[8,8,1024]{2,1,0:T(8,128)S(1)}) custom-call(s32[1]{0:T(128)} %bitcast.26.turn.first, bf16[4,264,1536]{2,1,0:T(8,128)(2,1)} %copy-done.55, bf16[4,264,1536]{2,1,0:T(8,128)(2,1)} %collective-permute-done.36.sib, ...), custom_call_target="tpu_custom_call", output_to_operand_aliasing={{0}: (4, {})} | custom-call | flops 3019898880 | bytes 20000000 | tf_op jit(solution)/shard_map/seed_rows/pallas_call | solution.py:507
  286.0 16.8 %expert_rows.5 = (bf16[8,1280,1536]{2,1,0:T(8,128)(2,1)}, bf16[8,1280,256]{2,1,0:T(8,128)(2,1)}, bf16[8,1280,128]{2,1,0:T(8,128)(2,1)}, bf16[4,264,1536]{2,1,0:T(8,128)(2,1)}, bf16[4,264,1536]{2,1,0:T(8,128)(2,1)}) custom-call(s32[1]{0:T(128)} %bitcast.26.turn.first, ...), custom_call_target="tpu_custom_call", output_to_operand_aliasing={{0}: (6, {}), {1}: (7, {}), {2}: (8, {})} | custom-call | flops 8053063680 | bytes 30000000 | tf_op jit(solution)/shard_map/expert_rows/pallas_call | solution.py:639
  302.9 5.0 fusion.10
  312.1 17.2 %expert_rows.6 = (bf16[8,1280,1536]{2,1,0:T(8,128)(2,1)}, bf16[8,1280,256]{2,1,0:T(8,128)(2,1)}, bf16[8,1280,128]{2,1,0:T(8,128)(2,1)}, bf16[4,264,1536]{2,1,0:T(8,128)(2,1)}, bf16[4,264,1536]{2,1,0:T(8,128)(2,1)}) custom-call(s32[1]{0:T(128)} %bitcast.26.turn.first, ...), custom_call_target="tpu_custom_call", output_to_operand_aliasing={{0}: (6, {}), {1}: (7, {}), {2}: (8, {})} | custom-call | flops 8053063680 | bytes 30000000 | tf_op jit(solution)/shard_map/expert_rows/pallas_call | solution.py:639
  329.3 5.2 fusion.14
  342.1 7.4 %mix_rows.4 = (bf16[4,256,1536]{2,1,0:T(8,128)(2,1)S(1)}, bf16[4,256,1536]{2,1,0:T(8,128)(2,1)}) custom-call(s32[1]{0:T(128)} %bitcast.26.turn.first, f32[8,8,1024]{2,1,0:T(8,128)S(1)} %copy-done.48, bf16[8,1280,128]{2,1,0:T(8,128)(2,1)S(1)} %copy-done.1, bf16[8,128,1536]{2,1,0:T(8,128)(2,1)S(1)} %copy-done.5), custom_call_target="tpu_custom_call" | custom-call | flops 3019898880 | bytes 20000000 | tf_op jit(solution)/shard_map/mix_rows/pallas_call | solution.py:710
  351.1 8.9 %seed_rows.7 = (bf16[8,1280,1536]{2,1,0:T(8,128)(2,1)}, f32[8,320,128]{2,1,0:T(8,128)S(1)}, f32[8,8,1024]{2,1,0:T(8,128)S(1)}) custom-call(s32[1]{0:T(128)} %bitcast.26.turn.first, bf16[4,264,1536]{2,1,0:T(8,128)(2,1)} %copy-done.54, bf16[4,264,1536]{2,1,0:T(8,128)(2,1)} %collective-permute-done.49.sib, ...), custom_call_target="tpu_custom_call", output_to_operand_aliasing={{0}: (4, {})} | custom-call | flops 3019898880 | bytes 20000000 | tf_op jit(solution)/shard_map/seed_rows/pallas_call | solution.py:507
  367.3 17.0 %expert_rows.7 = (bf16[8,1280,1536]{2,1,0:T(8,128)(2,1)}, bf16[8,1280,256]{2,1,0:T(8,128)(2,1)}, bf16[8,1280,128]{2,1,0:T(8,128)(2,1)}, bf16[4,264,1536]{2,1,0:T(8,128)(2,1)}, bf16[4,264,1536]{2,1,0:T(8,128)(2,1)}) custom-call(s32[1]{0:T(128)} %bitcast.26.turn.first, ...), custom_call_target="tpu_custom_call", output_to_operand_aliasing={{0}: (6, {}), {1}: (7, {}), {2}: (8, {})} | custom-call | flops 8053063680 | bytes 30000000 | tf_op jit(solution)/shard_map/expert_rows/pallas_call | solution.py:639
  384.3 4.2 fusion.26
  396.1 6.7 mix_rows.5
  404.7 6.0 collective-permute-done.64
  410.7 3.6 collective-permute-done.62
  418.4 7.6 %mix_rows.6 = (bf16[4,256,1536]{2,1,0:T(8,128)(2,1)S(1)}, bf16[4,256,1536]{2,1,0:T(8,128)(2,1)}) custom-call(s32[1]{0:T(128)} %bitcast.26.turn.first, f32[8,8,1024]{2,1,0:T(8,128)S(1)} %copy-done.37, bf16[8,1280,128]{2,1,0:T(8,128)(2,1)S(1)} %copy-done.2, bf16[8,128,1536]{2,1,0:T(8,128)(2,1)S(1)} %copy-done.6), custom_call_target="tpu_custom_call" | custom-call | flops 3019898880 | bytes 20000000 | tf_op jit(solution)/shard_map/mix_rows/pallas_call | solution.py:710
  428.7 8.7 %collective-permute-done.68 = bf16[256,1536]{1,0:T(8,128)(2,1)S(1)} collective-permute-done((bf16[256,1536]{1,0:T(8,128)(2,1)S(1)}, bf16[256,1536]{1,0:T(8,128)(2,1)S(1)}, u32[]{:S(2)}, u32[]{:S(2)}) %collective-permute-start.68) | collective-permute-done | bytes 786464 | tf_op jit(solution)/shard_map/ppermute | solution.py:871
  444.1 7.3 %mix_rows.7 = (bf16[4,256,1536]{2,1,0:T(8,128)(2,1)S(1)}, bf16[4,256,1536]{2,1,0:T(8,128)(2,1)}) custom-call(s32[1]{0:T(128)} %bitcast.26.turn.first, f32[8,8,1024]{2,1,0:T(8,128)S(1)} %copy-done.41, bf16[8,1280,128]{2,1,0:T(8,128)(2,1)S(1)} %copy-done.2, bf16[8,128,1536]{2,1,0:T(8,128)(2,1)S(1)} %copy-done.6), custom_call_target="tpu_custom_call" | custom-call | flops 3019898880 | bytes 20000000 | tf_op jit(solution)/shard_map/mix_rows/pallas_call | solution.py:710
  453.2 9.3 %weights_step.6 = (f32[2,8,1536,128]{3,2,1,0:T(8,128)}, f32[2,8,1536,128]{3,2,1,0:T(8,128)}, f32[2,8,1536,128]{3,2,1,0:T(8,128)}, f32[2,8,1536,128]{3,2,1,0:T(8,...) custom-call(s32[1]{0:T(128)} %bitcast.26.turn.first, ...), custom_call_target="tpu_custom_call" | custom-call | flops 1509949440 | bytes 26000000 | tf_op jit(solution)/shard_map/weights_step/pallas_call | solution.py:784
  462.5 4.2 fusion.34
  472.8 10.4 %weights_step.7 = (f32[2,8,1536,128]{3,2,1,0:T(8,128)}, f32[2,8,1536,128]{3,2,1,0:T(8,128)}, f32[2,8,1536,128]{3,2,1,0:T(8,128)}, f32[2,8,1536,128]{3,2,1,0:T(8,...) custom-call(s32[1]{0:T(128)} %get-tuple-element.995.turn, ...), custom_call_target="tpu_custom_call", output_to_operand_aliasing={{0}: (11, {}), {1}: (12, {}), {2}: (13, {}), {3}: (14, {}),... | custom-call | flops 1509949440 | bytes 26000000 | tf_op jit(solution)/shard_map/weights_step/pallas_call | solution.py:784
  483.2 4.1 fusion.38
  487.3 4.0 collective-permute-done.76
  499.2 18.4 %weights_step.8 = (f32[2,8,1536,128]{3,2,1,0:T(8,128)}, f32[2,8,1536,128]{3,2,1,0:T(8,128)}, f32[2,8,1536,128]{3,2,1,0:T(8,128)}, f32[2,8,1536,128]{3,2,1,0:T(8,...) custom-call(s32[1]{0:T(128)} %get-tuple-element.1049.turn, ...), custom_call_target="tpu_custom_call", output_to_operand_aliasing={{0}: (11, {}), {1}: (12, {}), {2}: (13, {}), {3}: (14, {}),... | custom-call | flops 3019898880 | bytes 52000000 | tf_op jit(solution)/shard_map/weights_step/pallas_call | solution.py:784
  525.7 4.4 heads_back.1
  544.1 17.8 %attend_back.1 = (bf16[1024,384]{1,0:T(8,128)(2,1)S(1)}, bf16[1024,128]{1,0:T(8,128)(2,1)S(1)}, bf16[1024,128]{1,0:T(8,128)(2,1)S(1)}) custom-call(s32[1]{0:T(128)} %copy.176.length, bf16[1024,384]{1,0:T(8,128)(2,1)S(1)} %copy-done.21, bf16[1024,128]{1,0:T(8,128)(2,1)S(1)} %copy-done.26, bf16[1024,128]{1,0:T(8,128)(2,1)S(1)} %copy-done.28, ...), custom_call_target="tpu_custom_call" | custom-call | tf_op jit(solution)/shard_map/attend_back/pallas_call | solution.py:374
  562.0 8.6 %collective-permute-done.82 = bf16[4,192,384]{2,1,0:T(8,128)(2,1)} collective-permute-done((bf16[4,192,384]{2,1,0:T(8,128)(2,1)}, bf16[4,192,384]{2,1,0:T(8,128)(2,1)}, u32[]{:S(2)}, u32[]{:S(2)}) %collective-permute-start.82) | collective-permute-done | bytes 589856 | tf_op jit(solution)/shard_map/ppermute | solution.py:871
  581.0 4.0 fusion.87
  600.1 18.4 %weights_step.9 = (f32[2,8,1536,128]{3,2,1,0:T(8,128)}, f32[2,8,1536,128]{3,2,1,0:T(8,128)}, f32[2,8,1536,128]{3,2,1,0:T(8,128)}, f32[2,8,1536,128]{3,2,1,0:T(8,...) custom-call(s32[1]{0:T(128)} %get-tuple-element.1148.turn, ...), custom_call_target="tpu_custom_call", output_to_operand_aliasing={{0}: (11, {}), {1}: (12, {}), {2}: (13, {}), {3}: (14, {}),... | custom-call | flops 3019898880 | bytes 52000000 | tf_op jit(solution)/shard_map/weights_step/pallas_call | solution.py:784
  633.8 9.8 %weights_step.10 = (f32[2,8,1536,128]{3,2,1,0:T(8,128)}, f32[2,8,1536,128]{3,2,1,0:T(8,128)}, f32[2,8,1536,128]{3,2,1,0:T(8,128)}, f32[2,8,1536,128]{3,2,1,0:T(8...) custom-call(s32[1]{0:T(128)} %get-tuple-element.1174.turn, ...), custom_call_target="tpu_custom_call", output_to_operand_aliasing={{0}: (11, {}), {1}: (12, {}), {2}: (13, {}), {3}: (14, {}),... | custom-call | flops 1509949440 | bytes 26000000 | tf_op jit(solution)/shard_map/weights_step/pallas_call | solution.py:784
  643.6 8.0 %collective-permute-done.96 = bf16[200,640]{1,0:T(8,128)(2,1)S(1)} collective-permute-done((bf16[200,640]{1,0:T(8,128)(2,1)S(1)}, bf16[200,640]{1,0:T(8,128)(2,1)S(1)}, u32[]{:S(2)}, u32[]{:S(2)}) %collective-permute-start.96) | collective-permute-done | bytes 256032 | tf_op jit(solution)/shard_map/ppermute | solution.py:888
  663.1 10.1 %weights_step.11 = (f32[2,8,1536,128]{3,2,1,0:T(8,128)}, f32[2,8,1536,128]{3,2,1,0:T(8,128)}, f32[2,8,1536,128]{3,2,1,0:T(8,128)}, f32[2,8,1536,128]{3,2,1,0:T(8...) custom-call(s32[1]{0:T(128)} %get-tuple-element.1216.turn, ...), custom_call_target="tpu_custom_call", output_to_operand_aliasing={{0}: (11, {}), {1}: (12, {}), {2}: (13, {}), {3}: (14, {}),... | custom-call | flops 1509949440 | bytes 26000000 | tf_op jit(solution)/shard_map/weights_step/pallas_call | solution.py:784
  675.7 5.3 collective-permute-done.102
  (587 shorter events, 238.5 us)
Async XLA Ops:
  9.2 26.6 %collective-permute-start.5 = (bf16[256,1536]{1,0:T(8,128)(2,1)}, bf16[256,1536]{1,0:T(8,128)(2,1)}, u32[]{:S(2)}, u32[]{:S(2)}) collective-permute-start(bf16[256,1536]{1,0:T(8,128)(2,1)} %refs_0_.6), channel_id=1, source_target_pairs={{0,2},{1,3},{2,0},{3,1},{4,6},{5,7},{6,4},{7,5},{8,10},{9,11},{10,... | collective-permute-start | bytes 2359304 | tf_op jit(solution)/shard_map/ppermute | solution.py:871
  128.1 22.1 %collective-permute-start.23 = (bf16[264,1536]{1,0:T(8,128)(2,1)}, bf16[264,1536]{1,0:T(8,128)(2,1)S(1)}, u32[]{:S(2)}, u32[]{:S(2)}) collective-permute-start(bf16[264,1536]{1,0:T(8,128)(2,1)} %collective-permute-done.19), channel_id=1, source_target_pairs={{0,8},{4,12},{8,16},{12,20},{16,24},{20,28},{24,0},{28,4},{1,9},{5... | collective-permute-start | bytes 2433032 | tf_op jit(solution)/shard_map/ppermute | solution.py:888
  128.4 21.9 %collective-permute-start.24 = (bf16[264,1536]{1,0:T(8,128)(2,1)}, bf16[264,1536]{1,0:T(8,128)(2,1)S(1)}, u32[]{:S(2)}, u32[]{:S(2)}) collective-permute-start(bf16[264,1536]{1,0:T(8,128)(2,1)} %collective-permute-done.16), channel_id=1, source_target_pairs={{0,4},{4,0},{8,12},{12,8},{16,20},{20,16},{24,28},{28,24},{1,5},{5... | collective-permute-start | bytes 2433032 | tf_op jit(solution)/shard_map/ppermute | solution.py:871
  194.4 25.2 %collective-permute-start.32 = (bf16[4,264,1536]{2,1,0:T(8,128)(2,1)S(1)}, bf16[4,264,1536]{2,1,0:T(8,128)(2,1)S(1)}, u32[]{:S(2)}, u32[]{:S(2)}) collective-permute-start(bf16[4,264,1536]{2,1,0:T(8,128)(2,1)S(1)} %pad_maximum_fusion.1.own), channel_id=1, source_target_pairs={{0,1},{1,0},{2,3},{3,2},{4,5},{5,4},{6,7},{7,6},{8,9},{9,8},{10,11... | collective-permute-start | bytes 9732104 | tf_op jit(solution)/shard_map/ppermute | solution.py:871
  196.6 23.0 %collective-permute-start.35 = (bf16[4,256,1536]{2,1,0:T(8,128)(2,1)S(1)}, bf16[4,256,1536]{2,1,0:T(8,128)(2,1)S(1)}, u32[]{:S(2)}, u32[]{:S(2)}) collective-permute-start(bf16[4,256,1536]{2,1,0:T(8,128)(2,1)S(1)} %pad_maximum_fusion.4.own_in), channel_id=1, source_target_pairs={{0,1},{1,0},{2,3},{3,2},{4,5},{5,4},{6,7},{7,6},{8,9},{9,8},{10,11... | collective-permute-start | bytes 9437192 | tf_op jit(solution)/shard_map/ppermute | solution.py:871
  196.9 22.7 %collective-permute-start.31 = (bf16[264,1536]{1,0:T(8,128)(2,1)S(1)}, bf16[264,1536]{1,0:T(8,128)(2,1)S(1)}, u32[]{:S(2)}, u32[]{:S(2)}) collective-permute-start(bf16[264,1536]{1,0:T(8,128)(2,1)S(1)} %copy-done.89), channel_id=1, source_target_pairs={{0,4},{4,0},{8,12},{12,8},{16,20},{20,16},{24,28},{28,24},{1,5},{5... | collective-permute-start | bytes 2433032 | tf_op jit(solution)/shard_map/ppermute | solution.py:871
  222.0 22.1 %collective-permute-start.36 = (bf16[4,264,1536]{2,1,0:T(8,128)(2,1)S(1)}, bf16[4,264,1536]{2,1,0:T(8,128)(2,1)}, u32[]{:S(2)}, u32[]{:S(2)}) collective-permute-start(bf16[4,264,1536]{2,1,0:T(8,128)(2,1)S(1)} %pad_maximum_fusion.2.own), channel_id=1, source_target_pairs={{0,1},{1,0},{2,3},{3,2},{4,5},{5,4},{6,7},{7,6},{8,9},{9,8},{10,11... | collective-permute-start | bytes 9732104 | tf_op jit(solution)/shard_map/ppermute | solution.py:871
  246.1 33.9 %collective-permute-start.43 = (bf16[4,256,1536]{2,1,0:T(8,128)(2,1)S(1)}, bf16[4,256,1536]{2,1,0:T(8,128)(2,1)S(1)}, u32[]{:S(2)}, u32[]{:S(2)}) collective-permute-start(bf16[4,256,1536]{2,1,0:T(8,128)(2,1)S(1)} %pad_maximum_fusion.5.own_in), channel_id=1, source_target_pairs={{0,1},{1,0},{2,3},{3,2},{4,5},{5,4},{6,7},{7,6},{8,9},{9,8},{10,11... | collective-permute-start | bytes 9437192 | tf_op jit(solution)/shard_map/ppermute | solution.py:871
  246.2 33.8 %collective-permute-start.40 = (bf16[264,1536]{1,0:T(8,128)(2,1)S(1)}, bf16[264,1536]{1,0:T(8,128)(2,1)S(1)}, u32[]{:S(2)}, u32[]{:S(2)}) collective-permute-start(bf16[264,1536]{1,0:T(8,128)(2,1)S(1)} %collective-permute-done.31), channel_id=1, source_target_pairs={{0,2},{1,3},{2,0},{3,1},{4,6},{5,7},{6,4},{7,5},{8,10},{9,11},{10,... | collective-permute-start | bytes 2433032 | tf_op jit(solution)/shard_map/ppermute | solution.py:871
  246.9 33.1 %collective-permute-start.41 = (bf16[256,1536]{1,0:T(8,128)(2,1)}, bf16[256,1536]{1,0:T(8,128)(2,1)}, u32[]{:S(2)}, u32[]{:S(2)}) collective-permute-start(bf16[256,1536]{1,0:T(8,128)(2,1)} %collective-permute-done.33), channel_id=1, source_target_pairs={{0,8},{4,12},{8,16},{12,20},{16,24},{20,28},{24,0},{28,4},{1,9},{5... | collective-permute-start | bytes 2359304 | tf_op jit(solution)/shard_map/ppermute | solution.py:888
  258.3 21.7 %collective-permute-start.42 = (bf16[256,1536]{1,0:T(8,128)(2,1)}, bf16[256,1536]{1,0:T(8,128)(2,1)S(1)}, u32[]{:S(2)}, u32[]{:S(2)}) collective-permute-start(bf16[256,1536]{1,0:T(8,128)(2,1)} %collective-permute-done.38), channel_id=1, source_target_pairs={{0,4},{4,0},{8,12},{12,8},{16,20},{20,16},{24,28},{28,24},{1,5},{5... | collective-permute-start | bytes 2359304 | tf_op jit(solution)/shard_map/ppermute | solution.py:871
  280.0 22.8 %collective-permute-start.48 = (bf16[4,264,1536]{2,1,0:T(8,128)(2,1)}, bf16[4,264,1536]{2,1,0:T(8,128)(2,1)}, u32[]{:S(2)}, u32[]{:S(2)}) collective-permute-start(bf16[4,264,1536]{2,1,0:T(8,128)(2,1)} %get-tuple-element.839), channel_id=1, source_target_pairs={{0,1},{1,0},{2,3},{3,2},{4,5},{5,4},{6,7},{7,6},{8,9},{9,8},{10,11... | collective-permute-start | bytes 9732104 | tf_op jit(solution)/shard_map/ppermute | solution.py:871
  283.3 24.6 %collective-permute-start.47 = (bf16[4,256,1536]{2,1,0:T(8,128)(2,1)S(1)}, bf16[4,256,1536]{2,1,0:T(8,128)(2,1)}, u32[]{:S(2)}, u32[]{:S(2)}) collective-permute-start(bf16[4,256,1536]{2,1,0:T(8,128)(2,1)S(1)} %pad_maximum_fusion.6.own_in), channel_id=1, source_target_pairs={{0,1},{1,0},{2,3},{3,2},{4,5},{5,4},{6,7},{7,6},{8,9},{9,8},{10,11... | collective-permute-start | bytes 9437192 | tf_op jit(solution)/shard_map/ppermute | solution.py:871
  283.4 24.5 %collective-permute-start.45 = (bf16[256,1536]{1,0:T(8,128)(2,1)}, bf16[256,1536]{1,0:T(8,128)(2,1)}, u32[]{:S(2)}, u32[]{:S(2)}) collective-permute-start(bf16[256,1536]{1,0:T(8,128)(2,1)} %collective-permute-done.41), channel_id=1, source_target_pairs={{0,2},{1,3},{2,0},{3,1},{4,6},{5,7},{6,4},{7,5},{8,10},{9,11},{10,... | collective-permute-start | bytes 2359304 | tf_op jit(solution)/shard_map/ppermute | solution.py:871
  284.9 23.0 %collective-permute-start.46 = (bf16[256,1536]{1,0:T(8,128)(2,1)}, bf16[256,1536]{1,0:T(8,128)(2,1)}, u32[]{:S(2)}, u32[]{:S(2)}) collective-permute-start(bf16[256,1536]{1,0:T(8,128)(2,1)} %collective-permute-done.41), channel_id=1, source_target_pairs={{0,4},{4,0},{8,12},{12,8},{16,20},{20,16},{24,28},{28,24},{1,5},{5... | collective-permute-start | bytes 2359304 | tf_op jit(solution)/shard_map/ppermute | solution.py:871
  285.5 22.4 %collective-permute-start.44 = (bf16[264,1536]{1,0:T(8,128)(2,1)}, bf16[264,1536]{1,0:T(8,128)(2,1)}, u32[]{:S(2)}, u32[]{:S(2)}) collective-permute-start(bf16[264,1536]{1,0:T(8,128)(2,1)} %collective-permute-done.16), channel_id=1, source_target_pairs={{0,8},{4,12},{8,16},{12,20},{16,24},{20,28},{24,0},{28,4},{1,9},{5... | collective-permute-start | bytes 2433032 | tf_op jit(solution)/shard_map/ppermute | solution.py:888
  309.5 25.0 %collective-permute-start.49 = (bf16[4,264,1536]{2,1,0:T(8,128)(2,1)S(1)}, bf16[4,264,1536]{2,1,0:T(8,128)(2,1)}, u32[]{:S(2)}, u32[]{:S(2)}) collective-permute-start(bf16[4,264,1536]{2,1,0:T(8,128)(2,1)S(1)} %pad_maximum_fusion.3.own), channel_id=1, source_target_pairs={{0,1},{1,0},{2,3},{3,2},{4,5},{5,4},{6,7},{7,6},{8,9},{9,8},{10,11... | collective-permute-start | bytes 9732104 | tf_op jit(solution)/shard_map/ppermute | solution.py:871
  310.0 24.5 %collective-permute-start.52 = (bf16[264,1536]{1,0:T(8,128)(2,1)}, bf16[264,1536]{1,0:T(8,128)(2,1)}, u32[]{:S(2)}, u32[]{:S(2)}) collective-permute-start(bf16[264,1536]{1,0:T(8,128)(2,1)} %get-tuple-element.863), channel_id=1, source_target_pairs={{0,4},{4,0},{8,12},{12,8},{16,20},{20,16},{24,28},{28,24},{1,5},{5... | collective-permute-start | bytes 2433032 | tf_op jit(solution)/shard_map/ppermute | solution.py:871
  311.5 23.0 %collective-permute-start.50 = (bf16[256,1536]{1,0:T(8,128)(2,1)}, bf16[256,1536]{1,0:T(8,128)(2,1)}, u32[]{:S(2)}, u32[]{:S(2)}) collective-permute-start(bf16[256,1536]{1,0:T(8,128)(2,1)} %collective-permute-done.46), channel_id=1, source_target_pairs={{0,2},{1,3},{2,0},{3,1},{4,6},{5,7},{6,4},{7,5},{8,10},{9,11},{10,... | collective-permute-start | bytes 2359304 | tf_op jit(solution)/shard_map/ppermute | solution.py:871
  334.5 25.6 %collective-permute-start.54 = (bf16[4,264,1536]{2,1,0:T(8,128)(2,1)}, bf16[4,264,1536]{2,1,0:T(8,128)(2,1)S(1)}, u32[]{:S(2)}, u32[]{:S(2)}) collective-permute-start(bf16[4,264,1536]{2,1,0:T(8,128)(2,1)} %get-tuple-element.888), channel_id=1, source_target_pairs={{0,1},{1,0},{2,3},{3,2},{4,5},{5,4},{6,7},{7,6},{8,9},{9,8},{10,11... | collective-permute-start | bytes 9732104 | tf_op jit(solution)/shard_map/ppermute | solution.py:871
  336.8 25.7 %collective-permute-start.53 = (bf16[4,256,1536]{2,1,0:T(8,128)(2,1)S(1)}, bf16[4,256,1536]{2,1,0:T(8,128)(2,1)}, u32[]{:S(2)}, u32[]{:S(2)}) collective-permute-start(bf16[4,256,1536]{2,1,0:T(8,128)(2,1)S(1)} %pad_maximum_fusion.7.own_in), channel_id=1, source_target_pairs={{0,1},{1,0},{2,3},{3,2},{4,5},{5,4},{6,7},{7,6},{8,9},{9,8},{10,11... | collective-permute-start | bytes 9437192 | tf_op jit(solution)/shard_map/ppermute | solution.py:871
  337.4 25.1 %collective-permute-start.55 = (bf16[264,1536]{1,0:T(8,128)(2,1)}, bf16[264,1536]{1,0:T(8,128)(2,1)S(1)}, u32[]{:S(2)}, u32[]{:S(2)}) collective-permute-start(bf16[264,1536]{1,0:T(8,128)(2,1)} %get-tuple-element.886), channel_id=1, source_target_pairs={{0,2},{1,3},{2,0},{3,1},{4,6},{5,7},{6,4},{7,5},{8,10},{9,11},{10,... | collective-permute-start | bytes 2433032 | tf_op jit(solution)/shard_map/ppermute | solution.py:871
  338.8 23.7 %collective-permute-start.56 = (bf16[264,1536]{1,0:T(8,128)(2,1)}, bf16[264,1536]{1,0:T(8,128)(2,1)S(1)}, u32[]{:S(2)}, u32[]{:S(2)}) collective-permute-start(bf16[264,1536]{1,0:T(8,128)(2,1)} %get-tuple-element.884), channel_id=1, source_target_pairs={{0,24},{4,28},{8,0},{12,4},{16,8},{20,12},{24,16},{28,20},{1,25},{... | collective-permute-start | bytes 2433032 | tf_op jit(solution)/shard_map/ppermute | solution.py:888
  362.5 21.7 %collective-permute-start.60 = (bf16[4,256,1536]{2,1,0:T(8,128)(2,1)}, bf16[4,256,1536]{2,1,0:T(8,128)(2,1)}, u32[]{:S(2)}, u32[]{:S(2)}) collective-permute-start(bf16[4,256,1536]{2,1,0:T(8,128)(2,1)} %get-tuple-element.918), channel_id=1, source_target_pairs={{0,1},{1,0},{2,3},{3,2},{4,5},{5,4},{6,7},{7,6},{8,9},{9,8},{10,11... | collective-permute-start | bytes 9437192 | tf_op jit(solution)/shard_map/ppermute | solution.py:871
  365.2 23.4 %collective-permute-start.58 = (bf16[264,1536]{1,0:T(8,128)(2,1)}, bf16[264,1536]{1,0:T(8,128)(2,1)}, u32[]{:S(2)}, u32[]{:S(2)}) collective-permute-start(bf16[264,1536]{1,0:T(8,128)(2,1)} %add_convert_fusion.11), channel_id=1, source_target_pairs={{0,2},{1,3},{2,0},{3,1},{4,6},{5,7},{6,4},{7,5},{8,10},{9,11},{10,... | collective-permute-start | bytes 2433032 | tf_op jit(solution)/shard_map/ppermute | solution.py:871
  365.8 22.7 %collective-permute-start.57 = (bf16[264,1536]{1,0:T(8,128)(2,1)}, bf16[264,1536]{1,0:T(8,128)(2,1)}, u32[]{:S(2)}, u32[]{:S(2)}) collective-permute-start(bf16[264,1536]{1,0:T(8,128)(2,1)} %get-tuple-element.913), channel_id=1, source_target_pairs={{0,4},{4,0},{8,12},{12,8},{16,20},{20,16},{24,28},{28,24},{1,5},{5... | collective-permute-start | bytes 2433032 | tf_op jit(solution)/shard_map/ppermute | solution.py:871
  367.3 21.8 %collective-permute-start.59 = (bf16[264,1536]{1,0:T(8,128)(2,1)}, bf16[264,1536]{1,0:T(8,128)(2,1)}, u32[]{:S(2)}, u32[]{:S(2)}) collective-permute-start(bf16[264,1536]{1,0:T(8,128)(2,1)} %get-tuple-element.908), channel_id=1, source_target_pairs={{0,8},{4,12},{8,16},{12,20},{16,24},{20,28},{24,0},{28,4},{1,9},{5... | collective-permute-start | bytes 2433032 | tf_op jit(solution)/shard_map/ppermute | solution.py:888
  416.3 22.3 %collective-permute-start.66 = (bf16[264,1536]{1,0:T(8,128)(2,1)S(1)}, bf16[264,1536]{1,0:T(8,128)(2,1)S(1)}, u32[]{:S(2)}, u32[]{:S(2)}) collective-permute-start(bf16[264,1536]{1,0:T(8,128)(2,1)S(1)} %add_convert_fusion.4), channel_id=1, source_target_pairs={{0,8},{4,12},{8,16},{12,20},{16,24},{20,28},{24,0},{28,4},{1,9},{5... | collective-permute-start | bytes 2433032 | tf_op jit(solution)/shard_map/ppermute | solution.py:888
  416.3 22.2 %collective-permute-start.65 = (bf16[264,1536]{1,0:T(8,128)(2,1)S(1)}, bf16[264,1536]{1,0:T(8,128)(2,1)S(1)}, u32[]{:S(2)}, u32[]{:S(2)}) collective-permute-start(bf16[264,1536]{1,0:T(8,128)(2,1)S(1)} %get-tuple-element.953), channel_id=1, source_target_pairs={{0,2},{1,3},{2,0},{3,1},{4,6},{5,7},{6,4},{7,5},{8,10},{9,11},{10,... | collective-permute-start | bytes 2433032 | tf_op jit(solution)/shard_map/ppermute | solution.py:871
  439.4 23.0 %collective-permute-start.71 = (bf16[4,256,1536]{2,1,0:T(8,128)(2,1)}, bf16[4,256,1536]{2,1,0:T(8,128)(2,1)}, u32[]{:S(2)}, u32[]{:S(2)}) collective-permute-start(bf16[4,256,1536]{2,1,0:T(8,128)(2,1)} %get-tuple-element.993), channel_id=1, source_target_pairs={{0,1},{1,0},{2,3},{3,2},{4,5},{5,4},{6,7},{7,6},{8,9},{9,8},{10,11... | collective-permute-start | bytes 9437192 | tf_op jit(solution)/shard_map/ppermute | solution.py:871
  439.6 27.0 %collective-permute-start.70 = (bf16[264,1536]{1,0:T(8,128)(2,1)S(1)}, bf16[264,1536]{1,0:T(8,128)(2,1)}, u32[]{:S(2)}, u32[]{:S(2)}) collective-permute-start(bf16[264,1536]{1,0:T(8,128)(2,1)S(1)} %add_convert_fusion.3), channel_id=1, source_target_pairs={{0,4},{4,0},{8,12},{12,8},{16,20},{20,16},{24,28},{28,24},{1,5},{5... | collective-permute-start | bytes 2433032 | tf_op jit(solution)/shard_map/ppermute | solution.py:871
  441.1 25.6 %collective-permute-start.69 = (bf16[264,1536]{1,0:T(8,128)(2,1)}, bf16[264,1536]{1,0:T(8,128)(2,1)}, u32[]{:S(2)}, u32[]{:S(2)}) collective-permute-start(bf16[264,1536]{1,0:T(8,128)(2,1)} %get-tuple-element.977), channel_id=1, source_target_pairs={{0,2},{1,3},{2,0},{3,1},{4,6},{5,7},{6,4},{7,5},{8,10},{9,11},{10,... | collective-permute-start | bytes 2433032 | tf_op jit(solution)/shard_map/ppermute | solution.py:871
  441.7 25.0 %collective-permute-start.72 = (bf16[256,1536]{1,0:T(8,128)(2,1)}, bf16[256,1536]{1,0:T(8,128)(2,1)}, u32[]{:S(2)}, u32[]{:S(2)}) collective-permute-start(bf16[256,1536]{1,0:T(8,128)(2,1)} %get-tuple-element.989), channel_id=1, source_target_pairs={{0,24},{4,28},{8,0},{12,4},{16,8},{20,12},{24,16},{28,20},{1,25},{... | collective-permute-start | bytes 2359304 | tf_op jit(solution)/shard_map/ppermute | solution.py:888
  469.5 22.4 %collective-permute-start.74 = (bf16[264,1536]{1,0:T(8,128)(2,1)}, bf16[264,1536]{1,0:T(8,128)(2,1)S(1)}, u32[]{:S(2)}, u32[]{:S(2)}) collective-permute-start(bf16[264,1536]{1,0:T(8,128)(2,1)} %add_convert_fusion.1), channel_id=1, source_target_pairs={{0,8},{4,12},{8,16},{12,20},{16,24},{20,28},{24,0},{28,4},{1,9},{5... | collective-permute-start | bytes 2433032 | tf_op jit(solution)/shard_map/ppermute | solution.py:888
  499.2 21.6 %collective-permute-start.80 = (bf16[256,1536]{1,0:T(8,128)(2,1)S(1)}, bf16[256,1536]{1,0:T(8,128)(2,1)}, u32[]{:S(2)}, u32[]{:S(2)}) collective-permute-start(bf16[256,1536]{1,0:T(8,128)(2,1)S(1)} %copy-done.107), channel_id=1, source_target_pairs={{0,8},{4,12},{8,16},{12,20},{16,24},{20,28},{24,0},{28,4},{1,9},{5... | collective-permute-start | bytes 2359304 | tf_op jit(solution)/shard_map/ppermute | solution.py:888
  533.1 37.6 %collective-permute-start.86 = (bf16[256,1536]{1,0:T(8,128)(2,1)}, bf16[256,1536]{1,0:T(8,128)(2,1)}, u32[]{:S(2)}, u32[]{:S(2)}) collective-permute-start(bf16[256,1536]{1,0:T(8,128)(2,1)} %add_convert_fusion.32), channel_id=1, source_target_pairs={{0,24},{4,28},{8,0},{12,4},{16,8},{20,12},{24,16},{28,20},{1,25},{... | collective-permute-start | bytes 2359304 | tf_op jit(solution)/shard_map/ppermute | solution.py:888
  536.9 33.7 %collective-permute-start.84 = (bf16[256,1536]{1,0:T(8,128)(2,1)}, bf16[256,1536]{1,0:T(8,128)(2,1)}, u32[]{:S(2)}, u32[]{:S(2)}) collective-permute-start(bf16[256,1536]{1,0:T(8,128)(2,1)} %add_convert_fusion.33), channel_id=1, source_target_pairs={{0,2},{1,3},{2,0},{3,1},{4,6},{5,7},{6,4},{7,5},{8,10},{9,11},{10,... | collective-permute-start | bytes 2359304 | tf_op jit(solution)/shard_map/ppermute | solution.py:871
  537.7 35.7 %collective-permute-start.83 = (bf16[256,1536]{1,0:T(8,128)(2,1)}, bf16[256,1536]{1,0:T(8,128)(2,1)}, u32[]{:S(2)}, u32[]{:S(2)}) collective-permute-start(bf16[256,1536]{1,0:T(8,128)(2,1)} %get-tuple-element.1111), channel_id=1, source_target_pairs={{0,2},{1,3},{2,0},{3,1},{4,6},{5,7},{6,4},{7,5},{8,10},{9,11},{10,... | collective-permute-start | bytes 2359304 | tf_op jit(solution)/shard_map/ppermute | solution.py:871
  539.0 34.4 %collective-permute-start.85 = (bf16[256,1536]{1,0:T(8,128)(2,1)}, bf16[256,1536]{1,0:T(8,128)(2,1)}, u32[]{:S(2)}, u32[]{:S(2)}) collective-permute-start(bf16[256,1536]{1,0:T(8,128)(2,1)} %get-tuple-element.1107), channel_id=1, source_target_pairs={{0,4},{4,0},{8,12},{12,8},{16,20},{20,16},{24,28},{28,24},{1,5},{5... | collective-permute-start | bytes 2359304 | tf_op jit(solution)/shard_map/ppermute | solution.py:871
  541.7 29.0 %collective-permute-start.82 = (bf16[4,192,384]{2,1,0:T(8,128)(2,1)}, bf16[4,192,384]{2,1,0:T(8,128)(2,1)}, u32[]{:S(2)}, u32[]{:S(2)}) collective-permute-start(bf16[4,192,384]{2,1,0:T(8,128)(2,1)} %pad_maximum_fusion.11), channel_id=1, source_target_pairs={{0,4},{4,0},{8,12},{12,8},{16,20},{20,16},{24,28},{28,24},{1,5},{5... | collective-permute-start | bytes 1769480 | tf_op jit(solution)/shard_map/ppermute | solution.py:871
  592.9 27.9 %collective-permute-start.94 = (bf16[256,1536]{1,0:T(8,128)(2,1)}, bf16[256,1536]{1,0:T(8,128)(2,1)}, u32[]{:S(2)}, u32[]{:S(2)}) collective-permute-start(bf16[256,1536]{1,0:T(8,128)(2,1)} %add_convert_fusion.30), channel_id=1, source_target_pairs={{0,8},{4,12},{8,16},{12,20},{16,24},{20,28},{24,0},{28,4},{1,9},{5... | collective-permute-start | bytes 2359304 | tf_op jit(solution)/shard_map/ppermute | solution.py:888
  594.5 26.3 %collective-permute-start.93 = (bf16[4,200,640]{2,1,0:T(8,128)(2,1)}, bf16[4,200,640]{2,1,0:T(8,128)(2,1)}, u32[]{:S(2)}, u32[]{:S(2)}) collective-permute-start(bf16[4,200,640]{2,1,0:T(8,128)(2,1)} %pad_maximum_fusion.9), channel_id=1, source_target_pairs={{0,4},{4,0},{8,12},{12,8},{16,20},{20,16},{24,28},{28,24},{1,5},{5... | collective-permute-start | bytes 3072008 | tf_op jit(solution)/shard_map/ppermute | solution.py:871
  598.2 22.6 %collective-permute-start.91 = (bf16[256,1536]{1,0:T(8,128)(2,1)}, bf16[256,1536]{1,0:T(8,128)(2,1)S(1)}, u32[]{:S(2)}, u32[]{:S(2)}) collective-permute-start(bf16[256,1536]{1,0:T(8,128)(2,1)} %add_convert_fusion.31), channel_id=1, source_target_pairs={{0,2},{1,3},{2,0},{3,1},{4,6},{5,7},{6,4},{7,5},{8,10},{9,11},{10,... | collective-permute-start | bytes 2359304 | tf_op jit(solution)/shard_map/ppermute | solution.py:871
  598.8 22.1 %collective-permute-start.92 = (bf16[256,1536]{1,0:T(8,128)(2,1)S(1)}, bf16[256,1536]{1,0:T(8,128)(2,1)S(1)}, u32[]{:S(2)}, u32[]{:S(2)}) collective-permute-start(bf16[256,1536]{1,0:T(8,128)(2,1)S(1)} %get-tuple-element.1145), channel_id=1, source_target_pairs={{0,1},{1,0},{2,3},{3,2},{4,5},{5,4},{6,7},{7,6},{8,9},{9,8},{10,11... | collective-permute-start | bytes 2359304 | tf_op jit(solution)/shard_map/ppermute | solution.py:871
  623.1 28.5 %collective-permute-start.99 = (bf16[256,1536]{1,0:T(8,128)(2,1)}, bf16[256,1536]{1,0:T(8,128)(2,1)}, u32[]{:S(2)}, u32[]{:S(2)}) collective-permute-start(bf16[256,1536]{1,0:T(8,128)(2,1)} %add_convert_fusion.29), channel_id=1, source_target_pairs={{0,4},{4,0},{8,12},{12,8},{16,20},{20,16},{24,28},{28,24},{1,5},{5... | collective-permute-start | bytes 2359304 | tf_op jit(solution)/shard_map/ppermute | solution.py:871
  628.4 23.1 %collective-permute-start.96 = (bf16[200,640]{1,0:T(8,128)(2,1)S(1)}, bf16[200,640]{1,0:T(8,128)(2,1)S(1)}, u32[]{:S(2)}, u32[]{:S(2)}) collective-permute-start(bf16[200,640]{1,0:T(8,128)(2,1)S(1)} %get-tuple-element.1310), channel_id=1, source_target_pairs={{0,16},{4,20},{8,24},{12,28},{16,0},{20,4},{24,8},{28,12},{1,17},{... | collective-permute-start | bytes 768008 | tf_op jit(solution)/shard_map/ppermute | solution.py:888
  628.6 22.9 %collective-permute-start.97 = (bf16[200,640]{1,0:T(8,128)(2,1)S(1)}, bf16[200,640]{1,0:T(8,128)(2,1)S(1)}, u32[]{:S(2)}, u32[]{:S(2)}) collective-permute-start(bf16[200,640]{1,0:T(8,128)(2,1)S(1)} %get-tuple-element.1309), channel_id=1, source_target_pairs={{0,8},{4,12},{8,16},{12,20},{16,24},{20,28},{24,0},{28,4},{1,9},{5... | collective-permute-start | bytes 768008 | tf_op jit(solution)/shard_map/ppermute | solution.py:888
  630.0 21.6 %collective-permute-start.98 = (bf16[256,1536]{1,0:T(8,128)(2,1)S(1)}, bf16[256,1536]{1,0:T(8,128)(2,1)S(1)}, u32[]{:S(2)}, u32[]{:S(2)}) collective-permute-start(bf16[256,1536]{1,0:T(8,128)(2,1)S(1)} %copy-done.106), channel_id=1, source_target_pairs={{0,2},{1,3},{2,0},{3,1},{4,6},{5,7},{6,4},{7,5},{8,10},{9,11},{10,... | collective-permute-start | bytes 2359304 | tf_op jit(solution)/shard_map/ppermute | solution.py:871
  (203 other events, 2137.1 us)

commit v4 on v3

--- a/solution.py
+++ b/solution.py
@@ -483,7 +483,7 @@
         gather_pair(i, buf, hots, s_scr, local, cap)
         return 0
 
-    lax.fori_loop(0, NB // 2, gather, 0, unroll=2)
+    lax.fori_loop(0, NB // 2, gather, 0)
     rows = NB * cap
     keep = pltpu.make_async_copy(s_scr, s_out.at[:, pl.ds(plane * rows, rows), :], sem.at[NB + 3])
     keep.start()
@@ -493,7 +493,7 @@
         u_out[e] = mm(s_scr[e], d_scr[e], NT)
         return 0
 
-    lax.fori_loop(0, local, expert, 0, unroll=4 if local % 4 == 0 else 1)
+    lax.fori_loop(0, local, expert, 0)
     keep.wait()
 
 
@@ -561,7 +561,7 @@
         gather_pair(i, buf, hots, x_scr, local, cap)
         return 0
 
-    lax.fori_loop(0, NB // 2, gather, 0, unroll=2)
+    lax.fori_loop(0, NB // 2, gather, 0)
     here = pl.ds(plane * rows, rows)
     keep_x = pltpu.make_async_copy(x_scr, x_out.at[:, here, :], sem.at[NB + 3])
     keep_x.start()
@@ -689,7 +689,7 @@
         y_scr[e] = mm(a_scr[e], down[e])
         return 0
 
-    lax.fori_loop(0, local, expert, 0, unroll=4 if local % 4 == 0 else 1)
+    lax.fori_loop(0, local, expert, 0, unroll=2 if local % 2 == 0 else 1)
     for half, out in ((1, sib), (0, own)):
 
         def combine(i, _):

time: 688 us -> 683 us (level)
  starting transfers between devices: 97.8 us -> 86.8 us
    ppermute x29, starting transfers between devices: 37.8 us -> 26.7 us  [onward(): return lax.ppermute(v, 'dp', [(i, (i + 2 * planes) % n) for i in range(n)])]
  transfers between devices with their start and end apart: 105 -> 105, of which waited for: 33 -> 33; matrix products, arithmetic and copies ran while one was open for 13% -> 14% of each run, Pallas kernels for 39% -> 40%
where the time goes in v4:
time: 683 us; the launch traced here: 673 us
  Pallas kernels  276 us (40%)
  waiting for transfers between devices  160 us (23%)
  other arithmetic  108 us (16%)
  starting transfers between devices  86.8 us (13%)
  local copies, waits for them, and re-layouts  33.9 us (5%)
    ppermute x29, waiting for transfers between devices, onward(): return lax.ppermute(v, 'dp', [(i, (i + 2 * planes) % n) for i in range(n)])  98.5 us
    pallas_call x6, Pallas kernels, weights_step(): pl.pallas_call(functools.partial(weights_body, len(older)), grid=(count,...  76.3 us
    pallas_call x4, Pallas kernels, expert_rows(): pl.pallas_call(functools.partial(main_body, cap, plane, fresh), in_specs=...  67.4 us
    ppermute x76, waiting for transfers between devices, flip(): lax.ppermute(v, axis, [(i, i ^ bit) for i in range(lax.axis_size(axis))])  61.2 us
    ppermute x76, starting transfers between devices, flip(): lax.ppermute(v, axis, [(i, i ^ bit) for i in range(lax.axis_size(axis))])  60.1 us
    convert_element_type x22, other arithmetic, plus(): functools.reduce(lambda a, b: a + b, [v.astype(F32) for v in vs]).astype(BF)  49.6 us
    pallas_call x4, Pallas kernels, seed_rows(): pl.pallas_call(functools.partial(seed_body, cap, plane, fresh), in_specs=...  36.3 us
    pallas_call x4, Pallas kernels, mix_rows(): pl.pallas_call(functools.partial(mix_body, cap, plane), in_specs=[pl.Bloc...  30.1 us
  transfers between devices with their start and end apart: 105, of which 33 were waited for; matrix products, arithmetic and copies ran while one was open for 14% of the time, Pallas kernels for 40%

profile of v4, /device:TPU:0, one launch (start us, length us, event | category | flops | bytes accessed | tf_op | source)
XLA Modules:
  0.0 673.1 jit_solution(10793639148354251760)
XLA Ops:
  14.1 5.8 collective-permute-done.1.refs_6_
  23.1 5.6 slot_targets.1
  37.4 8.2 %collective-permute-done.7.refs_10_ = bf16[192,1152]{1,0:T(8,128)(2,1)S(1)} collective-permute-done((bf16[192,1152]{1,0:T(8,128)(2,1)}, bf16[192,1152]{1,0:T(8,128)(2,1)S(1)}, u32[]{:S(2)}, u32[]{:S(2)}) %collective-permute-start.7) | collective-permute-done | bytes 442400 | tf_op jit(solution)/shard_map/ppermute | solution.py:888
  53.5 4.9 collective-permute-done.9.refs_11_
  58.4 6.6 collective-permute-done.10
  68.0 11.2 %qkv.1 = (bf16[1024,1536]{1,0:T(8,128)(2,1)}, bf16[1024,384]{1,0:T(8,128)(2,1)}, bf16[1024,128]{1,0:T(8,128)(2,1)}, bf16[1024,128]{1,0:T(8,128)(2,1)}, f32[8,1536]{1,0:T(8,128)}, /*index=5*/bf16[1536,1152]{1,0:T(8,128)(2,1)}) custom-call(s32[12]{0:T(128)} %stack.217.at, bf16[256,1536]{1,0:T(8,128)(2,1)} %refs_0_.6, bf16[256,1536]{1,0:T(8,128)(2,1)} %copy-done.139, ...), custom_call_target="tpu_custom_call" | custom-call | flops 3623878656 | bytes 20000000 | tf_op jit(solution)/shard_map/qkv/pallas_call | solution.py:142
  79.2 4.3 collective-permute-done.12
  88.8 13.9 %attend.1 = (bf16[1024,384]{1,0:T(8,128)(2,1)S(1)}, f32[3,8,1024]{2,1,0:T(8,128)S(1)}) custom-call(s32[1]{0:T(128)} %copy.176.length, bf16[1024,384]{1,0:T(8,128)(2,1)S(1)} %copy-done.20, bf16[1024,128]{1,0:T(8,128)(2,1)S(1)} %copy-done.25, bf16[1024,128]{1,0:T(8,128)(2,1)S(1)} %copy-done.27), custom_call_target="tpu_custom_call" | custom-call | tf_op jit(solution)/shard_map/attend/pallas_call | solution.py:273
  110.5 3.9 collective-permute-done.18
  114.4 13.7 %collective-permute-done.19 = bf16[264,1536]{1,0:T(8,128)(2,1)} collective-permute-done((bf16[264,1536]{1,0:T(8,128)(2,1)}, bf16[264,1536]{1,0:T(8,128)(2,1)}, u32[]{:S(2)}, u32[]{:S(2)}) %collective-permute-start.19) | collective-permute-done | bytes 811040 | tf_op jit(solution)/shard_map/ppermute | solution.py:871
  136.0 7.1 %round_weights.1 = (bf16[8,1536,256]{2,1,0:T(8,128)(2,1)S(1)}, bf16[8,128,1536]{2,1,0:T(8,128)(2,1)S(1)}) custom-call(s32[1]{0:T(128)} %bitcast.26.turn.first, f32[2,8,1536,128]{3,2,1,0:T(8,128)} %refs_0_.12, f32[8,128,1536]{2,1,0:T(8,128)S(1)} %copy-done), custom_call_target="tpu_custom_call" | custom-call | bytes 28000000 | tf_op jit(solution)/shard_map/round_weights/pallas_call | solution.py:736
  156.8 9.0 %seed_rows.4 = (bf16[8,1280,1536]{2,1,0:T(8,128)(2,1)}, f32[8,320,128]{2,1,0:T(8,128)S(1)}, f32[8,8,1024]{2,1,0:T(8,128)S(1)}) custom-call(s32[1]{0:T(128)} %bitcast.26.turn.first, bf16[4,264,1536]{2,1,0:T(8,128)(2,1)} %pad_maximum_fusion.own, bf16[4,264,1536]{2,1,0:T(8,128)(2,1)} %collective-permute-done.20.sib, bf16[8,128,1536]{2,1,0:T(8,128)(2,1)} %copy-done.4), custom_call_target="tpu_custom_call" | custom-call | flops 3019898880 | bytes 20000000 | tf_op jit(solution)/shard_map/seed_rows/pallas_call | solution.py:507
  165.8 6.8 %collective-permute-done.25 = bf16[256,1536]{1,0:T(8,128)(2,1)S(1)} collective-permute-done((bf16[256,1536]{1,0:T(8,128)(2,1)S(1)}, bf16[256,1536]{1,0:T(8,128)(2,1)S(1)}, u32[]{:S(2)}, u32[]{:S(2)}) %collective-permute-start.25) | collective-permute-done | bytes 786464 | tf_op jit(solution)/shard_map/ppermute | solution.py:888
  176.5 15.9 %collective-permute-done.29 = bf16[256,1536]{1,0:T(8,128)(2,1)S(1)} collective-permute-done((bf16[256,1536]{1,0:T(8,128)(2,1)S(1)}, bf16[256,1536]{1,0:T(8,128)(2,1)S(1)}, u32[]{:S(2)}, u32[]{:S(2)}) %collective-permute-start.29) | collective-permute-done | bytes 786464 | tf_op jit(solution)/shard_map/ppermute | solution.py:888
  198.9 20.6 %collective-permute-done.33 = bf16[256,1536]{1,0:T(8,128)(2,1)} collective-permute-done((bf16[256,1536]{1,0:T(8,128)(2,1)S(1)}, bf16[256,1536]{1,0:T(8,128)(2,1)}, u32[]{:S(2)}, u32[]{:S(2)}) %collective-permute-start.33) | collective-permute-done | bytes 786464 | tf_op jit(solution)/shard_map/ppermute | solution.py:888
  225.3 16.8 %expert_rows.4 = (bf16[8,1280,1536]{2,1,0:T(8,128)(2,1)}, bf16[8,1280,256]{2,1,0:T(8,128)(2,1)}, bf16[8,1280,128]{2,1,0:T(8,128)(2,1)}, bf16[4,264,1536]{2,1,0:T(8,128)(2,1)}, bf16[4,264,1536]{2,1,0:T(8,128)(2,1)}) custom-call(s32[1]{0:T(128)} %bitcast.26.turn.first, f32[8,8,1024]{2,1,0:T(8,128)} %copy-done.47, f32[8,320,128]{2,1,0:T(8,128)} %copy-done.46, ...), custom_call_target="tpu_custom_call" | custom-call | flops 8053063680 | bytes 30000000 | tf_op jit(solution)/shard_map/expert_rows/pallas_call | solution.py:639
  248.4 9.0 %seed_rows.5 = (bf16[8,1280,1536]{2,1,0:T(8,128)(2,1)}, f32[8,320,128]{2,1,0:T(8,128)S(1)}, f32[8,8,1024]{2,1,0:T(8,128)S(1)}) custom-call(s32[1]{0:T(128)} %bitcast.26.turn.first, bf16[4,264,1536]{2,1,0:T(8,128)(2,1)} %copy-done.53, bf16[4,264,1536]{2,1,0:T(8,128)(2,1)} %copy-done.71, ...), custom_call_target="tpu_custom_call", output_to_operand_aliasing={{0}: (4, {})} | custom-call | flops 3019898880 | bytes 20000000 | tf_op jit(solution)/shard_map/seed_rows/pallas_call | solution.py:507
  259.2 9.0 %seed_rows.6 = (bf16[8,1280,1536]{2,1,0:T(8,128)(2,1)}, f32[8,320,128]{2,1,0:T(8,128)S(1)}, f32[8,8,1024]{2,1,0:T(8,128)S(1)}) custom-call(s32[1]{0:T(128)} %bitcast.26.turn.first, bf16[4,264,1536]{2,1,0:T(8,128)(2,1)} %copy-done.55, bf16[4,264,1536]{2,1,0:T(8,128)(2,1)} %collective-permute-done.36.sib, ...), custom_call_target="tpu_custom_call", output_to_operand_aliasing={{0}: (4, {})} | custom-call | flops 3019898880 | bytes 20000000 | tf_op jit(solution)/shard_map/seed_rows/pallas_call | solution.py:507
  268.7 3.4 pad_maximum_fusion.6.own_in
  275.5 16.8 %expert_rows.5 = (bf16[8,1280,1536]{2,1,0:T(8,128)(2,1)}, bf16[8,1280,256]{2,1,0:T(8,128)(2,1)}, bf16[8,1280,128]{2,1,0:T(8,128)(2,1)}, bf16[4,264,1536]{2,1,0:T(8,128)(2,1)}, bf16[4,264,1536]{2,1,0:T(8,128)(2,1)}) custom-call(s32[1]{0:T(128)} %bitcast.26.turn.first, ...), custom_call_target="tpu_custom_call", output_to_operand_aliasing={{0}: (6, {}), {1}: (7, {}), {2}: (8, {})} | custom-call | flops 8053063680 | bytes 30000000 | tf_op jit(solution)/shard_map/expert_rows/pallas_call | solution.py:639
  292.4 5.0 fusion.10
  301.6 16.8 %expert_rows.6 = (bf16[8,1280,1536]{2,1,0:T(8,128)(2,1)}, bf16[8,1280,256]{2,1,0:T(8,128)(2,1)}, bf16[8,1280,128]{2,1,0:T(8,128)(2,1)}, bf16[4,264,1536]{2,1,0:T(8,128)(2,1)}, bf16[4,264,1536]{2,1,0:T(8,128)(2,1)}) custom-call(s32[1]{0:T(128)} %bitcast.26.turn.first, ...), custom_call_target="tpu_custom_call", output_to_operand_aliasing={{0}: (6, {}), {1}: (7, {}), {2}: (8, {})} | custom-call | flops 8053063680 | bytes 30000000 | tf_op jit(solution)/shard_map/expert_rows/pallas_call | solution.py:639
  318.4 5.2 fusion.14
  330.6 7.6 %mix_rows.4 = (bf16[4,256,1536]{2,1,0:T(8,128)(2,1)S(1)}, bf16[4,256,1536]{2,1,0:T(8,128)(2,1)}) custom-call(s32[1]{0:T(128)} %bitcast.26.turn.first, f32[8,8,1024]{2,1,0:T(8,128)S(1)} %copy-done.48, bf16[8,1280,128]{2,1,0:T(8,128)(2,1)S(1)} %copy-done.1, bf16[8,128,1536]{2,1,0:T(8,128)(2,1)S(1)} %copy-done.5), custom_call_target="tpu_custom_call" | custom-call | flops 3019898880 | bytes 20000000 | tf_op jit(solution)/shard_map/mix_rows/pallas_call | solution.py:710
  340.0 9.2 %seed_rows.7 = (bf16[8,1280,1536]{2,1,0:T(8,128)(2,1)}, f32[8,320,128]{2,1,0:T(8,128)S(1)}, f32[8,8,1024]{2,1,0:T(8,128)S(1)}) custom-call(s32[1]{0:T(128)} %bitcast.26.turn.first, bf16[4,264,1536]{2,1,0:T(8,128)(2,1)} %copy-done.54, bf16[4,264,1536]{2,1,0:T(8,128)(2,1)} %collective-permute-done.49.sib, ...), custom_call_target="tpu_custom_call", output_to_operand_aliasing={{0}: (4, {})} | custom-call | flops 3019898880 | bytes 20000000 | tf_op jit(solution)/shard_map/seed_rows/pallas_call | solution.py:507
  356.6 16.9 %expert_rows.7 = (bf16[8,1280,1536]{2,1,0:T(8,128)(2,1)}, bf16[8,1280,256]{2,1,0:T(8,128)(2,1)}, bf16[8,1280,128]{2,1,0:T(8,128)(2,1)}, bf16[4,264,1536]{2,1,0:T(8,128)(2,1)}, bf16[4,264,1536]{2,1,0:T(8,128)(2,1)}) custom-call(s32[1]{0:T(128)} %bitcast.26.turn.first, ...), custom_call_target="tpu_custom_call", output_to_operand_aliasing={{0}: (6, {}), {1}: (7, {}), {2}: (8, {})} | custom-call | flops 8053063680 | bytes 30000000 | tf_op jit(solution)/shard_map/expert_rows/pallas_call | solution.py:639
  373.6 4.2 fusion.26
  385.2 7.0 %mix_rows.5 = (bf16[4,256,1536]{2,1,0:T(8,128)(2,1)S(1)}, bf16[4,256,1536]{2,1,0:T(8,128)(2,1)S(1)}) custom-call(s32[1]{0:T(128)} %bitcast.26.turn.first, f32[8,8,1024]{2,1,0:T(8,128)S(1)} %copy-done.39, bf16[8,1280,128]{2,1,0:T(8,128)(2,1)S(1)} %copy-done.2, bf16[8,128,1536]{2,1,0:T(8,128)(2,1)S(1)} %copy-done.6), custom_call_target="tpu_custom_call" | custom-call | flops 3019898880 | bytes 20000000 | tf_op jit(solution)/shard_map/mix_rows/pallas_call | solution.py:710
  394.1 5.8 collective-permute-done.64
  399.8 3.6 collective-permute-done.62
  407.8 7.9 %mix_rows.6 = (bf16[4,256,1536]{2,1,0:T(8,128)(2,1)S(1)}, bf16[4,256,1536]{2,1,0:T(8,128)(2,1)}) custom-call(s32[1]{0:T(128)} %bitcast.26.turn.first, f32[8,8,1024]{2,1,0:T(8,128)S(1)} %copy-done.37, bf16[8,1280,128]{2,1,0:T(8,128)(2,1)S(1)} %copy-done.2, bf16[8,128,1536]{2,1,0:T(8,128)(2,1)S(1)} %copy-done.6), custom_call_target="tpu_custom_call" | custom-call | flops 3019898880 | bytes 20000000 | tf_op jit(solution)/shard_map/mix_rows/pallas_call | solution.py:710
  418.4 8.2 %collective-permute-done.68 = bf16[256,1536]{1,0:T(8,128)(2,1)S(1)} collective-permute-done((bf16[256,1536]{1,0:T(8,128)(2,1)S(1)}, bf16[256,1536]{1,0:T(8,128)(2,1)S(1)}, u32[]{:S(2)}, u32[]{:S(2)}) %collective-permute-start.68) | collective-permute-done | bytes 786464 | tf_op jit(solution)/shard_map/ppermute | solution.py:871
  433.1 7.6 %mix_rows.7 = (bf16[4,256,1536]{2,1,0:T(8,128)(2,1)S(1)}, bf16[4,256,1536]{2,1,0:T(8,128)(2,1)}) custom-call(s32[1]{0:T(128)} %bitcast.26.turn.first, f32[8,8,1024]{2,1,0:T(8,128)S(1)} %copy-done.41, bf16[8,1280,128]{2,1,0:T(8,128)(2,1)S(1)} %copy-done.2, bf16[8,128,1536]{2,1,0:T(8,128)(2,1)S(1)} %copy-done.6), custom_call_target="tpu_custom_call" | custom-call | flops 3019898880 | bytes 20000000 | tf_op jit(solution)/shard_map/mix_rows/pallas_call | solution.py:710
  442.5 9.2 %weights_step.6 = (f32[2,8,1536,128]{3,2,1,0:T(8,128)}, f32[2,8,1536,128]{3,2,1,0:T(8,128)}, f32[2,8,1536,128]{3,2,1,0:T(8,128)}, f32[2,8,1536,128]{3,2,1,0:T(8,...) custom-call(s32[1]{0:T(128)} %bitcast.26.turn.first, ...), custom_call_target="tpu_custom_call" | custom-call | flops 1509949440 | bytes 26000000 | tf_op jit(solution)/shard_map/weights_step/pallas_call | solution.py:784
  451.8 4.2 fusion.34
  462.1 10.5 %weights_step.7 = (f32[2,8,1536,128]{3,2,1,0:T(8,128)}, f32[2,8,1536,128]{3,2,1,0:T(8,128)}, f32[2,8,1536,128]{3,2,1,0:T(8,128)}, f32[2,8,1536,128]{3,2,1,0:T(8,...) custom-call(s32[1]{0:T(128)} %get-tuple-element.995.turn, ...), custom_call_target="tpu_custom_call", output_to_operand_aliasing={{0}: (11, {}), {1}: (12, {}), {2}: (13, {}), {3}: (14, {}),... | custom-call | flops 1509949440 | bytes 26000000 | tf_op jit(solution)/shard_map/weights_step/pallas_call | solution.py:784
  472.7 4.1 fusion.38
  476.9 3.9 collective-permute-done.76
  488.6 18.4 %weights_step.8 = (f32[2,8,1536,128]{3,2,1,0:T(8,128)}, f32[2,8,1536,128]{3,2,1,0:T(8,128)}, f32[2,8,1536,128]{3,2,1,0:T(8,128)}, f32[2,8,1536,128]{3,2,1,0:T(8,...) custom-call(s32[1]{0:T(128)} %get-tuple-element.1049.turn, ...), custom_call_target="tpu_custom_call", output_to_operand_aliasing={{0}: (11, {}), {1}: (12, {}), {2}: (13, {}), {3}: (14, {}),... | custom-call | flops 3019898880 | bytes 52000000 | tf_op jit(solution)/shard_map/weights_step/pallas_call | solution.py:784
  515.1 4.4 heads_back.1
  533.5 17.8 %attend_back.1 = (bf16[1024,384]{1,0:T(8,128)(2,1)S(1)}, bf16[1024,128]{1,0:T(8,128)(2,1)S(1)}, bf16[1024,128]{1,0:T(8,128)(2,1)S(1)}) custom-call(s32[1]{0:T(128)} %copy.176.length, bf16[1024,384]{1,0:T(8,128)(2,1)S(1)} %copy-done.21, bf16[1024,128]{1,0:T(8,128)(2,1)S(1)} %copy-done.26, bf16[1024,128]{1,0:T(8,128)(2,1)S(1)} %copy-done.28, ...), custom_call_target="tpu_custom_call" | custom-call | tf_op jit(solution)/shard_map/attend_back/pallas_call | solution.py:374
  551.4 8.6 %collective-permute-done.82 = bf16[4,192,384]{2,1,0:T(8,128)(2,1)} collective-permute-done((bf16[4,192,384]{2,1,0:T(8,128)(2,1)}, bf16[4,192,384]{2,1,0:T(8,128)(2,1)}, u32[]{:S(2)}, u32[]{:S(2)}) %collective-permute-start.82) | collective-permute-done | bytes 589856 | tf_op jit(solution)/shard_map/ppermute | solution.py:871
  570.4 4.0 fusion.87
  589.5 18.4 %weights_step.9 = (f32[2,8,1536,128]{3,2,1,0:T(8,128)}, f32[2,8,1536,128]{3,2,1,0:T(8,128)}, f32[2,8,1536,128]{3,2,1,0:T(8,128)}, f32[2,8,1536,128]{3,2,1,0:T(8,...) custom-call(s32[1]{0:T(128)} %get-tuple-element.1148.turn, ...), custom_call_target="tpu_custom_call", output_to_operand_aliasing={{0}: (11, {}), {1}: (12, {}), {2}: (13, {}), {3}: (14, {}),... | custom-call | flops 3019898880 | bytes 52000000 | tf_op jit(solution)/shard_map/weights_step/pallas_call | solution.py:784
  623.1 9.8 %weights_step.10 = (f32[2,8,1536,128]{3,2,1,0:T(8,128)}, f32[2,8,1536,128]{3,2,1,0:T(8,128)}, f32[2,8,1536,128]{3,2,1,0:T(8,128)}, f32[2,8,1536,128]{3,2,1,0:T(8...) custom-call(s32[1]{0:T(128)} %get-tuple-element.1174.turn, ...), custom_call_target="tpu_custom_call", output_to_operand_aliasing={{0}: (11, {}), {1}: (12, {}), {2}: (13, {}), {3}: (14, {}),... | custom-call | flops 1509949440 | bytes 26000000 | tf_op jit(solution)/shard_map/weights_step/pallas_call | solution.py:784
  633.0 8.0 %collective-permute-done.96 = bf16[200,640]{1,0:T(8,128)(2,1)S(1)} collective-permute-done((bf16[200,640]{1,0:T(8,128)(2,1)S(1)}, bf16[200,640]{1,0:T(8,128)(2,1)S(1)}, u32[]{:S(2)}, u32[]{:S(2)}) %collective-permute-start.96) | collective-permute-done | bytes 256032 | tf_op jit(solution)/shard_map/ppermute | solution.py:888
  652.5 9.9 %weights_step.11 = (f32[2,8,1536,128]{3,2,1,0:T(8,128)}, f32[2,8,1536,128]{3,2,1,0:T(8,128)}, f32[2,8,1536,128]{3,2,1,0:T(8,128)}, f32[2,8,1536,128]{3,2,1,0:T(8...) custom-call(s32[1]{0:T(128)} %get-tuple-element.1216.turn, ...), custom_call_target="tpu_custom_call", output_to_operand_aliasing={{0}: (11, {}), {1}: (12, {}), {2}: (13, {}), {3}: (14, {}),... | custom-call | flops 1509949440 | bytes 26000000 | tf_op jit(solution)/shard_map/weights_step/pallas_call | solution.py:784
  665.1 5.3 collective-permute-done.102
  (587 shorter events, 235.4 us)
Async XLA Ops:
  9.2 26.6 %collective-permute-start.5 = (bf16[256,1536]{1,0:T(8,128)(2,1)}, bf16[256,1536]{1,0:T(8,128)(2,1)}, u32[]{:S(2)}, u32[]{:S(2)}) collective-permute-start(bf16[256,1536]{1,0:T(8,128)(2,1)} %refs_0_.6), channel_id=1, source_target_pairs={{0,2},{1,3},{2,0},{3,1},{4,6},{5,7},{6,4},{7,5},{8,10},{9,11},{10,... | collective-permute-start | bytes 2359304 | tf_op jit(solution)/shard_map/ppermute | solution.py:871
  128.1 22.1 %collective-permute-start.23 = (bf16[264,1536]{1,0:T(8,128)(2,1)}, bf16[264,1536]{1,0:T(8,128)(2,1)S(1)}, u32[]{:S(2)}, u32[]{:S(2)}) collective-permute-start(bf16[264,1536]{1,0:T(8,128)(2,1)} %collective-permute-done.19), channel_id=1, source_target_pairs={{0,8},{4,12},{8,16},{12,20},{16,24},{20,28},{24,0},{28,4},{1,9},{5... | collective-permute-start | bytes 2433032 | tf_op jit(solution)/shard_map/ppermute | solution.py:888
  128.3 21.9 %collective-permute-start.24 = (bf16[264,1536]{1,0:T(8,128)(2,1)}, bf16[264,1536]{1,0:T(8,128)(2,1)S(1)}, u32[]{:S(2)}, u32[]{:S(2)}) collective-permute-start(bf16[264,1536]{1,0:T(8,128)(2,1)} %collective-permute-done.16), channel_id=1, source_target_pairs={{0,4},{4,0},{8,12},{12,8},{16,20},{20,16},{24,28},{28,24},{1,5},{5... | collective-permute-start | bytes 2433032 | tf_op jit(solution)/shard_map/ppermute | solution.py:871
  194.3 25.2 %collective-permute-start.32 = (bf16[4,264,1536]{2,1,0:T(8,128)(2,1)S(1)}, bf16[4,264,1536]{2,1,0:T(8,128)(2,1)S(1)}, u32[]{:S(2)}, u32[]{:S(2)}) collective-permute-start(bf16[4,264,1536]{2,1,0:T(8,128)(2,1)S(1)} %pad_maximum_fusion.1.own), channel_id=1, source_target_pairs={{0,1},{1,0},{2,3},{3,2},{4,5},{5,4},{6,7},{7,6},{8,9},{9,8},{10,11... | collective-permute-start | bytes 9732104 | tf_op jit(solution)/shard_map/ppermute | solution.py:871
  196.5 23.0 %collective-permute-start.35 = (bf16[4,256,1536]{2,1,0:T(8,128)(2,1)S(1)}, bf16[4,256,1536]{2,1,0:T(8,128)(2,1)S(1)}, u32[]{:S(2)}, u32[]{:S(2)}) collective-permute-start(bf16[4,256,1536]{2,1,0:T(8,128)(2,1)S(1)} %pad_maximum_fusion.4.own_in), channel_id=1, source_target_pairs={{0,1},{1,0},{2,3},{3,2},{4,5},{5,4},{6,7},{7,6},{8,9},{9,8},{10,11... | collective-permute-start | bytes 9437192 | tf_op jit(solution)/shard_map/ppermute | solution.py:871
  196.9 22.7 %collective-permute-start.31 = (bf16[264,1536]{1,0:T(8,128)(2,1)S(1)}, bf16[264,1536]{1,0:T(8,128)(2,1)S(1)}, u32[]{:S(2)}, u32[]{:S(2)}) collective-permute-start(bf16[264,1536]{1,0:T(8,128)(2,1)S(1)} %copy-done.89), channel_id=1, source_target_pairs={{0,4},{4,0},{8,12},{12,8},{16,20},{20,16},{24,28},{28,24},{1,5},{5... | collective-permute-start | bytes 2433032 | tf_op jit(solution)/shard_map/ppermute | solution.py:871
  221.9 22.1 %collective-permute-start.36 = (bf16[4,264,1536]{2,1,0:T(8,128)(2,1)S(1)}, bf16[4,264,1536]{2,1,0:T(8,128)(2,1)}, u32[]{:S(2)}, u32[]{:S(2)}) collective-permute-start(bf16[4,264,1536]{2,1,0:T(8,128)(2,1)S(1)} %pad_maximum_fusion.2.own), channel_id=1, source_target_pairs={{0,1},{1,0},{2,3},{3,2},{4,5},{5,4},{6,7},{7,6},{8,9},{9,8},{10,11... | collective-permute-start | bytes 9732104 | tf_op jit(solution)/shard_map/ppermute | solution.py:871
  246.1 22.5 %collective-permute-start.43 = (bf16[4,256,1536]{2,1,0:T(8,128)(2,1)S(1)}, bf16[4,256,1536]{2,1,0:T(8,128)(2,1)S(1)}, u32[]{:S(2)}, u32[]{:S(2)}) collective-permute-start(bf16[4,256,1536]{2,1,0:T(8,128)(2,1)S(1)} %pad_maximum_fusion.5.own_in), channel_id=1, source_target_pairs={{0,1},{1,0},{2,3},{3,2},{4,5},{5,4},{6,7},{7,6},{8,9},{9,8},{10,11... | collective-permute-start | bytes 9437192 | tf_op jit(solution)/shard_map/ppermute | solution.py:871
  246.1 22.4 %collective-permute-start.40 = (bf16[264,1536]{1,0:T(8,128)(2,1)S(1)}, bf16[264,1536]{1,0:T(8,128)(2,1)S(1)}, u32[]{:S(2)}, u32[]{:S(2)}) collective-permute-start(bf16[264,1536]{1,0:T(8,128)(2,1)S(1)} %collective-permute-done.31), channel_id=1, source_target_pairs={{0,2},{1,3},{2,0},{3,1},{4,6},{5,7},{6,4},{7,5},{8,10},{9,11},{10,... | collective-permute-start | bytes 2433032 | tf_op jit(solution)/shard_map/ppermute | solution.py:871
  246.8 21.7 %collective-permute-start.41 = (bf16[256,1536]{1,0:T(8,128)(2,1)}, bf16[256,1536]{1,0:T(8,128)(2,1)}, u32[]{:S(2)}, u32[]{:S(2)}) collective-permute-start(bf16[256,1536]{1,0:T(8,128)(2,1)} %collective-permute-done.33), channel_id=1, source_target_pairs={{0,8},{4,12},{8,16},{12,20},{16,24},{20,28},{24,0},{28,4},{1,9},{5... | collective-permute-start | bytes 2359304 | tf_op jit(solution)/shard_map/ppermute | solution.py:888
  246.8 21.7 %collective-permute-start.42 = (bf16[256,1536]{1,0:T(8,128)(2,1)}, bf16[256,1536]{1,0:T(8,128)(2,1)S(1)}, u32[]{:S(2)}, u32[]{:S(2)}) collective-permute-start(bf16[256,1536]{1,0:T(8,128)(2,1)} %collective-permute-done.38), channel_id=1, source_target_pairs={{0,4},{4,0},{8,12},{12,8},{16,20},{20,16},{24,28},{28,24},{1,5},{5... | collective-permute-start | bytes 2359304 | tf_op jit(solution)/shard_map/ppermute | solution.py:871
  268.6 23.8 %collective-permute-start.48 = (bf16[4,264,1536]{2,1,0:T(8,128)(2,1)}, bf16[4,264,1536]{2,1,0:T(8,128)(2,1)}, u32[]{:S(2)}, u32[]{:S(2)}) collective-permute-start(bf16[4,264,1536]{2,1,0:T(8,128)(2,1)} %get-tuple-element.839), channel_id=1, source_target_pairs={{0,1},{1,0},{2,3},{3,2},{4,5},{5,4},{6,7},{7,6},{8,9},{9,8},{10,11... | collective-permute-start | bytes 9732104 | tf_op jit(solution)/shard_map/ppermute | solution.py:871
  272.1 25.3 %collective-permute-start.47 = (bf16[4,256,1536]{2,1,0:T(8,128)(2,1)S(1)}, bf16[4,256,1536]{2,1,0:T(8,128)(2,1)}, u32[]{:S(2)}, u32[]{:S(2)}) collective-permute-start(bf16[4,256,1536]{2,1,0:T(8,128)(2,1)S(1)} %pad_maximum_fusion.6.own_in), channel_id=1, source_target_pairs={{0,1},{1,0},{2,3},{3,2},{4,5},{5,4},{6,7},{7,6},{8,9},{9,8},{10,11... | collective-permute-start | bytes 9437192 | tf_op jit(solution)/shard_map/ppermute | solution.py:871
  272.2 25.2 %collective-permute-start.45 = (bf16[256,1536]{1,0:T(8,128)(2,1)}, bf16[256,1536]{1,0:T(8,128)(2,1)}, u32[]{:S(2)}, u32[]{:S(2)}) collective-permute-start(bf16[256,1536]{1,0:T(8,128)(2,1)} %collective-permute-done.41), channel_id=1, source_target_pairs={{0,2},{1,3},{2,0},{3,1},{4,6},{5,7},{6,4},{7,5},{8,10},{9,11},{10,... | collective-permute-start | bytes 2359304 | tf_op jit(solution)/shard_map/ppermute | solution.py:871
  273.4 24.0 %collective-permute-start.46 = (bf16[256,1536]{1,0:T(8,128)(2,1)}, bf16[256,1536]{1,0:T(8,128)(2,1)}, u32[]{:S(2)}, u32[]{:S(2)}) collective-permute-start(bf16[256,1536]{1,0:T(8,128)(2,1)} %collective-permute-done.41), channel_id=1, source_target_pairs={{0,4},{4,0},{8,12},{12,8},{16,20},{20,16},{24,28},{28,24},{1,5},{5... | collective-permute-start | bytes 2359304 | tf_op jit(solution)/shard_map/ppermute | solution.py:871
  274.2 23.2 %collective-permute-start.44 = (bf16[264,1536]{1,0:T(8,128)(2,1)}, bf16[264,1536]{1,0:T(8,128)(2,1)}, u32[]{:S(2)}, u32[]{:S(2)}) collective-permute-start(bf16[264,1536]{1,0:T(8,128)(2,1)} %collective-permute-done.16), channel_id=1, source_target_pairs={{0,8},{4,12},{8,16},{12,20},{16,24},{20,28},{24,0},{28,4},{1,9},{5... | collective-permute-start | bytes 2433032 | tf_op jit(solution)/shard_map/ppermute | solution.py:888
  299.0 24.6 %collective-permute-start.49 = (bf16[4,264,1536]{2,1,0:T(8,128)(2,1)S(1)}, bf16[4,264,1536]{2,1,0:T(8,128)(2,1)}, u32[]{:S(2)}, u32[]{:S(2)}) collective-permute-start(bf16[4,264,1536]{2,1,0:T(8,128)(2,1)S(1)} %pad_maximum_fusion.3.own), channel_id=1, source_target_pairs={{0,1},{1,0},{2,3},{3,2},{4,5},{5,4},{6,7},{7,6},{8,9},{9,8},{10,11... | collective-permute-start | bytes 9732104 | tf_op jit(solution)/shard_map/ppermute | solution.py:871
  299.5 24.1 %collective-permute-start.52 = (bf16[264,1536]{1,0:T(8,128)(2,1)}, bf16[264,1536]{1,0:T(8,128)(2,1)}, u32[]{:S(2)}, u32[]{:S(2)}) collective-permute-start(bf16[264,1536]{1,0:T(8,128)(2,1)} %get-tuple-element.863), channel_id=1, source_target_pairs={{0,4},{4,0},{8,12},{12,8},{16,20},{20,16},{24,28},{28,24},{1,5},{5... | collective-permute-start | bytes 2433032 | tf_op jit(solution)/shard_map/ppermute | solution.py:871
  301.1 22.6 %collective-permute-start.50 = (bf16[256,1536]{1,0:T(8,128)(2,1)}, bf16[256,1536]{1,0:T(8,128)(2,1)}, u32[]{:S(2)}, u32[]{:S(2)}) collective-permute-start(bf16[256,1536]{1,0:T(8,128)(2,1)} %collective-permute-done.46), channel_id=1, source_target_pairs={{0,2},{1,3},{2,0},{3,1},{4,6},{5,7},{6,4},{7,5},{8,10},{9,11},{10,... | collective-permute-start | bytes 2359304 | tf_op jit(solution)/shard_map/ppermute | solution.py:871
  323.6 25.5 %collective-permute-start.54 = (bf16[4,264,1536]{2,1,0:T(8,128)(2,1)}, bf16[4,264,1536]{2,1,0:T(8,128)(2,1)S(1)}, u32[]{:S(2)}, u32[]{:S(2)}) collective-permute-start(bf16[4,264,1536]{2,1,0:T(8,128)(2,1)} %get-tuple-element.888), channel_id=1, source_target_pairs={{0,1},{1,0},{2,3},{3,2},{4,5},{5,4},{6,7},{7,6},{8,9},{9,8},{10,11... | collective-permute-start | bytes 9732104 | tf_op jit(solution)/shard_map/ppermute | solution.py:871
  326.0 25.6 %collective-permute-start.53 = (bf16[4,256,1536]{2,1,0:T(8,128)(2,1)S(1)}, bf16[4,256,1536]{2,1,0:T(8,128)(2,1)}, u32[]{:S(2)}, u32[]{:S(2)}) collective-permute-start(bf16[4,256,1536]{2,1,0:T(8,128)(2,1)S(1)} %pad_maximum_fusion.7.own_in), channel_id=1, source_target_pairs={{0,1},{1,0},{2,3},{3,2},{4,5},{5,4},{6,7},{7,6},{8,9},{9,8},{10,11... | collective-permute-start | bytes 9437192 | tf_op jit(solution)/shard_map/ppermute | solution.py:871
  326.5 25.1 %collective-permute-start.55 = (bf16[264,1536]{1,0:T(8,128)(2,1)}, bf16[264,1536]{1,0:T(8,128)(2,1)S(1)}, u32[]{:S(2)}, u32[]{:S(2)}) collective-permute-start(bf16[264,1536]{1,0:T(8,128)(2,1)} %get-tuple-element.886), channel_id=1, source_target_pairs={{0,2},{1,3},{2,0},{3,1},{4,6},{5,7},{6,4},{7,5},{8,10},{9,11},{10,... | collective-permute-start | bytes 2433032 | tf_op jit(solution)/shard_map/ppermute | solution.py:871
  328.0 23.6 %collective-permute-start.56 = (bf16[264,1536]{1,0:T(8,128)(2,1)}, bf16[264,1536]{1,0:T(8,128)(2,1)S(1)}, u32[]{:S(2)}, u32[]{:S(2)}) collective-permute-start(bf16[264,1536]{1,0:T(8,128)(2,1)} %get-tuple-element.884), channel_id=1, source_target_pairs={{0,24},{4,28},{8,0},{12,4},{16,8},{20,12},{24,16},{28,20},{1,25},{... | collective-permute-start | bytes 2433032 | tf_op jit(solution)/shard_map/ppermute | solution.py:888
  351.6 22.0 %collective-permute-start.60 = (bf16[4,256,1536]{2,1,0:T(8,128)(2,1)}, bf16[4,256,1536]{2,1,0:T(8,128)(2,1)}, u32[]{:S(2)}, u32[]{:S(2)}) collective-permute-start(bf16[4,256,1536]{2,1,0:T(8,128)(2,1)} %get-tuple-element.918), channel_id=1, source_target_pairs={{0,1},{1,0},{2,3},{3,2},{4,5},{5,4},{6,7},{7,6},{8,9},{9,8},{10,11... | collective-permute-start | bytes 9437192 | tf_op jit(solution)/shard_map/ppermute | solution.py:871
  354.3 23.6 %collective-permute-start.58 = (bf16[264,1536]{1,0:T(8,128)(2,1)}, bf16[264,1536]{1,0:T(8,128)(2,1)}, u32[]{:S(2)}, u32[]{:S(2)}) collective-permute-start(bf16[264,1536]{1,0:T(8,128)(2,1)} %add_convert_fusion.11), channel_id=1, source_target_pairs={{0,2},{1,3},{2,0},{3,1},{4,6},{5,7},{6,4},{7,5},{8,10},{9,11},{10,... | collective-permute-start | bytes 2433032 | tf_op jit(solution)/shard_map/ppermute | solution.py:871
  355.1 22.7 %collective-permute-start.57 = (bf16[264,1536]{1,0:T(8,128)(2,1)}, bf16[264,1536]{1,0:T(8,128)(2,1)}, u32[]{:S(2)}, u32[]{:S(2)}) collective-permute-start(bf16[264,1536]{1,0:T(8,128)(2,1)} %get-tuple-element.913), channel_id=1, source_target_pairs={{0,4},{4,0},{8,12},{12,8},{16,20},{20,16},{24,28},{28,24},{1,5},{5... | collective-permute-start | bytes 2433032 | tf_op jit(solution)/shard_map/ppermute | solution.py:871
  356.4 21.8 %collective-permute-start.59 = (bf16[264,1536]{1,0:T(8,128)(2,1)}, bf16[264,1536]{1,0:T(8,128)(2,1)}, u32[]{:S(2)}, u32[]{:S(2)}) collective-permute-start(bf16[264,1536]{1,0:T(8,128)(2,1)} %get-tuple-element.908), channel_id=1, source_target_pairs={{0,8},{4,12},{8,16},{12,20},{16,24},{20,28},{24,0},{28,4},{1,9},{5... | collective-permute-start | bytes 2433032 | tf_op jit(solution)/shard_map/ppermute | solution.py:888
  405.4 22.3 %collective-permute-start.66 = (bf16[264,1536]{1,0:T(8,128)(2,1)S(1)}, bf16[264,1536]{1,0:T(8,128)(2,1)S(1)}, u32[]{:S(2)}, u32[]{:S(2)}) collective-permute-start(bf16[264,1536]{1,0:T(8,128)(2,1)S(1)} %add_convert_fusion.4), channel_id=1, source_target_pairs={{0,8},{4,12},{8,16},{12,20},{16,24},{20,28},{24,0},{28,4},{1,9},{5... | collective-permute-start | bytes 2433032 | tf_op jit(solution)/shard_map/ppermute | solution.py:888
  405.5 22.2 %collective-permute-start.65 = (bf16[264,1536]{1,0:T(8,128)(2,1)S(1)}, bf16[264,1536]{1,0:T(8,128)(2,1)S(1)}, u32[]{:S(2)}, u32[]{:S(2)}) collective-permute-start(bf16[264,1536]{1,0:T(8,128)(2,1)S(1)} %get-tuple-element.953), channel_id=1, source_target_pairs={{0,2},{1,3},{2,0},{3,1},{4,6},{5,7},{6,4},{7,5},{8,10},{9,11},{10,... | collective-permute-start | bytes 2433032 | tf_op jit(solution)/shard_map/ppermute | solution.py:871
  428.6 23.2 %collective-permute-start.71 = (bf16[4,256,1536]{2,1,0:T(8,128)(2,1)}, bf16[4,256,1536]{2,1,0:T(8,128)(2,1)}, u32[]{:S(2)}, u32[]{:S(2)}) collective-permute-start(bf16[4,256,1536]{2,1,0:T(8,128)(2,1)} %get-tuple-element.993), channel_id=1, source_target_pairs={{0,1},{1,0},{2,3},{3,2},{4,5},{5,4},{6,7},{7,6},{8,9},{9,8},{10,11... | collective-permute-start | bytes 9437192 | tf_op jit(solution)/shard_map/ppermute | solution.py:871
  428.8 27.2 %collective-permute-start.70 = (bf16[264,1536]{1,0:T(8,128)(2,1)S(1)}, bf16[264,1536]{1,0:T(8,128)(2,1)}, u32[]{:S(2)}, u32[]{:S(2)}) collective-permute-start(bf16[264,1536]{1,0:T(8,128)(2,1)S(1)} %add_convert_fusion.3), channel_id=1, source_target_pairs={{0,4},{4,0},{8,12},{12,8},{16,20},{20,16},{24,28},{28,24},{1,5},{5... | collective-permute-start | bytes 2433032 | tf_op jit(solution)/shard_map/ppermute | solution.py:871
  430.1 25.9 %collective-permute-start.69 = (bf16[264,1536]{1,0:T(8,128)(2,1)}, bf16[264,1536]{1,0:T(8,128)(2,1)}, u32[]{:S(2)}, u32[]{:S(2)}) collective-permute-start(bf16[264,1536]{1,0:T(8,128)(2,1)} %get-tuple-element.977), channel_id=1, source_target_pairs={{0,2},{1,3},{2,0},{3,1},{4,6},{5,7},{6,4},{7,5},{8,10},{9,11},{10,... | collective-permute-start | bytes 2433032 | tf_op jit(solution)/shard_map/ppermute | solution.py:871
  431.0 25.0 %collective-permute-start.72 = (bf16[256,1536]{1,0:T(8,128)(2,1)}, bf16[256,1536]{1,0:T(8,128)(2,1)}, u32[]{:S(2)}, u32[]{:S(2)}) collective-permute-start(bf16[256,1536]{1,0:T(8,128)(2,1)} %get-tuple-element.989), channel_id=1, source_target_pairs={{0,24},{4,28},{8,0},{12,4},{16,8},{20,12},{24,16},{28,20},{1,25},{... | collective-permute-start | bytes 2359304 | tf_op jit(solution)/shard_map/ppermute | solution.py:888
  458.9 22.4 %collective-permute-start.74 = (bf16[264,1536]{1,0:T(8,128)(2,1)}, bf16[264,1536]{1,0:T(8,128)(2,1)S(1)}, u32[]{:S(2)}, u32[]{:S(2)}) collective-permute-start(bf16[264,1536]{1,0:T(8,128)(2,1)} %add_convert_fusion.1), channel_id=1, source_target_pairs={{0,8},{4,12},{8,16},{12,20},{16,24},{20,28},{24,0},{28,4},{1,9},{5... | collective-permute-start | bytes 2433032 | tf_op jit(solution)/shard_map/ppermute | solution.py:888
  488.6 21.6 %collective-permute-start.80 = (bf16[256,1536]{1,0:T(8,128)(2,1)S(1)}, bf16[256,1536]{1,0:T(8,128)(2,1)}, u32[]{:S(2)}, u32[]{:S(2)}) collective-permute-start(bf16[256,1536]{1,0:T(8,128)(2,1)S(1)} %copy-done.107), channel_id=1, source_target_pairs={{0,8},{4,12},{8,16},{12,20},{16,24},{20,28},{24,0},{28,4},{1,9},{5... | collective-permute-start | bytes 2359304 | tf_op jit(solution)/shard_map/ppermute | solution.py:888
  522.5 37.6 %collective-permute-start.86 = (bf16[256,1536]{1,0:T(8,128)(2,1)}, bf16[256,1536]{1,0:T(8,128)(2,1)}, u32[]{:S(2)}, u32[]{:S(2)}) collective-permute-start(bf16[256,1536]{1,0:T(8,128)(2,1)} %add_convert_fusion.32), channel_id=1, source_target_pairs={{0,24},{4,28},{8,0},{12,4},{16,8},{20,12},{24,16},{28,20},{1,25},{... | collective-permute-start | bytes 2359304 | tf_op jit(solution)/shard_map/ppermute | solution.py:888
  526.3 33.7 %collective-permute-start.84 = (bf16[256,1536]{1,0:T(8,128)(2,1)}, bf16[256,1536]{1,0:T(8,128)(2,1)}, u32[]{:S(2)}, u32[]{:S(2)}) collective-permute-start(bf16[256,1536]{1,0:T(8,128)(2,1)} %add_convert_fusion.33), channel_id=1, source_target_pairs={{0,2},{1,3},{2,0},{3,1},{4,6},{5,7},{6,4},{7,5},{8,10},{9,11},{10,... | collective-permute-start | bytes 2359304 | tf_op jit(solution)/shard_map/ppermute | solution.py:871
  527.1 35.7 %collective-permute-start.83 = (bf16[256,1536]{1,0:T(8,128)(2,1)}, bf16[256,1536]{1,0:T(8,128)(2,1)}, u32[]{:S(2)}, u32[]{:S(2)}) collective-permute-start(bf16[256,1536]{1,0:T(8,128)(2,1)} %get-tuple-element.1111), channel_id=1, source_target_pairs={{0,2},{1,3},{2,0},{3,1},{4,6},{5,7},{6,4},{7,5},{8,10},{9,11},{10,... | collective-permute-start | bytes 2359304 | tf_op jit(solution)/shard_map/ppermute | solution.py:871
  528.3 34.4 %collective-permute-start.85 = (bf16[256,1536]{1,0:T(8,128)(2,1)}, bf16[256,1536]{1,0:T(8,128)(2,1)}, u32[]{:S(2)}, u32[]{:S(2)}) collective-permute-start(bf16[256,1536]{1,0:T(8,128)(2,1)} %get-tuple-element.1107), channel_id=1, source_target_pairs={{0,4},{4,0},{8,12},{12,8},{16,20},{20,16},{24,28},{28,24},{1,5},{5... | collective-permute-start | bytes 2359304 | tf_op jit(solution)/shard_map/ppermute | solution.py:871
  531.1 29.0 %collective-permute-start.82 = (bf16[4,192,384]{2,1,0:T(8,128)(2,1)}, bf16[4,192,384]{2,1,0:T(8,128)(2,1)}, u32[]{:S(2)}, u32[]{:S(2)}) collective-permute-start(bf16[4,192,384]{2,1,0:T(8,128)(2,1)} %pad_maximum_fusion.11), channel_id=1, source_target_pairs={{0,4},{4,0},{8,12},{12,8},{16,20},{20,16},{24,28},{28,24},{1,5},{5... | collective-permute-start | bytes 1769480 | tf_op jit(solution)/shard_map/ppermute | solution.py:871
  582.4 27.9 %collective-permute-start.94 = (bf16[256,1536]{1,0:T(8,128)(2,1)}, bf16[256,1536]{1,0:T(8,128)(2,1)}, u32[]{:S(2)}, u32[]{:S(2)}) collective-permute-start(bf16[256,1536]{1,0:T(8,128)(2,1)} %add_convert_fusion.30), channel_id=1, source_target_pairs={{0,8},{4,12},{8,16},{12,20},{16,24},{20,28},{24,0},{28,4},{1,9},{5... | collective-permute-start | bytes 2359304 | tf_op jit(solution)/shard_map/ppermute | solution.py:888
  584.1 26.2 %collective-permute-start.93 = (bf16[4,200,640]{2,1,0:T(8,128)(2,1)}, bf16[4,200,640]{2,1,0:T(8,128)(2,1)}, u32[]{:S(2)}, u32[]{:S(2)}) collective-permute-start(bf16[4,200,640]{2,1,0:T(8,128)(2,1)} %pad_maximum_fusion.9), channel_id=1, source_target_pairs={{0,4},{4,0},{8,12},{12,8},{16,20},{20,16},{24,28},{28,24},{1,5},{5... | collective-permute-start | bytes 3072008 | tf_op jit(solution)/shard_map/ppermute | solution.py:871
  587.6 22.7 %collective-permute-start.91 = (bf16[256,1536]{1,0:T(8,128)(2,1)}, bf16[256,1536]{1,0:T(8,128)(2,1)S(1)}, u32[]{:S(2)}, u32[]{:S(2)}) collective-permute-start(bf16[256,1536]{1,0:T(8,128)(2,1)} %add_convert_fusion.31), channel_id=1, source_target_pairs={{0,2},{1,3},{2,0},{3,1},{4,6},{5,7},{6,4},{7,5},{8,10},{9,11},{10,... | collective-permute-start | bytes 2359304 | tf_op jit(solution)/shard_map/ppermute | solution.py:871
  588.2 22.1 %collective-permute-start.92 = (bf16[256,1536]{1,0:T(8,128)(2,1)S(1)}, bf16[256,1536]{1,0:T(8,128)(2,1)S(1)}, u32[]{:S(2)}, u32[]{:S(2)}) collective-permute-start(bf16[256,1536]{1,0:T(8,128)(2,1)S(1)} %get-tuple-element.1145), channel_id=1, source_target_pairs={{0,1},{1,0},{2,3},{3,2},{4,5},{5,4},{6,7},{7,6},{8,9},{9,8},{10,11... | collective-permute-start | bytes 2359304 | tf_op jit(solution)/shard_map/ppermute | solution.py:871
  612.6 28.3 %collective-permute-start.99 = (bf16[256,1536]{1,0:T(8,128)(2,1)}, bf16[256,1536]{1,0:T(8,128)(2,1)}, u32[]{:S(2)}, u32[]{:S(2)}) collective-permute-start(bf16[256,1536]{1,0:T(8,128)(2,1)} %add_convert_fusion.29), channel_id=1, source_target_pairs={{0,4},{4,0},{8,12},{12,8},{16,20},{20,16},{24,28},{28,24},{1,5},{5... | collective-permute-start | bytes 2359304 | tf_op jit(solution)/shard_map/ppermute | solution.py:871
  617.8 23.1 %collective-permute-start.96 = (bf16[200,640]{1,0:T(8,128)(2,1)S(1)}, bf16[200,640]{1,0:T(8,128)(2,1)S(1)}, u32[]{:S(2)}, u32[]{:S(2)}) collective-permute-start(bf16[200,640]{1,0:T(8,128)(2,1)S(1)} %get-tuple-element.1310), channel_id=1, source_target_pairs={{0,16},{4,20},{8,24},{12,28},{16,0},{20,4},{24,8},{28,12},{1,17},{... | collective-permute-start | bytes 768008 | tf_op jit(solution)/shard_map/ppermute | solution.py:888
  618.0 22.9 %collective-permute-start.97 = (bf16[200,640]{1,0:T(8,128)(2,1)S(1)}, bf16[200,640]{1,0:T(8,128)(2,1)S(1)}, u32[]{:S(2)}, u32[]{:S(2)}) collective-permute-start(bf16[200,640]{1,0:T(8,128)(2,1)S(1)} %get-tuple-element.1309), channel_id=1, source_target_pairs={{0,8},{4,12},{8,16},{12,20},{16,24},{20,28},{24,0},{28,4},{1,9},{5... | collective-permute-start | bytes 768008 | tf_op jit(solution)/shard_map/ppermute | solution.py:888
  619.4 21.6 %collective-permute-start.98 = (bf16[256,1536]{1,0:T(8,128)(2,1)S(1)}, bf16[256,1536]{1,0:T(8,128)(2,1)S(1)}, u32[]{:S(2)}, u32[]{:S(2)}) collective-permute-start(bf16[256,1536]{1,0:T(8,128)(2,1)S(1)} %copy-done.106), channel_id=1, source_target_pairs={{0,2},{1,3},{2,0},{3,1},{4,6},{5,7},{6,4},{7,5},{8,10},{9,11},{10,... | collective-permute-start | bytes 2359304 | tf_op jit(solution)/shard_map/ppermute | solution.py:871
  (203 other events, 2123.7 us)
